TPU v7x, 32 devices: a whole 2x2x4 slice. The times are simulated.
32 devices in a mesh: row: 2 (over y), col: 16 (over z, x, core).
Axes of the slice: x: 2, y: 2, z: 4, core: 2. Of those that a mesh axis runs over, the one named last changes fastest.
Arguments:
- object_field: float32 [2, 2, 768, 6144], P(None, None, 'row', 'col'), may hold values from -5 to 5
- offsets: int32 [8, 16, 2], P('row', 'col'), may hold values from 0 to 256
- amplitudes: float32 [8, 16, 256, 256], P('row', 'col'), may hold values from 0.3 to 3
- probe: float32 [2, 256, 256], replicated, may hold values from -5 to 5
- phase: float32 [256, 256], replicated, may hold values from -3.140625 to 3.140625
Outputs:
- object_grad: float32 [2, 2, 768, 6144], P(None, None, 'row', 'col')
- probe_grad: float32 [2, 256, 256], replicated
All inputs are finite; a program needn't handle non-finite values.
Results may differ from a plain program's by a relative error of at most 0.0003.
Values sent between devices are 32-bit elements; how exact they have to be, the bound alone decides.
No kernel may reach another device: no remote copies, remote signals or barrier semaphores. Data moves between devices by JAX's collectives and lax.ppermute only.
A program may use at most 64 MiB of HBM per device.

v0:
```python
import math

import jax
import jax.numpy as jnp
from jax import lax
from jax.sharding import PartitionSpec as P

HALO = 64


HIGH = lax.Precision.HIGHEST


def padded(block, sides, width):
    for axis, dim in sides:
        count = lax.axis_size(axis)
        forward = [(i, i + 1) for i in range(count - 1)]
        forward.append((count - 1, 0))
        backward = [(target, source) for source, target in forward]
        low = lax.ppermute(
            lax.slice_in_dim(block, block.shape[dim] - width, None, axis=dim), axis, forward
        )
        high = lax.ppermute(lax.slice_in_dim(block, 0, width, axis=dim), axis, backward)
        block = jnp.concatenate([low, block, high], axis=dim)
    return block


def mixing(count, sign):
    index = jnp.arange(count, dtype=jnp.int32)
    product = index[:, None] * index[None, :] % count
    angle = product.astype(jnp.float32) * (2.0 * math.pi / count)
    factor = 1.0 / math.sqrt(count)
    cosine = jnp.cos(angle) * factor
    sine = jnp.sin(angle) * factor * sign
    real_row = jnp.stack([cosine, -sine])
    imag_row = jnp.stack([sine, cosine])
    return jnp.stack([real_row, imag_row])


def transform(table, field):
    first = jnp.einsum("dckn,pcnm->pdkm", table, field, precision=HIGH)
    return jnp.einsum("pcnm,dckm->pdnk", first, table, precision=HIGH)


def local(object_field, offsets, amplitudes, probe, phase):
    slices = object_field.shape[0]
    size = probe.shape[1]
    count = offsets.shape[0]
    extended = []
    for s in range(slices):
        extended.append(padded(object_field[s], (("row", 1), ("col", 2)), HALO))
    row_off = offsets[:, 0, 0]
    col_off = offsets[:, 0, 1]
    forward_table = mixing(size, -1.0)
    inverse_table = mixing(size, 1.0)
    prop_re = jnp.cos(phase)
    prop_im = jnp.sin(phase)
    psi = jnp.broadcast_to(probe[None], (count, 2, size, size))
    wins = []
    psis = []
    exit_wave = psi
    for s in range(slices):
        field = extended[s]

        def cut(start_r, start_c):
            return lax.dynamic_slice(field, (0, start_r, start_c), (2, size, size))

        window = jax.vmap(cut)(row_off, col_off)
        wins.append(window)
        psis.append(psi)
        exit_wave = jnp.stack(
            [
                psi[:, 0] * window[:, 0] - psi[:, 1] * window[:, 1],
                psi[:, 0] * window[:, 1] + psi[:, 1] * window[:, 0],
            ],
            axis=1,
        )
        if s < slices - 1:
            freq = transform(forward_table, exit_wave)
            moved = jnp.stack(
                [
                    freq[:, 0] * prop_re - freq[:, 1] * prop_im,
                    freq[:, 0] * prop_im + freq[:, 1] * prop_re,
                ],
                axis=1,
            )
            psi = transform(inverse_table, moved)
    far = transform(forward_table, exit_wave)
    magnitude = jnp.sqrt(far[:, 0] * far[:, 0] + far[:, 1] * far[:, 1])
    keep = 1.0 - amplitudes[:, 0] / jnp.maximum(magnitude, 0.5)
    back = transform(inverse_table, far * keep[:, None])
    grads = [None] * slices
    probe_re = None
    probe_im = None
    for s in range(slices - 1, -1, -1):
        wave = psis[s]
        grads[s] = jnp.stack(
            [
                wave[:, 0] * back[:, 0] + wave[:, 1] * back[:, 1],
                wave[:, 0] * back[:, 1] - wave[:, 1] * back[:, 0],
            ],
            axis=1,
        )
        window = wins[s]
        conj_re = window[:, 0] * back[:, 0] + window[:, 1] * back[:, 1]
        conj_im = window[:, 0] * back[:, 1] - window[:, 1] * back[:, 0]
        if s > 0:
            freq = transform(forward_table, jnp.stack([conj_re, conj_im], axis=1))
            moved = jnp.stack(
                [
                    freq[:, 0] * prop_re + freq[:, 1] * prop_im,
                    freq[:, 1] * prop_re - freq[:, 0] * prop_im,
                ],
                axis=1,
            )
            back = transform(inverse_table, moved)
        else:
            probe_re = jnp.sum(conj_re, axis=0)
            probe_im = jnp.sum(conj_im, axis=0)
    stacked = jnp.stack(grads, axis=1)
    span = extended[0].shape[1]
    tile = span - 2 * HALO

    def add_window(index, gathered):
        start_r = row_off[index]
        start_c = col_off[index]
        current = lax.dynamic_slice(gathered, (0, 0, start_r, start_c), (slices, 2, size, size))
        return lax.dynamic_update_slice(
            gathered, current + stacked[index], (0, 0, start_r, start_c)
        )

    gathered = lax.fori_loop(0, count, add_window, jnp.zeros((slices, 2, span, span), jnp.float32))
    row_rims = jnp.concatenate(
        [gathered[:, :, 0:HALO, :], gathered[:, :, span - HALO : span, :]], axis=2
    )
    row_back = padded(row_rims, (("row", 2),), HALO)
    inner = gathered[:, :, HALO : HALO + tile, :]
    inner = inner.at[:, :, 0:HALO, :].add(row_back[:, :, 0:HALO, :])
    inner = inner.at[:, :, tile - HALO : tile, :].add(row_back[:, :, 3 * HALO : 4 * HALO, :])
    col_rims = jnp.concatenate([inner[:, :, :, 0:HALO], inner[:, :, :, span - HALO : span]], axis=3)
    col_back = padded(col_rims, (("col", 3),), HALO)
    result = inner[:, :, :, HALO : HALO + tile]
    result = result.at[:, :, :, 0:HALO].add(col_back[:, :, :, 0:HALO])
    result = result.at[:, :, :, tile - HALO : tile].add(col_back[:, :, :, 3 * HALO : 4 * HALO])
    total_re, total_im = lax.psum((probe_re, probe_im), ("row", "col"))
    everyone = count * lax.axis_size("row") * lax.axis_size("col")
    factor = 1.0 / math.sqrt(everyone)
    probe_grad = jnp.stack([total_re, total_im]) * factor
    return (result, probe_grad)


def solution(mesh):
    in_specs = (
        P(None, None, "row", "col"),
        P("row", "col", None),
        P("row", "col", None, None),
        P(),
        P(),
    )
    out_specs = (P(None, None, "row", "col"), P())
    return jax.shard_map(local, mesh=mesh, in_specs=in_specs, out_specs=out_specs, check_vma=False)
```

profile of v0, /device:TPU:0, one launch (start us, length us, event | category | flops | bytes accessed | tf_op | source)
XLA Modules:
  0.0 416.7 jit_solution(3488956586962940255)
XLA Ops:
  29.2 4.4 %collective-permute-start.7 = (f32[2,512,64]{2,1,0:T(8,128)S(1)}, f32[2,512,64]{2,1,0:T(8,128)S(1)}, u32[]{:S(2)}, u32[]{:S(2)}) collective-permute-start(f32[2,512,64]{2,1,0:T(8,128)S(1)} %get-tuple-element.263), channel_id=1, source_target_pairs={{1,0},{2,1},{3,2},{4,3},{5,4},{6,5},{7,6},{8,7},{9,8},{10,9},{11,1... | collective-permute-start | bytes 786440 | tf_op jit(solution)/shard_map/ppermute | solution.py:23
  36.0 4.4 %collective-permute-start.3 = (f32[2,512,64]{2,1,0:T(8,128)}, f32[2,512,64]{2,1,0:T(8,128)}, u32[]{:S(2)}, u32[]{:S(2)}) collective-permute-start(f32[2,512,64]{2,1,0:T(8,128)} %get-tuple-element.261), channel_id=1, source_target_pairs={{1,0},{2,1},{3,2},{4,3},{5,4},{6,5},{7,6},{8,7},{9,8},{10,9},{11,1... | collective-permute-start | bytes 786440 | tf_op jit(solution)/shard_map/ppermute | solution.py:23
  45.2 17.5 %while.21 = (s32[]{:T(128)}, f32[2,512,512]{2,1,0:T(8,128)}, s32[4,3]{1,0:T(4,128)S(1)}, f32[4,2,256,256]{2,3,1,0:T(8,128)}, s32[]{:T(128)}) while((s32[]{:T(128)}, f32[2,512,512]{2,1,0:T(8,128)}, s32[4,3]{1,0:T(4,128)S(1)}, f32[4,2,256,256]{2,3,1,0:T(8,128)}, s32[]{:T(128)}) %tuple.113), condition=%wide.while_cond.5, body=%wide.while_body.5.sunk | while | flops 2 | bytes 3146353 | solution.py:66
  64.5 3.5 fusion
  68.0 3.6 fusion.27
  75.4 5.3 %fusion.36 = f32[4,2,256,256]{2,3,1,0:T(8,128)} fusion(f32[4,256,2,256,1]{3,1,4,2,0:T(8,128)S(1)} %fusion.25, f32[1,2,256,256]{3,2,1,0:T(8,128)S(1)} %get-tuple-element.273, f32[1,2,256,256]{3,2,1,0:T(8,128)S(1)} %get-tuple-element.270), kind=kOutput, calls=%fused_computation.49 | convolution fusion | flops 3221487616 | bytes 5242880 | tf_op jit(solution)/shard_map/pcnm,dckm->pdnk/dot_general | solution.py:42
  85.7 17.2 %while.20 = (s32[]{:T(128)}, f32[2,512,512]{2,1,0:T(8,128)}, s32[4,3]{1,0:T(4,128)S(1)}, f32[4,2,256,256]{2,3,1,0:T(8,128)}, s32[]{:T(128)}) while((s32[]{:T(128)}, f32[2,512,512]{2,1,0:T(8,128)}, s32[4,3]{1,0:T(4,128)S(1)}, f32[4,2,256,256]{2,3,1,0:T(8,128)}, s32[]{:T(128)}) %tuple.125), condition=%wide.while_cond.4, body=%wide.while_body.4.sunk | while | flops 2 | bytes 3146353 | solution.py:66
  108.9 3.6 fusion.30
  113.0 3.5 fusion.23
  116.5 3.8 fusion.39
  124.3 3.6 fusion.33
  128.2 3.7 fusion.21
  131.9 3.6 fusion.42
  142.1 81.5 %while.19 = (s32[]{:T(128)}, f32[2,2,512,512]{3,2,1,0:T(8,128)}, s32[4]{0:T(128)S(1)}, s32[4]{0:T(128)S(1)}, f32[4,2,2,256,256]{3,4,2,0,1:T(8,128)}, /*index=5*/s32[]{:T(128)}, s32[]{:T(128)}, s32[]{:T(128)}) while((s32[]{:T(128)}, f32[2,2,512,512]{3,2,1,0:T(8,128)}, s32[4]{0:T(128)S(1)}, s32[4]{0:T(128)S(1)}, ...), condition=%wide.region_1.2_spmd, body=%wide.region_0.1_spmd.sunk | while | flops 262152 | bytes 9437377 | solution.py:132
  150.7 11.8 %dynamic_update_slice.8 = f32[2,2,512,512]{3,2,1,0:T(8,128)} dynamic-update-slice(f32[2,2,512,512]{3,2,1,0:T(8,128)} %get-tuple-element.412, f32[2,2,256,256]{3,2,1,0:T(8,128)S(1)} %bitcast_add_fusion.2, s32[]{:T(128)} %constant.160.clone.1..sunk, s32[]{:T(128)} %constant.160.clone.1..sunk, s32[]{:T(128)S(6)} %select_n.115, s32[]{:T(128)S(6)} %select_n.116) | dynamic-update-slice | bytes 2097156 | tf_op jit(solution)/shard_map/while/body/eval_jaxpr/dynamic_update_slice | solution.py:128
  171.0 12.2 %dynamic_update_slice.8 = f32[2,2,512,512]{3,2,1,0:T(8,128)} dynamic-update-slice(f32[2,2,512,512]{3,2,1,0:T(8,128)} %get-tuple-element.412, f32[2,2,256,256]{3,2,1,0:T(8,128)S(1)} %bitcast_add_fusion.2, s32[]{:T(128)} %constant.160.clone.1..sunk, s32[]{:T(128)} %constant.160.clone.1..sunk, s32[]{:T(128)S(6)} %select_n.115, s32[]{:T(128)S(6)} %select_n.116) | dynamic-update-slice | bytes 2097156 | tf_op jit(solution)/shard_map/while/body/eval_jaxpr/dynamic_update_slice | solution.py:128
  191.7 11.8 %dynamic_update_slice.8 = f32[2,2,512,512]{3,2,1,0:T(8,128)} dynamic-update-slice(f32[2,2,512,512]{3,2,1,0:T(8,128)} %get-tuple-element.412, f32[2,2,256,256]{3,2,1,0:T(8,128)S(1)} %bitcast_add_fusion.2, s32[]{:T(128)} %constant.160.clone.1..sunk, s32[]{:T(128)} %constant.160.clone.1..sunk, s32[]{:T(128)S(6)} %select_n.115, s32[]{:T(128)S(6)} %select_n.116) | dynamic-update-slice | bytes 2097156 | tf_op jit(solution)/shard_map/while/body/eval_jaxpr/dynamic_update_slice | solution.py:128
  212.1 11.5 %dynamic_update_slice.8 = f32[2,2,512,512]{3,2,1,0:T(8,128)} dynamic-update-slice(f32[2,2,512,512]{3,2,1,0:T(8,128)} %get-tuple-element.412, f32[2,2,256,256]{3,2,1,0:T(8,128)S(1)} %bitcast_add_fusion.2, s32[]{:T(128)} %constant.160.clone.1..sunk, s32[]{:T(128)} %constant.160.clone.1..sunk, s32[]{:T(128)S(6)} %select_n.115, s32[]{:T(128)S(6)} %select_n.116) | dynamic-update-slice | bytes 2097156 | tf_op jit(solution)/shard_map/while/body/eval_jaxpr/dynamic_update_slice | solution.py:128
  229.2 5.0 %collective-permute-done.8 = f32[2,2,64,512]{3,2,1,0:T(8,128)S(1)} collective-permute-done((f32[2,2,64,512]{3,2,1,0:T(8,128)S(1)}, f32[2,2,64,512]{3,2,1,0:T(8,128)S(1)}, u32[]{:S(2)}, u32[]{:S(2)}) %collective-permute-start.8) | collective-permute-done | bytes 524320 | tf_op jit(solution)/shard_map/ppermute | solution.py:20
  235.2 6.4 %collective-permute-done.9 = f32[2,2,64,512]{3,2,1,0:T(8,128)S(1)} collective-permute-done((f32[2,2,64,512]{3,2,1,0:T(8,128)S(1)}, f32[2,2,64,512]{3,2,1,0:T(8,128)S(1)}, u32[]{:S(2)}, u32[]{:S(2)}) %collective-permute-start.9) | collective-permute-done | bytes 524320 | tf_op jit(solution)/shard_map/ppermute | solution.py:23
  244.6 9.1 %collective-permute-start.10 = (f32[2,2,384,64]{2,3,1,0:T(8,128)S(1)}, f32[2,2,384,64]{2,3,1,0:T(8,128)}, u32[]{:S(2)}, u32[]{:S(2)}) collective-permute-start(f32[2,2,384,64]{2,3,1,0:T(8,128)S(1)} %copy.61), channel_id=1, source_target_pairs={{0,1},{1,2},{2,3},{3,4},{4,5},{5,6},{6,7},{7,8},{8,9},{9,10},{10,1... | collective-permute-start | bytes 1179656 | tf_op jit(solution)/shard_map/ppermute | solution.py:20
  259.4 129.5 %all-reduce.3.cloned.1.call-done = (f32[1,256,256]{1,2,0:T(8,128)}, f32[1,256,256]{1,2,0:T(8,128)}) async-done(((f32[1,256,256]{1,2,0:T(8,128)}, f32[1,256,256]{1,2,0:T(8,128)}), (f32[1,256,256]{1,2,0:T(8,128)}, f32[1,256,256]{1,2,0:T(8,128)})) %all-reduce.3.cloned.1.call-update) | async-done | bytes 524304 | tf_op jit(solution)/shard_map/psum | solution.py:145
  399.3 3.9 scatter-add.16
  405.9 3.7 scatter-add.19
  (175 shorter events, 138.0 us)
Async XLA Ops:
  7.2 381.7 %all-reduce.3.cloned.1.call-start = ((), (), s32[]{:S(2)}) async-start(), calls=%async_computation | async-start | bytes 1048576 | tf_op jit(solution)/shard_map/psum | solution.py:145
  9.0 13.2 %copy-start.3 = (f32[2,384,384]{2,1,0:T(8,128)}, f32[2,384,384]{2,1,0:T(8,128)S(1)}, u32[]{:S(2)}) copy-start(f32[2,384,384]{2,1,0:T(8,128)S(1)} %get-tuple-element.256) | copy-start | bytes 3538948
  9.0 18.9 %copy-start.6 = (f32[2,384,384]{2,1,0:T(8,128)}, f32[2,384,384]{2,1,0:T(8,128)S(1)}, u32[]{:S(2)}) copy-start(f32[2,384,384]{2,1,0:T(8,128)S(1)} %get-tuple-element.257) | copy-start | bytes 3538948
  9.0 11.8 %copy-start.19 = (s32[4,1,2]{0,2,1:T(2,128)S(1)}, s32[4,1,2]{0,2,1:T(2,128)}, u32[]{:S(2)}) copy-start(s32[4,1,2]{0,2,1:T(2,128)} %param.16) | copy-start | bytes 100
  9.8 18.1 %collective-permute-start.4 = (f32[2,64,384]{2,1,0:T(8,128)}, f32[2,64,384]{2,1,0:T(8,128)}, u32[]{:S(2)}, u32[]{:S(2)}) collective-permute-start(f32[2,64,384]{2,1,0:T(8,128)} %get-tuple-element.266), channel_id=1, source_target_pairs={{0,16},{16,0},{1,17},{17,1},{2,18},{18,2},{3,19},{19,3},{4,20},{20... | collective-permute-start | bytes 589832 | tf_op jit(solution)/shard_map/ppermute | solution.py:20
  12.8 15.1 %collective-permute-start.5 = (f32[2,64,384]{2,1,0:T(8,128)}, f32[2,64,384]{2,1,0:T(8,128)}, u32[]{:S(2)}, u32[]{:S(2)}) collective-permute-start(f32[2,64,384]{2,1,0:T(8,128)} %get-tuple-element.267), channel_id=1, source_target_pairs={{16,0},{0,16},{17,1},{1,17},{18,2},{2,18},{19,3},{3,19},{20,4},{4,... | collective-permute-start | bytes 589832 | tf_op jit(solution)/shard_map/ppermute | solution.py:23
  13.6 20.2 %collective-permute-start = (f32[2,64,384]{2,1,0:T(8,128)}, f32[2,64,384]{2,1,0:T(8,128)}, u32[]{:S(2)}, u32[]{:S(2)}) collective-permute-start(f32[2,64,384]{2,1,0:T(8,128)} %get-tuple-element.264), channel_id=1, source_target_pairs={{0,16},{16,0},{1,17},{17,1},{2,18},{18,2},{3,19},{19,3},{4,20},{20... | collective-permute-start | bytes 589832 | tf_op jit(solution)/shard_map/ppermute | solution.py:20
  15.6 18.3 %collective-permute-start.1 = (f32[2,64,384]{2,1,0:T(8,128)}, f32[2,64,384]{2,1,0:T(8,128)}, u32[]{:S(2)}, u32[]{:S(2)}) collective-permute-start(f32[2,64,384]{2,1,0:T(8,128)} %get-tuple-element.265), channel_id=1, source_target_pairs={{16,0},{0,16},{17,1},{1,17},{18,2},{2,18},{19,3},{3,19},{20,4},{4,... | collective-permute-start | bytes 589832 | tf_op jit(solution)/shard_map/ppermute | solution.py:23
  22.2 4.4 %copy-start.14 = (f32[4,1,256,256]{3,2,1,0:T(8,128)S(1)}, f32[4,1,256,256]{3,2,1,0:T(8,128)}, u32[]{:S(2)}) copy-start(f32[4,1,256,256]{3,2,1,0:T(8,128)} %param.17) | copy-start | bytes 3145732
  26.6 7.1 %copy-start.15 = (f32[1,256,256]{2,1,0:T(8,128)S(1)}, f32[1,256,256]{2,1,0:T(8,128)}, u32[]{:S(2)}) copy-start(f32[1,256,256]{2,1,0:T(8,128)} %get-tuple-element.281) | copy-start | bytes 786436
  26.6 7.1 %copy-start.16 = (f32[1,256,256]{2,1,0:T(8,128)S(1)}, f32[1,256,256]{2,1,0:T(8,128)}, u32[]{:S(2)}) copy-start(f32[1,256,256]{2,1,0:T(8,128)} %get-tuple-element.282) | copy-start | bytes 786436
  27.9 5.7 %copy-start.17 = (f32[1,256,256]{2,1,0:T(8,128)S(1)}, f32[1,256,256]{2,1,0:T(8,128)}, u32[]{:S(2)}) copy-start(f32[1,256,256]{2,1,0:T(8,128)} %get-tuple-element.283) | copy-start | bytes 786436
  27.9 5.7 %copy-start.18 = (f32[1,256,256]{2,1,0:T(8,128)S(1)}, f32[1,256,256]{2,1,0:T(8,128)}, u32[]{:S(2)}) copy-start(f32[1,256,256]{2,1,0:T(8,128)} %fusion.70) | copy-start | bytes 786436
  29.1 4.7 %copy-start.4 = (f32[2,384,384]{2,1,0:T(8,128)S(1)}, f32[2,384,384]{2,1,0:T(8,128)}, u32[]{:S(2)}) copy-start(f32[2,384,384]{2,1,0:T(8,128)} %copy-done.3) | copy-start | bytes 3538948
  29.1 11.5 %collective-permute-start.6 = (f32[2,512,64]{2,1,0:T(8,128)S(1)}, f32[2,512,64]{2,1,0:T(8,128)S(1)}, u32[]{:S(2)}, u32[]{:S(2)}) collective-permute-start(f32[2,512,64]{2,1,0:T(8,128)S(1)} %get-tuple-element.262), channel_id=1, source_target_pairs={{0,1},{1,2},{2,3},{3,4},{4,5},{5,6},{6,7},{7,8},{8,9},{9,10},{10,1... | collective-permute-start | bytes 786440 | tf_op jit(solution)/shard_map/ppermute | solution.py:20
  29.2 11.4 %collective-permute-start.7 = (f32[2,512,64]{2,1,0:T(8,128)S(1)}, f32[2,512,64]{2,1,0:T(8,128)S(1)}, u32[]{:S(2)}, u32[]{:S(2)}) collective-permute-start(f32[2,512,64]{2,1,0:T(8,128)S(1)} %get-tuple-element.263), channel_id=1, source_target_pairs={{1,0},{2,1},{3,2},{4,3},{5,4},{6,5},{7,6},{8,7},{9,8},{10,9},{11,1... | collective-permute-start | bytes 786440 | tf_op jit(solution)/shard_map/ppermute | solution.py:23
  33.8 6.8 %copy-start.7 = (f32[2,384,384]{2,1,0:T(8,128)S(1)}, f32[2,384,384]{2,1,0:T(8,128)}, u32[]{:S(2)}) copy-start(f32[2,384,384]{2,1,0:T(8,128)} %copy-done.6) | copy-start | bytes 3538948
  36.0 44.7 %collective-permute-start.2 = (f32[2,512,64]{2,1,0:T(8,128)}, f32[2,512,64]{2,1,0:T(8,128)}, u32[]{:S(2)}, u32[]{:S(2)}) collective-permute-start(f32[2,512,64]{2,1,0:T(8,128)} %get-tuple-element.260), channel_id=1, source_target_pairs={{0,1},{1,2},{2,3},{3,4},{4,5},{5,6},{6,7},{7,8},{8,9},{9,10},{10,1... | collective-permute-start | bytes 786440 | tf_op jit(solution)/shard_map/ppermute | solution.py:20
  36.0 44.7 %collective-permute-start.3 = (f32[2,512,64]{2,1,0:T(8,128)}, f32[2,512,64]{2,1,0:T(8,128)}, u32[]{:S(2)}, u32[]{:S(2)}) collective-permute-start(f32[2,512,64]{2,1,0:T(8,128)} %get-tuple-element.261), channel_id=1, source_target_pairs={{1,0},{2,1},{3,2},{4,3},{5,4},{6,5},{7,6},{8,7},{9,8},{10,9},{11,1... | collective-permute-start | bytes 786440 | tf_op jit(solution)/shard_map/ppermute | solution.py:23
  75.4 5.3 %copy-start.5 = (f32[2,384,384]{2,1,0:T(8,128)S(1)}, f32[2,384,384]{2,1,0:T(8,128)}, u32[]{:S(2)}) copy-start(f32[2,384,384]{2,1,0:T(8,128)} %copy-done.3) | copy-start | bytes 3538948
  224.9 9.2 %collective-permute-start.8 = (f32[2,2,64,512]{3,2,1,0:T(8,128)S(1)}, f32[2,2,64,512]{3,2,1,0:T(8,128)S(1)}, u32[]{:S(2)}, u32[]{:S(2)}) collective-permute-start(f32[2,2,64,512]{3,2,1,0:T(8,128)S(1)} %get-tuple-element.239), channel_id=1, source_target_pairs={{0,16},{16,0},{1,17},{17,1},{2,18},{18,2},{3,19},{19,3},{4,20},{20... | collective-permute-start | bytes 1572872 | tf_op jit(solution)/shard_map/ppermute | solution.py:20
  226.6 15.1 %collective-permute-start.9 = (f32[2,2,64,512]{3,2,1,0:T(8,128)S(1)}, f32[2,2,64,512]{3,2,1,0:T(8,128)S(1)}, u32[]{:S(2)}, u32[]{:S(2)}) collective-permute-start(f32[2,2,64,512]{3,2,1,0:T(8,128)S(1)} %get-tuple-element.238), channel_id=1, source_target_pairs={{16,0},{0,16},{17,1},{1,17},{18,2},{2,18},{19,3},{3,19},{20,4},{4,... | collective-permute-start | bytes 1572872 | tf_op jit(solution)/shard_map/ppermute | solution.py:23
  244.6 150.2 %collective-permute-start.10 = (f32[2,2,384,64]{2,3,1,0:T(8,128)S(1)}, f32[2,2,384,64]{2,3,1,0:T(8,128)}, u32[]{:S(2)}, u32[]{:S(2)}) collective-permute-start(f32[2,2,384,64]{2,3,1,0:T(8,128)S(1)} %copy.61), channel_id=1, source_target_pairs={{0,1},{1,2},{2,3},{3,4},{4,5},{5,6},{6,7},{7,8},{8,9},{9,10},{10,1... | collective-permute-start | bytes 1179656 | tf_op jit(solution)/shard_map/ppermute | solution.py:20
  259.4 143.9 %collective-permute-start.11 = (f32[2,2,384,64]{2,3,1,0:T(8,128)}, f32[2,2,384,64]{2,3,1,0:T(8,128)}, u32[]{:S(2)}, u32[]{:S(2)}) collective-permute-start(f32[2,2,384,64]{2,3,1,0:T(8,128)} %copy.63), channel_id=1, source_target_pairs={{1,0},{2,1},{3,2},{4,3},{5,4},{6,5},{7,6},{8,7},{9,8},{10,9},{11,1... | collective-permute-start | bytes 1179656 | tf_op jit(solution)/shard_map/ppermute | solution.py:23
  (9 other events, 30.6 us)
Sparse Core Ops, SparseCore 0:
  257.3 131.5 all-reduce.2
where the time goes:
time: 425 us; the launch traced here: 417 us
  waiting for transfers between devices  141 us (33%)
  local copies, waits for them, and re-layouts  134 us (32%)
  matrix products  44.6 us (10%)
  other arithmetic  41.5 us (10%)
  starting transfers between devices  25.3 us (6%)
  loops' own time  15.9 us (4%)
  between operations  14.8 us (3%)
    psum x1, waiting for transfers between devices, local(): total_re, total_im = lax.psum((probe_re, probe_im), ('row', 'col'))  130 us
    dynamic_update_slice x4, local copies, waits for them, and re-layouts, add_window(): lax.dynamic_update_slice(gathered, current + stacked[index], (0, 0, start...  47.4 us
    gather x40, local copies, waits for them, and re-layouts  34.4 us
    dot_general x6, matrix products, transform(): return jnp.einsum('pcnm,dckm->pdnk', first, table, precision=HIGH)  23.4 us
    dot_general x6, matrix products, transform(): first = jnp.einsum('dckn,pcnm->pdkm', table, field, precision=HIGH)  21.1 us
    ppermute x6, starting transfers between devices, padded(): lax.ppermute(lax.slice_in_dim(block, block.shape[dim] - width, None, axis...  16 us
    another operation x1, loops' own time, local(): lax.fori_loop(0, count, add_window, jnp.zeros((slices, 2, span, span), jn...  15.6 us
    ppermute x6, starting transfers between devices, padded(): lax.ppermute(lax.slice_in_dim(block, 0, width, axis=dim), axis, backward)  9.25 us
  transfers between devices with their start and end apart: 13, of which 4 were waited for; matrix products, arithmetic and copies ran while one was open for 19% of the time, Pallas kernels for 0%

commit v1 on v0

v1 whole, which is shorter than its diff:
```python
import functools
import math

import jax
import jax.numpy as jnp
import numpy as np
from jax import lax
from jax.experimental import pallas as pl
from jax.experimental.pallas import tpu as pltpu
from jax.sharding import PartitionSpec as P

HALO = 64
LANES = 128
F32 = jnp.float32
BF16 = jnp.bfloat16
VMEM = pl.BlockSpec(memory_space=pltpu.VMEM)
SMEM = pl.BlockSpec(memory_space=pltpu.SMEM)


def tables(size):
    half = size // 2
    n = np.arange(half)[:, None]
    k = np.arange(half)[None, :]
    parts = []
    for frequency in (2 * k, 2 * k + 1):
        angle = -2.0 * math.pi * (n * frequency % size) / size
        re, im = np.cos(angle) / math.sqrt(size), np.sin(angle) / math.sqrt(size)
        block = np.block([[re, im], [-im, re]]).astype(np.float32)
        for matrix in (block, block.T):
            high = matrix.astype(jnp.bfloat16)
            low = (matrix - high.astype(np.float32)).astype(jnp.bfloat16)
            parts += [high, low]
    return np.stack(parts)


def split(x):
    high = x.astype(BF16)
    return high, (x - high.astype(F32)).astype(BF16)


def dot(a, b):
    return jnp.dot(a, b, preferred_element_type=F32)


def right(x, t_ref, which):
    high, low = split(x)
    th, tl = t_ref[2 * which], t_ref[2 * which + 1]
    return dot(high, th) + dot(low, th) + dot(high, tl)


def left(t_ref, which, x):
    high, low = split(x)
    th, tl = t_ref[2 * which], t_ref[2 * which + 1]
    return dot(th, high) + dot(th, low) + dot(tl, high)


def forward(t_ref, xr, xi):
    h = xr.shape[0] // 2
    even = right(jnp.concatenate([xr[:, :h] + xr[:, h:], xi[:, :h] + xi[:, h:]], 1), t_ref, 0)
    odd = right(jnp.concatenate([xr[:, :h] - xr[:, h:], xi[:, :h] - xi[:, h:]], 1), t_ref, 2)
    yr = jnp.concatenate([even[:, :h], odd[:, :h]], 1)
    yi = jnp.concatenate([even[:, h:], odd[:, h:]], 1)
    even = left(t_ref, 1, jnp.concatenate([yr[:h] + yr[h:], yi[:h] + yi[h:]], 0))
    odd = left(t_ref, 3, jnp.concatenate([yr[:h] - yr[h:], yi[:h] - yi[h:]], 0))
    zr = jnp.concatenate([even[:h], odd[:h]], 0)
    zi = jnp.concatenate([even[h:], odd[h:]], 0)
    return zr, zi


def inverse(t_ref, zr, zi):
    h = zr.shape[0] // 2
    even = left(t_ref, 0, jnp.concatenate([zr[:h], zi[:h]], 0))
    odd = left(t_ref, 2, jnp.concatenate([zr[h:], zi[h:]], 0))
    p, m = even + odd, even - odd
    yr = jnp.concatenate([p[:h], m[:h]], 0)
    yi = jnp.concatenate([p[h:], m[h:]], 0)
    even = right(jnp.concatenate([yr[:, :h], yi[:, :h]], 1), t_ref, 1)
    odd = right(jnp.concatenate([yr[:, h:], yi[:, h:]], 1), t_ref, 3)
    p, m = even + odd, even - odd
    return jnp.concatenate([p[:, :h], m[:, :h]], 1), jnp.concatenate([p[:, h:], m[:, h:]], 1)


def call(kernel, out_shape, flops=0, **kwargs):
    return pl.pallas_call(
        kernel,
        out_shape=out_shape,
        cost_estimate=pl.CostEstimate(flops=flops, bytes_accessed=4 << 20, transcendentals=0),
        compiler_params=pltpu.CompilerParams(vmem_limit_bytes=56 << 20),
        **kwargs,
    )


def shaped(*shape):
    return jax.ShapeDtypeStruct(shape, F32)


def side_by_side(re, im):
    lane = lax.broadcasted_iota(jnp.int32, re.shape, 1)
    turned = pltpu.roll(im, HALO, 1)
    return lane < HALO, turned


def high_rim(re, im):
    low, turned = side_by_side(re, im)
    return jnp.where(low, turned, re)


def low_rim(re, im):
    low, turned = side_by_side(re, im)
    return jnp.where(low, re, turned)


def rims_kernel(x_ref, high_ref, low_ref):
    for s in range(x_ref.shape[0]):
        high_ref[s] = high_rim(x_ref[s, 0, :, -LANES:], x_ref[s, 1, :, -LANES:])
        low_ref[s] = low_rim(x_ref[s, 0, :, :LANES], x_ref[s, 1, :, :LANES])


def rims(x):
    slices, _, rows, _ = x.shape
    out = shaped(slices, rows, LANES)
    return call(rims_kernel, (out, out), in_specs=[VMEM], out_specs=(VMEM, VMEM))(x)


def exact(x):
    first = x.astype(BF16)
    rest = x - first.astype(F32)
    second = rest.astype(BF16)
    return first, second, (rest - second.astype(F32)).astype(BF16)


def unmixed(x):
    size = x.shape[1]
    half = size // 2

    def choose(dim):
        i = lax.broadcasted_iota(jnp.int32, (size, size), dim)
        j = lax.broadcasted_iota(jnp.int32, (size, size), 1 - dim)
        picked = jnp.where(j < half, 2 * j, 2 * (j - half) + 1)
        return jnp.where(i == picked, 1.0, 0.0).astype(BF16)

    across, down = choose(0), choose(1)
    a, b, c = exact(x)
    a, b, c = exact(dot(a, across) + dot(b, across) + dot(c, across))
    return dot(down, a) + dot(down, b) + dot(down, c)


def prepare_kernel(phase_ref, amp_ref, prop_ref, out_ref):
    phase = unmixed(phase_ref[...])
    prop_ref[0] = jnp.cos(phase)
    prop_ref[1] = jnp.sin(phase)

    @pl.loop(0, amp_ref.shape[0])
    def _(p):
        out_ref[p] = unmixed(amp_ref[p])


def prepare(phase, amplitudes):
    count, size, _ = amplitudes.shape
    return call(
        prepare_kernel,
        (shaped(2, size, size), shaped(count, size, size)),
        flops=1 << 29,
        in_specs=[VMEM, VMEM],
        out_specs=(VMEM, VMEM),
    )(phase, amplitudes)


def assemble(ext, tile, rows, high, low, corner_high, corner_low):
    size = tile.shape[1]
    end = LANES + size
    spans = ((0, rows, 0, HALO), (HALO, None, 0, size), (HALO + size, rows, HALO, HALO))
    for top, strip, source, length in spans:
        here = pl.ds(top, length)
        there = pl.ds(source, length)
        for c in range(2):
            ext[c, here, LANES:end] = tile[c] if strip is None else strip[c, there, :]
        h = high[...] if strip is None else corner_high[there, :]
        w = low[...] if strip is None else corner_low[there, :]
        ext[0, here, 0:LANES] = h
        ext[1, here, 0:LANES] = pltpu.roll(h, HALO, 1)
        ext[0, here, end : end + LANES] = w
        ext[1, here, end : end + LANES] = pltpu.roll(w, HALO, 1)


def place(off_ref, p):
    row = off_ref[p, 0]
    col = off_ref[p, 1] + HALO
    base = pl.multiple_of(col // LANES * LANES, LANES)
    return row // 8 * 8, row % 8, base, col % LANES


def window(ext, off_ref, p, c, size):
    row, dr, base, dc = place(off_ref, p)
    slab = ext[c, pl.ds(pl.multiple_of(row, 8), size + 8), pl.ds(base, size + LANES)]
    wide, tall = size + LANES, size + 8
    slab = pltpu.roll(slab, wide - dc, 1)[:, :size]
    return pltpu.roll(slab, tall - dr, 0)[:size]


def add_window(acc, off_ref, p, c, value):
    size = value.shape[0]
    row, dr, base, dc = place(off_ref, p)
    value = jnp.concatenate([value, jnp.zeros((8, size), F32)], 0)
    value = pltpu.roll(value, dr, 0)
    value = jnp.concatenate([value, jnp.zeros((size + 8, LANES), F32)], 1)
    value = pltpu.roll(value, dc, 1)
    at = (c, pl.ds(pl.multiple_of(row, 8), size + 8), pl.ds(base, size + LANES))
    acc[at] = acc[at] + value


def times(ar, ai, br, bi):
    return ar * br - ai * bi, ar * bi + ai * br


def conj_times(ar, ai, br, bi):
    return ar * br + ai * bi, ar * bi - ai * br


def first_kernel(off, tile, rows, high, low, ch, cl, probe, prop, t, psi_out, w_out, ext):
    p = pl.program_id(0)
    size = probe.shape[1]

    @pl.when(p == 0)
    def _():
        assemble(ext, tile, rows, high, low, ch, cl)

    wr, wi = window(ext, off, p, 0, size), window(ext, off, p, 1, size)
    w_out[0, 0] = wr
    w_out[0, 1] = wi
    fr, fi = forward(t, *times(probe[0], probe[1], wr, wi))
    xr, xi = inverse(t, *times(prop[0], prop[1], fr, fi))
    psi_out[0, 0] = xr
    psi_out[0, 1] = xi


def leave(acc, tile_out, high_out, low_out, span):
    end = acc.shape[2] - LANES
    for c in range(2):
        tile_out[c] = acc[c, 0:span, LANES:end]
    high_out[...] = high_rim(acc[0, 0:span, 0:LANES], acc[1, 0:span, 0:LANES])
    low_out[...] = low_rim(acc[0, 0:span, end:], acc[1, 0:span, end:])


def second_kernel(
    off, tile, rows, high, low, ch, cl, psi, amp, t, u_out, tile_out, high_out, low_out, ext, acc
):
    p = pl.program_id(0)
    size = psi.shape[2]

    @pl.when(p == 0)
    def _():
        assemble(ext, tile, rows, high, low, ch, cl)
        acc[...] = jnp.zeros_like(acc)

    wr, wi = window(ext, off, p, 0, size), window(ext, off, p, 1, size)
    fr, fi = forward(t, *times(psi[0, 0], psi[0, 1], wr, wi))
    magnitude = jnp.sqrt(fr * fr + fi * fi)
    keep = 1.0 - amp[0] / jnp.maximum(magnitude, 0.5)
    br, bi = inverse(t, fr * keep, fi * keep)
    ur, ui = conj_times(window(ext, off, p, 0, size), window(ext, off, p, 1, size), br, bi)
    u_out[0, 0] = ur
    u_out[0, 1] = ui
    gr, gi = conj_times(psi[0, 0], psi[0, 1], br, bi)
    add_window(acc, off, p, 0, gr)
    add_window(acc, off, p, 1, gi)

    @pl.when(p == pl.num_programs(0) - 1)
    def _():
        leave(acc, tile_out, high_out, low_out, tile_out.shape[1])


def third_kernel(
    off, u, w, probe, prop, t, sum_out, tile_out, high_out, low_out, acc
):
    p = pl.program_id(0)

    @pl.when(p == 0)
    def _():
        acc[...] = jnp.zeros_like(acc)
        sum_out[...] = jnp.zeros_like(sum_out)

    fr, fi = forward(t, u[0, 0], u[0, 1])
    br, bi = inverse(t, *conj_times(prop[0], prop[1], fr, fi))
    sr, si = conj_times(w[0, 0], w[0, 1], br, bi)
    sum_out[0] += sr
    sum_out[1] += si
    gr, gi = conj_times(probe[0], probe[1], br, bi)
    add_window(acc, off, p, 0, gr)
    add_window(acc, off, p, 1, gi)

    @pl.when(p == pl.num_programs(0) - 1)
    def _():
        leave(acc, tile_out, high_out, low_out, tile_out.shape[1])


def merge_kernel(x_ref, from_right, from_left, inner_ref, strip_ref):
    span = x_ref.shape[1]
    size = span - 2 * HALO
    for c in range(2):
        h, w = from_right[...], from_left[...]
        if c:
            h, w = pltpu.roll(h, HALO, 1), pltpu.roll(w, HALO, 1)
        lane = lax.broadcasted_iota(jnp.int32, h.shape, 1)
        h = jnp.where(lane < HALO, 0.0, h)
        w = jnp.where(lane < HALO, w, 0.0)
        full = jnp.concatenate(
            [x_ref[c, :, :LANES] + w, x_ref[c, :, LANES:-LANES], x_ref[c, :, -LANES:] + h], 1
        )
        inner_ref[c] = full[HALO : HALO + size]
        strip_ref[c, 0:HALO] = full[0:HALO]
        strip_ref[c, HALO:] = full[HALO + size :]


def finish_kernel(inner0, strip0, inner1, strip1, out_ref):
    for s, (inner, strip) in enumerate(((inner0, strip0), (inner1, strip1))):
        for c in range(2):
            size = inner.shape[1]
            out_ref[s, c] = inner[c]
            out_ref[s, c, 0:HALO] += strip[c, HALO:]
            out_ref[s, c, size - HALO :] += strip[c, 0:HALO]


def shift(x, axis, by):
    count = lax.axis_size(axis)
    return lax.ppermute(x, axis, [(i, (i + by) % count) for i in range(count)])


def to_both(strips, axis, width, by):
    if lax.axis_size(axis) == 2:
        return shift(strips, axis, 1)
    return jnp.concatenate(
        [shift(strips[:, :width], axis, by), shift(strips[:, width:], axis, -by)], axis=1
    )


def total(x):
    sizes = {axis: lax.axis_size(axis) for axis in ("row", "col")}
    bits = [("col", 1), ("col", 2), ("row", 1)]
    bits = [(axis, bit) for axis, bit in bits if bit < sizes[axis]]
    rest = []
    for axis in ("col", "row"):
        bit = 1
        while bit < sizes[axis]:
            if (axis, bit) not in bits:
                rest.append((axis, bit))
            bit *= 2

    def swap(y, axis, bit):
        return lax.ppermute(y, axis, [(i, i ^ bit) for i in range(sizes[axis])])

    for axis, bit in bits:
        half = x.shape[0] // 2
        upper = lax.axis_index(axis) // bit % 2
        mine = lax.dynamic_slice_in_dim(x, upper * half, half, 0)
        other = lax.dynamic_slice_in_dim(x, (1 - upper) * half, half, 0)
        x = mine + swap(other, axis, bit)
    for axis, bit in rest:
        x = x + swap(x, axis, bit)
    for axis, bit in reversed(bits):
        upper = lax.axis_index(axis) // bit % 2
        other = swap(x, axis, bit)
        x = jnp.where(upper == 0, jnp.concatenate([x, other]), jnp.concatenate([other, x]))
    return x


def local(object_field, offsets, amplitudes, probe, phase):
    tile = object_field.shape[2]
    size = probe.shape[1]
    count = offsets.shape[0]
    off = offsets[:, 0]
    span = tile + 2 * HALO
    ext = pltpu.VMEM((2, span + 8, tile + 2 * LANES), F32)
    t = jnp.asarray(tables(size))
    flops = count * 2 * 4 * 3 * 2 * size**3

    received = []
    for s in range(2):
        edges = jnp.concatenate(
            [object_field[s, :, tile - HALO :], object_field[s, :, :HALO]], axis=1
        )
        received.append(to_both(edges, "row", HALO, 1))
    high, low = rims(object_field)
    high, low = shift(high, "col", 1), shift(low, "col", -1)
    corners = []
    for s in range(2):
        ch, cl = rims(received[s][None])
        corners.append((shift(ch[0], "col", 1), shift(cl[0], "col", -1)))
    prop, amp = prepare(phase, amplitudes[:, 0])

    def block(*shape):
        return pl.BlockSpec((1, *shape), lambda p: (p,) + (0,) * len(shape))

    one = block(2, size, size)
    field = shaped(count, 2, size, size)
    psi, w0 = call(
        first_kernel,
        (field, field),
        flops=flops,
        grid=(count,),
        in_specs=[SMEM] + [VMEM] * 9,
        out_specs=(one, one),
        scratch_shapes=[ext],
    )(off, object_field[0], received[0], high[0], low[0], *corners[0], probe, prop, t)
    left_over = (shaped(2, span, tile), shaped(span, LANES), shaped(span, LANES))
    u, tile1, high1, low1 = call(
        second_kernel,
        (field, *left_over),
        flops=flops,
        grid=(count,),
        in_specs=[SMEM] + [VMEM] * 6 + [one, block(size, size), VMEM],
        out_specs=(one, VMEM, VMEM, VMEM),
        scratch_shapes=[ext, ext],
    )(off, object_field[1], received[1], high[1], low[1], *corners[1], psi, amp, t)
    merge = call(
        merge_kernel,
        (shaped(2, tile, tile), shaped(2, 2 * HALO, tile)),
        in_specs=[VMEM] * 3,
        out_specs=(VMEM, VMEM),
    )
    inner1, strip1 = merge(tile1, shift(high1, "col", -1), shift(low1, "col", 1))
    back1 = to_both(strip1, "row", HALO, -1)
    partial, tile0, high0, low0 = call(
        third_kernel,
        (shaped(2, size, size), *left_over),
        flops=flops,
        grid=(count,),
        in_specs=[SMEM, one, one] + [VMEM] * 3,
        out_specs=(VMEM, VMEM, VMEM, VMEM),
        scratch_shapes=[ext],
    )(off, u, w0, probe, prop, t)
    inner0, strip0 = merge(tile0, shift(high0, "col", -1), shift(low0, "col", 1))
    back0 = to_both(strip0, "row", HALO, -1)
    grad = call(
        finish_kernel,
        shaped(2, 2, tile, tile),
        in_specs=[VMEM] * 4,
        out_specs=VMEM,
    )(inner0, back0, inner1, back1)
    everyone = count * lax.axis_size("row") * lax.axis_size("col")
    summed = total(partial.reshape(2 * size, size)) * (1.0 / math.sqrt(everyone))
    return grad, summed.reshape(2, size, size)


def solution(mesh):
    in_specs = (
        P(None, None, "row", "col"),
        P("row", "col", None),
        P("row", "col", None, None),
        P(),
        P(),
    )
    out_specs = (P(None, None, "row", "col"), P())
    return jax.shard_map(local, mesh=mesh, in_specs=in_specs, out_specs=out_specs, check_vma=False)
```

time: 425 us -> 139 us (0.33); the launches traced: 417 us -> 138 us
  local copies, waits for them, and re-layouts: 134 us -> 11.2 us
  waiting for transfers between devices: 141 us -> 34.9 us
  Pallas kernels: 0 us -> 59.1 us
  matrix products: 44.6 us -> 0 us
  other arithmetic: 41.5 us -> 1.96 us
  loops' own time: 15.9 us -> 0 us
  between operations: 14.8 us -> 0.91 us
  starting transfers between devices: 25.3 us -> 30.3 us
    psum x1 -> x0, waiting for transfers between devices: 130 us -> none  [local(): total_re, total_im = lax.psum((probe_re, probe_im), ('row', 'col'))]
    pallas_call x0 -> x10, Pallas kernels: none -> 59.1 us  [the longest x1 14.2 us: local(): call(second_kernel, (field, *left_over), flops=flops, grid=(count,), in_s...]
    dynamic_update_slice x4 -> x0, local copies, waits for them, and re-layouts: 47.4 us -> none  [add_window(): lax.dynamic_update_slice(gathered, current + stacked[index], (0, 0, start...]
    dot_general x12 -> x0, matrix products: 44.6 us -> none  [the longest x6 23.4 us: transform(): return jnp.einsum('pcnm,dckm->pdnk', first, table, precision=HIGH)]
    gather x40 -> x0, local copies, waits for them, and re-layouts: 34.4 us -> none
    ppermute x12 -> x22, waiting for transfers between devices: 11.5 us -> 34.9 us  [the longest x8 17.5 us: swap(): return lax.ppermute(y, axis, [(i, i ^ bit) for i in range(sizes[axis])])]
    another operation x3 -> x0, loops' own time: 15.9 us -> none  [the longest x1 15.6 us: local(): lax.fori_loop(0, count, add_window, jnp.zeros((slices, 2, span, span), jn...]
    slice x11 -> x0, local copies, waits for them, and re-layouts: 14.1 us -> none  [the longest x2 3.59 us: local(): inner[:, :, :, 0:HALO]]
  transfers between devices with their start and end apart: 13 -> 22, of which waited for: 4 -> 11; matrix products, arithmetic and copies ran while one was open for 19% -> 3% of each run, Pallas kernels for 0% -> 24%
where the time goes in v1:
time: 139 us; the launch traced here: 138 us
  Pallas kernels  59.1 us (43%)
  waiting for transfers between devices  34.9 us (25%)
  starting transfers between devices  30.3 us (22%)
  local copies, waits for them, and re-layouts  11.2 us (8%)
  other arithmetic  1.96 us (1%)
    ppermute x14, starting transfers between devices, shift(): return lax.ppermute(x, axis, [(i, (i + by) % count) for i in range(count)])  22.4 us
    ppermute x8, waiting for transfers between devices, swap(): return lax.ppermute(y, axis, [(i, i ^ bit) for i in range(sizes[axis])])  17.5 us
    ppermute x14, waiting for transfers between devices, shift(): return lax.ppermute(x, axis, [(i, (i + by) % count) for i in range(count)])  17.3 us
    pallas_call x1, Pallas kernels, local(): call(second_kernel, (field, *left_over), flops=flops, grid=(count,), in_s...  14.2 us
    pallas_call x1, Pallas kernels, local(): call(third_kernel, (shaped(2, size, size), *left_over), flops=flops, grid...  11.7 us
    pallas_call x1, Pallas kernels, local(): call(first_kernel, (field, field), flops=flops, grid=(count,), in_specs=[...  11 us
    ppermute x8, starting transfers between devices, swap(): return lax.ppermute(y, axis, [(i, i ^ bit) for i in range(sizes[axis])])  7.88 us
    pallas_call x1, Pallas kernels, prepare(): call(prepare_kernel, (shaped(2, size, size), shaped(count, size, size)),...  6.63 us
  transfers between devices with their start and end apart: 22, of which 11 were waited for; matrix products, arithmetic and copies ran while one was open for 3% of the time, Pallas kernels for 24%

profile of v1, /device:TPU:0, one launch (start us, length us, event | category | flops | bytes accessed | tf_op | source)
XLA Modules:
  0.0 138.2 jit_solution(1125292363719150373)
XLA Ops:
  2.0 3.1 %collective-permute-start = (f32[2,128,384]{2,1,0:T(8,128)S(1)}, f32[2,128,384]{2,1,0:T(8,128)S(1)}, u32[]{:S(2)}, u32[]{:S(2)}) collective-permute-start(f32[2,128,384]{2,1,0:T(8,128)S(1)} %pad_maximum_fusion), channel_id=1, source_target_pairs={{0,16},{16,0},{1,17},{17,1},{2,18},{18,2},{3,19},{19,3},{4,20},{20... | collective-permute-start | bytes 1179656 | tf_op jit(solution)/shard_map/ppermute | solution.py:326
  5.1 2.9 %shard_map.77 = (f32[2,384,128]{2,1,0:T(8,128)}, f32[2,384,128]{2,1,0:T(8,128)}) custom-call(f32[2,2,384,384]{3,2,1,0:T(8,128)} %x_ref.1), custom_call_target="tpu_custom_call" | custom-call | bytes 4194304 | tf_op jit(solution)/shard_map/pallas_call | solution.py:122
  8.1 4.4 %collective-permute-start.2 = (f32[2,384,128]{2,1,0:T(8,128)}, f32[2,384,128]{2,1,0:T(8,128)S(1)}, u32[]{:S(2)}, u32[]{:S(2)}) collective-permute-start(f32[2,384,128]{2,1,0:T(8,128)} %get-tuple-element.25), channel_id=1, source_target_pairs={{0,15},{1,0},{2,1},{3,2},{4,3},{5,4},{6,5},{7,6},{8,7},{9,8},{10,9... | collective-permute-start | bytes 1179656 | tf_op jit(solution)/shard_map/ppermute | solution.py:326
  14.7 6.6 %shard_map.80 = (f32[2,256,256]{2,1,0:T(8,128)}, f32[4,256,256]{2,1,0:T(8,128)}) custom-call(f32[256,256]{1,0:T(8,128)} %phase_ref.1, f32[4,256,256]{2,1,0:T(8,128)} %bitcast.36), custom_call_target="tpu_custom_call" | custom-call | flops 536870912 | bytes 4194304 | tf_op jit(solution)/shard_map/pallas_call | solution.py:160
  22.2 1.7 %shard_map.78 = (f32[1,128,128]{2,1,0:T(8,128)}, f32[1,128,128]{2,1,0:T(8,128)}) custom-call(f32[1,2,128,384]{3,2,1,0:T(8,128)} %bitcast.33), custom_call_target="tpu_custom_call" | custom-call | bytes 4194304 | tf_op jit(solution)/shard_map/pallas_call | solution.py:122
  23.9 4.4 %collective-permute-start.4 = (f32[128,128]{1,0:T(8,128)}, f32[128,128]{1,0:T(8,128)S(1)}, u32[]{:S(2)}, u32[]{:S(2)}) collective-permute-start(f32[128,128]{1,0:T(8,128)} %bitcast.37), channel_id=1, source_target_pairs={{0,15},{1,0},{2,1},{3,2},{4,3},{5,4},{6,5},{7,6},{8,7},{9,8},{10,9... | collective-permute-start | bytes 196616 | tf_op jit(solution)/shard_map/ppermute | solution.py:326
  30.8 4.4 %collective-permute-start.7 = (f32[128,128]{1,0:T(8,128)}, f32[128,128]{1,0:T(8,128)S(1)}, u32[]{:S(2)}, u32[]{:S(2)}) collective-permute-start(f32[128,128]{1,0:T(8,128)} %bitcast.39), channel_id=1, source_target_pairs={{0,15},{1,0},{2,1},{3,2},{4,3},{5,4},{6,5},{7,6},{8,7},{9,8},{10,9... | collective-permute-start | bytes 196616 | tf_op jit(solution)/shard_map/ppermute | solution.py:326
  38.1 11.0 %shard_map.81 = (f32[4,2,256,256]{3,2,1,0:T(8,128)}, f32[4,2,256,256]{3,2,1,0:T(8,128)}) custom-call(s32[4,2]{1,0:T(4,128)} %copy.10.off, f32[2,384,384]{2,1,0:T(8,128)} %get-tuple-element.50.tile, f32[2,128,384]{2,1,0:T(8,128)} %copy-done.2, f32[384,128]{1,0:T(8,128)} %get-tuple-element.54.high, f32[384,128]{1,0:T(8,128)} %get-tuple-element.52.low, ...), custom_call_target="tpu_custom_call" | custom-call | flops 3221225472 | bytes 4194304 | tf_op jit(solution)/shard_map/pallas_call | solution.py:396
  49.8 14.2 %shard_map.82 = (f32[4,2,256,256]{3,2,1,0:T(8,128)}, f32[2,512,384]{2,1,0:T(8,128)}, f32[512,128]{1,0:T(8,128)}, f32[512,128]{1,0:T(8,128)}) custom-call(s32[4,2]{1,0:T(4,128)} %copy.10.off, f32[2,384,384]{2,1,0:T(8,128)} %get-tuple-element.51.tile, f32[2,128,384]{2,1,0:T(8,128)} %copy-done.1, f32[384,128]{1,0:T(8,128)} %get-tuple-element.55.high, ...), custom_call_target="tpu_custom_call" | custom-call | flops 3221225472 | bytes 4194304 | tf_op jit(solution)/shard_map/pallas_call | solution.py:406
  64.0 11.7 %shard_map.83 = (f32[2,256,256]{2,1,0:T(8,128)}, f32[2,512,384]{2,1,0:T(8,128)}, f32[512,128]{1,0:T(8,128)}, f32[512,128]{1,0:T(8,128)}) custom-call(s32[4,2]{1,0:T(4,128)} %copy.10.off, f32[4,2,256,256]{3,2,1,0:T(8,128)} %get-tuple-element.33.u, f32[4,2,256,256]{3,2,1,0:T(8,128)} %get-tuple-element.34.w, f32[2,256,256]{2,1,0:T(8,128)} %probe.3, ...), custom_call_target="tpu_custom_call" | custom-call | flops 3221225472 | bytes 4194304 | tf_op jit(solution)/shard_map/pallas_call | solution.py:423
  79.5 5.5 %collective-permute-done.15 = f32[128,256]{1,0:T(8,128)S(1)} collective-permute-done((f32[128,256]{1,0:T(8,128)S(1)}, f32[128,256]{1,0:T(8,128)S(1)}, u32[]{:S(2)}, u32[]{:S(2)}) %collective-permute-start.15) | collective-permute-done | bytes 131104 | tf_op jit(solution)/shard_map/ppermute | solution.py:350
  85.1 1.9 %collective-permute-start.16 = (f32[64,256]{1,0:T(8,128)S(1)}, f32[64,256]{1,0:T(8,128)S(1)}, u32[]{:S(2)}, u32[]{:S(2)}) collective-permute-start(f32[64,256]{1,0:T(8,128)S(1)} %constant_dynamic-slice_fusion), channel_id=1, source_target_pairs={{0,16},{16,0},{1,17},{17,1},{2,18},{18,2},{3,19},{19,3},{4,20},{20... | collective-permute-start | bytes 196616 | tf_op jit(solution)/shard_map/ppermute | solution.py:350
  87.0 2.4 %collective-permute-done.16 = f32[64,256]{1,0:T(8,128)S(1)} collective-permute-done((f32[64,256]{1,0:T(8,128)S(1)}, f32[64,256]{1,0:T(8,128)S(1)}, u32[]{:S(2)}, u32[]{:S(2)}) %collective-permute-start.16) | collective-permute-done | bytes 65568 | tf_op jit(solution)/shard_map/ppermute | solution.py:350
  89.5 4.3 %collective-permute-done.17 = f32[64,256]{1,0:T(8,128)S(1)} collective-permute-done((f32[64,256]{1,0:T(8,128)S(1)}, f32[64,256]{1,0:T(8,128)S(1)}, u32[]{:S(2)}, u32[]{:S(2)}) %collective-permute-start.17) | collective-permute-done | bytes 65568 | tf_op jit(solution)/shard_map/ppermute | solution.py:350
  93.8 2.1 %collective-permute-start.18 = (f32[64,256]{1,0:T(8,128)S(1)}, f32[64,256]{1,0:T(8,128)S(1)}, u32[]{:S(2)}, u32[]{:S(2)}) collective-permute-start(f32[64,256]{1,0:T(8,128)S(1)} %add.61), channel_id=1, source_target_pairs={{0,8},{1,9},{2,10},{3,11},{4,12},{5,13},{6,14},{7,15},{8,0},{9,1},... | collective-permute-start | bytes 196616 | tf_op jit(solution)/shard_map/ppermute | solution.py:350
  95.8 3.9 %collective-permute-done.18 = f32[64,256]{1,0:T(8,128)S(1)} collective-permute-done((f32[64,256]{1,0:T(8,128)S(1)}, f32[64,256]{1,0:T(8,128)S(1)}, u32[]{:S(2)}, u32[]{:S(2)}) %collective-permute-start.18) | collective-permute-done | bytes 65568 | tf_op jit(solution)/shard_map/ppermute | solution.py:350
  99.7 1.9 %collective-permute-start.19 = (f32[64,256]{1,0:T(8,128)S(1)}, f32[64,256]{1,0:T(8,128)S(1)}, u32[]{:S(2)}, u32[]{:S(2)}) collective-permute-start(f32[64,256]{1,0:T(8,128)S(1)} %add.62), channel_id=1, source_target_pairs={{0,16},{16,0},{1,17},{17,1},{2,18},{18,2},{3,19},{19,3},{4,20},{20... | collective-permute-start | bytes 196616 | tf_op jit(solution)/shard_map/ppermute | solution.py:350
  102.1 4.0 %collective-permute-start.11 = (f32[512,128]{1,0:T(8,128)S(1)}, f32[512,128]{1,0:T(8,128)S(1)}, u32[]{:S(2)}, u32[]{:S(2)}) collective-permute-start(f32[512,128]{1,0:T(8,128)S(1)} %copy-done.11), channel_id=1, source_target_pairs={{0,15},{1,0},{2,1},{3,2},{4,3},{5,4},{6,5},{7,6},{8,7},{9,8},{10,9... | collective-permute-start | bytes 786440 | tf_op jit(solution)/shard_map/ppermute | solution.py:326
  106.3 4.0 %collective-permute-done.9.from_left = f32[512,128]{1,0:T(8,128)S(1)} collective-permute-done((f32[512,128]{1,0:T(8,128)S(1)}, f32[512,128]{1,0:T(8,128)S(1)}, u32[]{:S(2)}, u32[]{:S(2)}) %collective-permute-start.9) | collective-permute-done | bytes 262176 | tf_op jit(solution)/shard_map/ppermute | solution.py:326
  111.0 2.9 %shard_map.84 = (f32[2,384,384]{2,1,0:T(8,128)}, f32[2,128,384]{2,1,0:T(8,128)}) custom-call(f32[2,512,384]{2,1,0:T(8,128)} %get-tuple-element.35.x_ref, f32[512,128]{1,0:T(8,128)} %copy-done.7, f32[512,128]{1,0:T(8,128)} %copy-done.8), custom_call_target="tpu_custom_call" | custom-call | bytes 4194304 | tf_op jit(solution)/shard_map/pallas_call | solution.py:432
  115.4 2.9 %shard_map.85 = (f32[2,384,384]{2,1,0:T(8,128)}, f32[2,128,384]{2,1,0:T(8,128)}) custom-call(f32[2,512,384]{2,1,0:T(8,128)} %get-tuple-element.40.x_ref, f32[512,128]{1,0:T(8,128)} %copy-done.5, f32[512,128]{1,0:T(8,128)} %copy-done.6), custom_call_target="tpu_custom_call" | custom-call | bytes 4194304 | tf_op jit(solution)/shard_map/pallas_call | solution.py:421
  121.3 3.6 %collective-permute-done.10.strip0 = f32[2,128,384]{2,1,0:T(8,128)S(1)} collective-permute-done((f32[2,128,384]{2,1,0:T(8,128)}, f32[2,128,384]{2,1,0:T(8,128)S(1)}, u32[]{:S(2)}, u32[]{:S(2)}) %collective-permute-start.10) | collective-permute-done | bytes 393248 | tf_op jit(solution)/shard_map/ppermute | solution.py:326
  124.8 8.4 %collective-permute-done.13.strip1 = f32[2,128,384]{2,1,0:T(8,128)S(1)} collective-permute-done((f32[2,128,384]{2,1,0:T(8,128)}, f32[2,128,384]{2,1,0:T(8,128)S(1)}, u32[]{:S(2)}, u32[]{:S(2)}) %collective-permute-start.13) | collective-permute-done | bytes 393248 | tf_op jit(solution)/shard_map/ppermute | solution.py:326
  134.0 3.4 %shard_map.86 = f32[2,2,384,384]{3,2,1,0:T(8,128)} custom-call(f32[2,384,384]{2,1,0:T(8,128)} %get-tuple-element.38.inner0, f32[2,128,384]{2,1,0:T(8,128)} %copy-done.3, f32[2,384,384]{2,1,0:T(8,128)} %get-tuple-element.43.inner1, f32[2,128,384]{2,1,0:T(8,128)} %copy-done.4), custom_call_target="tpu_custom_call" | custom-call | bytes 4194304 | tf_op jit(solution)/shard_map/pallas_call | solution.py:434
  (84 shorter events, 21.7 us)
Async XLA Ops:
  2.0 19.4 %collective-permute-start = (f32[2,128,384]{2,1,0:T(8,128)S(1)}, f32[2,128,384]{2,1,0:T(8,128)S(1)}, u32[]{:S(2)}, u32[]{:S(2)}) collective-permute-start(f32[2,128,384]{2,1,0:T(8,128)S(1)} %pad_maximum_fusion), channel_id=1, source_target_pairs={{0,16},{16,0},{1,17},{17,1},{2,18},{18,2},{3,19},{19,3},{4,20},{20... | collective-permute-start | bytes 1179656 | tf_op jit(solution)/shard_map/ppermute | solution.py:326
  5.0 23.3 %collective-permute-start.5 = (f32[2,128,384]{2,1,0:T(8,128)S(1)}, f32[2,128,384]{2,1,0:T(8,128)S(1)}, u32[]{:S(2)}, u32[]{:S(2)}) collective-permute-start(f32[2,128,384]{2,1,0:T(8,128)S(1)} %pad_maximum_fusion.1), channel_id=1, source_target_pairs={{0,16},{16,0},{1,17},{17,1},{2,18},{18,2},{3,19},{19,3},{4,20},{20... | collective-permute-start | bytes 1179656 | tf_op jit(solution)/shard_map/ppermute | solution.py:326
  8.1 22.8 %collective-permute-start.1 = (f32[2,384,128]{2,1,0:T(8,128)}, f32[2,384,128]{2,1,0:T(8,128)S(1)}, u32[]{:S(2)}, u32[]{:S(2)}) collective-permute-start(f32[2,384,128]{2,1,0:T(8,128)} %get-tuple-element.24), channel_id=1, source_target_pairs={{0,1},{1,2},{2,3},{3,4},{4,5},{5,6},{6,7},{7,8},{8,9},{9,10},{10,1... | collective-permute-start | bytes 1179656 | tf_op jit(solution)/shard_map/ppermute | solution.py:326
  8.1 28.0 %collective-permute-start.2 = (f32[2,384,128]{2,1,0:T(8,128)}, f32[2,384,128]{2,1,0:T(8,128)S(1)}, u32[]{:S(2)}, u32[]{:S(2)}) collective-permute-start(f32[2,384,128]{2,1,0:T(8,128)} %get-tuple-element.25), channel_id=1, source_target_pairs={{0,15},{1,0},{2,1},{3,2},{4,3},{5,4},{6,5},{7,6},{8,7},{9,8},{10,9... | collective-permute-start | bytes 1179656 | tf_op jit(solution)/shard_map/ppermute | solution.py:326
  23.9 25.3 %collective-permute-start.3 = (f32[128,128]{1,0:T(8,128)}, f32[128,128]{1,0:T(8,128)S(1)}, u32[]{:S(2)}, u32[]{:S(2)}) collective-permute-start(f32[128,128]{1,0:T(8,128)} %bitcast.38), channel_id=1, source_target_pairs={{0,1},{1,2},{2,3},{3,4},{4,5},{5,6},{6,7},{7,8},{8,9},{9,10},{10,1... | collective-permute-start | bytes 196616 | tf_op jit(solution)/shard_map/ppermute | solution.py:326
  23.9 25.3 %collective-permute-start.4 = (f32[128,128]{1,0:T(8,128)}, f32[128,128]{1,0:T(8,128)S(1)}, u32[]{:S(2)}, u32[]{:S(2)}) collective-permute-start(f32[128,128]{1,0:T(8,128)} %bitcast.37), channel_id=1, source_target_pairs={{0,15},{1,0},{2,1},{3,2},{4,3},{5,4},{6,5},{7,6},{8,7},{9,8},{10,9... | collective-permute-start | bytes 196616 | tf_op jit(solution)/shard_map/ppermute | solution.py:326
  30.8 6.6 %collective-permute-start.6 = (f32[128,128]{1,0:T(8,128)}, f32[128,128]{1,0:T(8,128)S(1)}, u32[]{:S(2)}, u32[]{:S(2)}) collective-permute-start(f32[128,128]{1,0:T(8,128)} %bitcast.40), channel_id=1, source_target_pairs={{0,1},{1,2},{2,3},{3,4},{4,5},{5,6},{6,7},{7,8},{8,9},{9,10},{10,1... | collective-permute-start | bytes 196616 | tf_op jit(solution)/shard_map/ppermute | solution.py:326
  30.8 6.7 %collective-permute-start.7 = (f32[128,128]{1,0:T(8,128)}, f32[128,128]{1,0:T(8,128)S(1)}, u32[]{:S(2)}, u32[]{:S(2)}) collective-permute-start(f32[128,128]{1,0:T(8,128)} %bitcast.39), channel_id=1, source_target_pairs={{0,15},{1,0},{2,1},{3,2},{4,3},{5,4},{6,5},{7,6},{8,7},{9,8},{10,9... | collective-permute-start | bytes 196616 | tf_op jit(solution)/shard_map/ppermute | solution.py:326
  75.7 26.4 %copy-start.11 = (f32[512,128]{1,0:T(8,128)S(1)}, f32[512,128]{1,0:T(8,128)}, u32[]{:S(2)}) copy-start(f32[512,128]{1,0:T(8,128)} %get-tuple-element.41) | copy-start | bytes 786436
  75.7 30.4 %copy-start.10 = (f32[512,128]{1,0:T(8,128)S(1)}, f32[512,128]{1,0:T(8,128)}, u32[]{:S(2)}) copy-start(f32[512,128]{1,0:T(8,128)} %get-tuple-element.42) | copy-start | bytes 786436
  76.8 1.6 %collective-permute-start.14 = (f32[256,256]{1,0:T(8,128)S(1)}, f32[256,256]{1,0:T(8,128)S(1)}, u32[]{:S(2)}, u32[]{:S(2)}) collective-permute-start(f32[256,256]{1,0:T(8,128)S(1)} %constant_dynamic-slice_fusion.2), channel_id=1, source_target_pairs={{0,1},{1,0},{2,3},{3,2},{4,5},{5,4},{6,7},{7,6},{8,9},{9,8},{10,11... | collective-permute-start | bytes 786440 | tf_op jit(solution)/shard_map/ppermute | solution.py:350
  79.4 5.6 %collective-permute-start.15 = (f32[128,256]{1,0:T(8,128)S(1)}, f32[128,256]{1,0:T(8,128)S(1)}, u32[]{:S(2)}, u32[]{:S(2)}) collective-permute-start(f32[128,256]{1,0:T(8,128)S(1)} %constant_dynamic-slice_fusion.1), channel_id=1, source_target_pairs={{0,2},{1,3},{2,0},{3,1},{4,6},{5,7},{6,4},{7,5},{8,10},{9,11},{10,... | collective-permute-start | bytes 393224 | tf_op jit(solution)/shard_map/ppermute | solution.py:350
  85.1 4.3 %collective-permute-start.16 = (f32[64,256]{1,0:T(8,128)S(1)}, f32[64,256]{1,0:T(8,128)S(1)}, u32[]{:S(2)}, u32[]{:S(2)}) collective-permute-start(f32[64,256]{1,0:T(8,128)S(1)} %constant_dynamic-slice_fusion), channel_id=1, source_target_pairs={{0,16},{16,0},{1,17},{17,1},{2,18},{18,2},{3,19},{19,3},{4,20},{20... | collective-permute-start | bytes 196616 | tf_op jit(solution)/shard_map/ppermute | solution.py:350
  89.4 4.3 %collective-permute-start.17 = (f32[64,256]{1,0:T(8,128)S(1)}, f32[64,256]{1,0:T(8,128)S(1)}, u32[]{:S(2)}, u32[]{:S(2)}) collective-permute-start(f32[64,256]{1,0:T(8,128)S(1)} %dynamic-slice_add_fusion.2), channel_id=1, source_target_pairs={{0,4},{1,5},{2,6},{3,7},{4,0},{5,1},{6,2},{7,3},{8,12},{9,13},{10,... | collective-permute-start | bytes 196616 | tf_op jit(solution)/shard_map/ppermute | solution.py:350
  93.8 5.9 %collective-permute-start.18 = (f32[64,256]{1,0:T(8,128)S(1)}, f32[64,256]{1,0:T(8,128)S(1)}, u32[]{:S(2)}, u32[]{:S(2)}) collective-permute-start(f32[64,256]{1,0:T(8,128)S(1)} %add.61), channel_id=1, source_target_pairs={{0,8},{1,9},{2,10},{3,11},{4,12},{5,13},{6,14},{7,15},{8,0},{9,1},... | collective-permute-start | bytes 196616 | tf_op jit(solution)/shard_map/ppermute | solution.py:350
  99.7 6.4 %collective-permute-start.19 = (f32[64,256]{1,0:T(8,128)S(1)}, f32[64,256]{1,0:T(8,128)S(1)}, u32[]{:S(2)}, u32[]{:S(2)}) collective-permute-start(f32[64,256]{1,0:T(8,128)S(1)} %add.62), channel_id=1, source_target_pairs={{0,16},{16,0},{1,17},{17,1},{2,18},{18,2},{3,19},{19,3},{4,20},{20... | collective-permute-start | bytes 196616 | tf_op jit(solution)/shard_map/ppermute | solution.py:350
  101.6 4.6 %collective-permute-start.8 = (f32[512,128]{1,0:T(8,128)S(1)}, f32[512,128]{1,0:T(8,128)S(1)}, u32[]{:S(2)}, u32[]{:S(2)}) collective-permute-start(f32[512,128]{1,0:T(8,128)S(1)} %copy-done.13), channel_id=1, source_target_pairs={{0,15},{1,0},{2,1},{3,2},{4,3},{5,4},{6,5},{7,6},{8,7},{9,8},{10,9... | collective-permute-start | bytes 786440 | tf_op jit(solution)/shard_map/ppermute | solution.py:326
  101.6 8.6 %collective-permute-start.9 = (f32[512,128]{1,0:T(8,128)S(1)}, f32[512,128]{1,0:T(8,128)S(1)}, u32[]{:S(2)}, u32[]{:S(2)}) collective-permute-start(f32[512,128]{1,0:T(8,128)S(1)} %copy-done.12), channel_id=1, source_target_pairs={{0,1},{1,2},{2,3},{3,4},{4,5},{5,6},{6,7},{7,8},{8,9},{9,10},{10,1... | collective-permute-start | bytes 786440 | tf_op jit(solution)/shard_map/ppermute | solution.py:326
  102.1 11.9 %collective-permute-start.11 = (f32[512,128]{1,0:T(8,128)S(1)}, f32[512,128]{1,0:T(8,128)S(1)}, u32[]{:S(2)}, u32[]{:S(2)}) collective-permute-start(f32[512,128]{1,0:T(8,128)S(1)} %copy-done.11), channel_id=1, source_target_pairs={{0,15},{1,0},{2,1},{3,2},{4,3},{5,4},{6,5},{7,6},{8,7},{9,8},{10,9... | collective-permute-start | bytes 786440 | tf_op jit(solution)/shard_map/ppermute | solution.py:326
  106.1 8.6 %collective-permute-start.12 = (f32[512,128]{1,0:T(8,128)S(1)}, f32[512,128]{1,0:T(8,128)S(1)}, u32[]{:S(2)}, u32[]{:S(2)}) collective-permute-start(f32[512,128]{1,0:T(8,128)S(1)} %copy-done.10), channel_id=1, source_target_pairs={{0,1},{1,2},{2,3},{3,4},{4,5},{5,6},{6,7},{7,8},{8,9},{9,10},{10,1... | collective-permute-start | bytes 786440 | tf_op jit(solution)/shard_map/ppermute | solution.py:326
  106.2 13.4 %collective-permute-start.20 = (f32[128,256]{1,0:T(8,128)S(1)}, f32[128,256]{1,0:T(8,128)S(1)}, u32[]{:S(2)}, u32[]{:S(2)}) collective-permute-start(f32[128,256]{1,0:T(8,128)S(1)} %maximum_select_fusion.2), channel_id=1, source_target_pairs={{0,2},{1,3},{2,0},{3,1},{4,6},{5,7},{6,4},{7,5},{8,10},{9,11},{10,... | collective-permute-start | bytes 393224 | tf_op jit(solution)/shard_map/ppermute | solution.py:350
  113.8 11.0 %collective-permute-start.10 = (f32[2,128,384]{2,1,0:T(8,128)}, f32[2,128,384]{2,1,0:T(8,128)S(1)}, u32[]{:S(2)}, u32[]{:S(2)}) collective-permute-start(f32[2,128,384]{2,1,0:T(8,128)} %get-tuple-element.39), channel_id=1, source_target_pairs={{0,16},{16,0},{1,17},{17,1},{2,18},{18,2},{3,19},{19,3},{4,20},{20... | collective-permute-start | bytes 1179656 | tf_op jit(solution)/shard_map/ppermute | solution.py:326
  118.3 14.9 %collective-permute-start.13 = (f32[2,128,384]{2,1,0:T(8,128)}, f32[2,128,384]{2,1,0:T(8,128)S(1)}, u32[]{:S(2)}, u32[]{:S(2)}) collective-permute-start(f32[2,128,384]{2,1,0:T(8,128)} %get-tuple-element.44), channel_id=1, source_target_pairs={{0,16},{16,0},{1,17},{17,1},{2,18},{18,2},{3,19},{19,3},{4,20},{20... | collective-permute-start | bytes 1179656 | tf_op jit(solution)/shard_map/ppermute | solution.py:326
  119.6 17.8 %collective-permute-start.21 = (f32[256,256]{1,0:T(8,128)S(1)}, f32[256,256]{1,0:T(8,128)S(1)}, u32[]{:S(2)}, u32[]{:S(2)}) collective-permute-start(f32[256,256]{1,0:T(8,128)S(1)} %maximum_select_fusion.1), channel_id=1, source_target_pairs={{0,1},{1,0},{2,3},{3,2},{4,5},{5,4},{6,7},{7,6},{8,9},{9,8},{10,11... | collective-permute-start | bytes 786440 | tf_op jit(solution)/shard_map/ppermute | solution.py:350
  (16 other events, 84.7 us)

commit v2 on v1

v2 whole, which is shorter than its diff:
```python
import functools
import math

import jax
import jax.numpy as jnp
import numpy as np
from jax import lax
from jax.experimental import pallas as pl
from jax.experimental.pallas import tpu as pltpu
from jax.sharding import PartitionSpec as P

HALO = 64
ROOM = 20
CUT_ROOM = 56
PREPARE_ROOM = 56
LANES = 128
F32 = jnp.float32
BF16 = jnp.bfloat16
VMEM = pl.BlockSpec(memory_space=pltpu.VMEM)
SMEM = pl.BlockSpec(memory_space=pltpu.SMEM)


def tables(size):
    half = size // 2
    n = np.arange(half)[:, None]
    k = np.arange(half)[None, :]
    parts = []
    for frequency in (2 * k, 2 * k + 1):
        angle = -2.0 * math.pi * (n * frequency % size) / size
        re, im = np.cos(angle) / math.sqrt(size), np.sin(angle) / math.sqrt(size)
        block = np.block([[re, im], [-im, re]]).astype(np.float32)
        for matrix in (block, block.T):
            high = matrix.astype(jnp.bfloat16)
            low = (matrix - high.astype(np.float32)).astype(jnp.bfloat16)
            parts += [high, low]
    return np.stack(parts)


def split(x):
    high = x.astype(BF16)
    return high, (x - high.astype(F32)).astype(BF16)


def dot(a, b):
    return jnp.dot(a, b, preferred_element_type=F32)


def right(x, t_ref, which):
    high, low = split(x)
    th, tl = t_ref[2 * which], t_ref[2 * which + 1]
    return dot(high, th) + dot(low, th) + dot(high, tl)


def left(t_ref, which, x):
    high, low = split(x)
    th, tl = t_ref[2 * which], t_ref[2 * which + 1]
    return dot(th, high) + dot(th, low) + dot(tl, high)


def forward(t_ref, xr, xi):
    h = xr.shape[0] // 2
    even = right(jnp.concatenate([xr[:, :h] + xr[:, h:], xi[:, :h] + xi[:, h:]], 1), t_ref, 0)
    odd = right(jnp.concatenate([xr[:, :h] - xr[:, h:], xi[:, :h] - xi[:, h:]], 1), t_ref, 2)
    yr = jnp.concatenate([even[:, :h], odd[:, :h]], 1)
    yi = jnp.concatenate([even[:, h:], odd[:, h:]], 1)
    even = left(t_ref, 1, jnp.concatenate([yr[:h] + yr[h:], yi[:h] + yi[h:]], 0))
    odd = left(t_ref, 3, jnp.concatenate([yr[:h] - yr[h:], yi[:h] - yi[h:]], 0))
    zr = jnp.concatenate([even[:h], odd[:h]], 0)
    zi = jnp.concatenate([even[h:], odd[h:]], 0)
    return zr, zi


def inverse(t_ref, zr, zi):
    h = zr.shape[0] // 2
    even = left(t_ref, 0, jnp.concatenate([zr[:h], zi[:h]], 0))
    odd = left(t_ref, 2, jnp.concatenate([zr[h:], zi[h:]], 0))
    p, m = even + odd, even - odd
    yr = jnp.concatenate([p[:h], m[:h]], 0)
    yi = jnp.concatenate([p[h:], m[h:]], 0)
    even = right(jnp.concatenate([yr[:, :h], yi[:, :h]], 1), t_ref, 1)
    odd = right(jnp.concatenate([yr[:, h:], yi[:, h:]], 1), t_ref, 3)
    p, m = even + odd, even - odd
    return jnp.concatenate([p[:, :h], m[:, :h]], 1), jnp.concatenate([p[:, h:], m[:, h:]], 1)


def call(kernel, out_shape, flops=0, room=8, **kwargs):
    return pl.pallas_call(
        kernel,
        out_shape=out_shape,
        cost_estimate=pl.CostEstimate(flops=flops, bytes_accessed=4 << 20, transcendentals=0),
        compiler_params=pltpu.CompilerParams(vmem_limit_bytes=room << 20),
        **kwargs,
    )


def shaped(*shape):
    return jax.ShapeDtypeStruct(shape, F32)


def side_by_side(re, im):
    lane = lax.broadcasted_iota(jnp.int32, re.shape, 1)
    turned = pltpu.roll(im, HALO, 1)
    return lane < HALO, turned


def high_rim(re, im):
    low, turned = side_by_side(re, im)
    return jnp.where(low, turned, re)


def low_rim(re, im):
    low, turned = side_by_side(re, im)
    return jnp.where(low, re, turned)


def cut_kernel(x_ref, *refs):
    slices, _, size, _ = x_ref.shape
    edges, (last, first, columns, sem, col_sem) = refs[:slices], refs[slices:]
    rows, cols = [], []
    for s in range(slices):
        for i, start in enumerate((size - HALO, 0)):
            rows.append(
                pltpu.make_async_copy(
                    x_ref.at[s, :, pl.ds(start, HALO), :],
                    edges[s].at[:, pl.ds(i * HALO, HALO), :],
                    sem.at[s, i],
                )
            )
        for i, start in enumerate((size - LANES, 0)):
            cols.append(
                pltpu.make_async_copy(
                    x_ref.at[s, :, :, pl.ds(start, LANES)], columns.at[s, i], col_sem.at[s, i]
                )
            )
    for copy in cols + rows:
        copy.start()
    for s in range(slices):
        cols[2 * s].wait()
        last[s] = high_rim(columns[s, 0, 0], columns[s, 0, 1])
        cols[2 * s + 1].wait()
        first[s] = low_rim(columns[s, 1, 0], columns[s, 1, 1])
    for copy in rows:
        copy.wait()


def cut(x):
    slices, _, size, _ = x.shape
    rim = shaped(slices, size, LANES)
    outs = (shaped(2, 2 * HALO, size),) * slices + (rim, rim)
    return call(
        cut_kernel,
        outs,
        room=CUT_ROOM,
        in_specs=[pl.BlockSpec(memory_space=pltpu.HBM)],
        out_specs=(VMEM,) * len(outs),
        scratch_shapes=[
            pltpu.VMEM((slices, 2, 2, size, LANES), F32),
            pltpu.SemaphoreType.DMA((slices, 2)),
            pltpu.SemaphoreType.DMA((slices, 2)),
        ],
        name="cut",
    )(x)


def row_corners_kernel(rows_ref, high_ref, low_ref):
    high_ref[...] = high_rim(rows_ref[0, :, -LANES:], rows_ref[1, :, -LANES:])
    low_ref[...] = low_rim(rows_ref[0, :, :LANES], rows_ref[1, :, :LANES])


def row_corners(rows):
    out = shaped(2 * HALO, LANES)
    return call(
        row_corners_kernel, (out, out), in_specs=[VMEM], out_specs=(VMEM, VMEM), name="corners"
    )(rows)


def rim_corners_kernel(s, high_ref, low_ref, out_ref):
    for i, ref in enumerate((high_ref, low_ref)):
        out_ref[i, 0:HALO] = ref[s, -HALO:]
        out_ref[i, HALO:] = ref[s, 0:HALO]


def rim_corners(high, low, s):
    return call(
        functools.partial(rim_corners_kernel, s),
        shaped(2, 2 * HALO, LANES),
        in_specs=[VMEM, VMEM],
        out_specs=VMEM,
        name="corners",
    )(high, low)


def unmixed(x, turned):
    size = x.shape[1]
    half = size // 2
    i = lax.broadcasted_iota(jnp.int32, (size, size), 0)
    j = lax.broadcasted_iota(jnp.int32, (size, size), 1)
    picked = jnp.where(j < half, 2 * j, 2 * (j - half) + 1)
    choose = jnp.where(i == picked, 1.0, 0.0).astype(BF16)
    first = x.astype(BF16)
    rest = x - first.astype(F32)
    second = rest.astype(BF16)
    third = (rest - second.astype(F32)).astype(BF16)
    across = dot(first, choose) + dot(second, choose) + dot(third, choose)
    columns = []
    for k in range(size // LANES):
        turned[k] = across[:, k * LANES : (k + 1) * LANES]
        parts = [turned[k, pl.ds(odd, half, stride=2), :] for odd in (0, 1)]
        columns.append(jnp.concatenate(parts, 0))
    return jnp.concatenate(columns, 1)


def prepare_kernel(phase_ref, amp_ref, prop_ref, out_ref, turned):
    @pl.when(pl.program_id(0) == 0)
    def _():
        phase = unmixed(phase_ref[...], turned)
        prop_ref[0] = jnp.cos(phase)
        prop_ref[1] = jnp.sin(phase)

    out_ref[0] = unmixed(amp_ref[0], turned)


def prepare(phase, amplitudes):
    count, size, _ = amplitudes.shape
    one = pl.BlockSpec((1, size, size), lambda p: (p, 0, 0))
    return call(
        prepare_kernel,
        (shaped(2, size, size), shaped(count, size, size)),
        flops=1 << 29,
        room=PREPARE_ROOM,
        grid=(count,),
        in_specs=[VMEM, one],
        out_specs=(VMEM, one),
        scratch_shapes=[pltpu.VMEM((size // LANES, size, LANES), F32)],
        name="prepare",
    )(phase, amplitudes)


def assemble(ext, tile, rows, high, low, corner_high, corner_low):
    size = tile.shape[2]
    tiles = size // LANES
    spans = ((0, rows, 0, HALO), (HALO, None, 0, size), (HALO + size, rows, HALO, HALO))
    for top, strip, source, length in spans:
        here = pl.ds(top, length)
        there = pl.ds(source, length)
        for c in range(2):
            for j in range(tiles):
                across = slice(j * LANES, (j + 1) * LANES)
                ext[c, j + 1, here] = (
                    tile[0, c, :, across] if strip is None else strip[c, there, across]
                )
        h = high[...] if strip is None else corner_high[there, :]
        w = low[...] if strip is None else corner_low[there, :]
        ext[0, 0, here] = h
        ext[1, 0, here] = pltpu.roll(h, HALO, 1)
        ext[0, tiles + 1, here] = w
        ext[1, tiles + 1, here] = pltpu.roll(w, HALO, 1)


def place(off_ref, p):
    col = off_ref[p, 1] + HALO
    return off_ref[p, 0], col // LANES, col % LANES


def window(ext, off_ref, p, c, size):
    row, tile, turn = place(off_ref, p)
    keep = lax.broadcasted_iota(jnp.int32, (size, LANES), 1) < LANES - turn
    turned = [
        pltpu.roll(ext[c, tile + j, pl.ds(row, size), :], LANES - turn, 1)
        for j in range(size // LANES + 1)
    ]
    return jnp.concatenate(
        [jnp.where(keep, turned[j], turned[j + 1]) for j in range(size // LANES)], 1
    )


def add_window(acc, off_ref, p, c, value):
    size = value.shape[0]
    row, tile, turn = place(off_ref, p)
    keep = lax.broadcasted_iota(jnp.int32, (size, LANES), 1) >= turn
    count = size // LANES
    turned = [pltpu.roll(value[:, j * LANES : (j + 1) * LANES], turn, 1) for j in range(count)]
    zero = jnp.zeros((size, LANES), F32)
    before = [zero] + turned
    after = turned + [zero]
    for j in range(count + 1):
        at = (c, tile + j, pl.ds(row, size))
        acc[at] = acc[at] + jnp.where(keep, after[j], before[j])


def times(ar, ai, br, bi):
    return ar * br - ai * bi, ar * bi + ai * br


def conj_times(ar, ai, br, bi):
    return ar * br + ai * bi, ar * bi - ai * br


def first_kernel(off, tile, rows, high, low, ch, cl, probe, prop, t, psi_out, w_out, ext):
    p = pl.program_id(0)
    size = probe.shape[1]

    @pl.when(p == 0)
    def _():
        assemble(ext, tile, rows, high.at[0], low.at[0], ch, cl)

    wr, wi = window(ext, off, p, 0, size), window(ext, off, p, 1, size)
    w_out[0, 0] = wr
    w_out[0, 1] = wi
    fr, fi = forward(t, *times(probe[0], probe[1], wr, wi))
    xr, xi = inverse(t, *times(prop[0], prop[1], fr, fi))
    psi_out[0, 0] = xr
    psi_out[0, 1] = xi


def leave(acc, tile_out, strip_out, high_out, low_out):
    last = acc.shape[1] - 1
    size = tile_out.shape[1]
    for c in range(2):
        for j in range(1, last):
            across = slice((j - 1) * LANES, j * LANES)
            tile_out[c, :, across] = acc[c, j, HALO : HALO + size]
            strip_out[c, 0:HALO, across] = acc[c, j, 0:HALO]
            strip_out[c, HALO:, across] = acc[c, j, HALO + size :]
    high_out[...] = high_rim(acc[0, 0], acc[1, 0])
    low_out[...] = low_rim(acc[0, last], acc[1, last])


def second_kernel(
    off, tile, rows, high, low, corners, psi, amp, t, u_out, tile_out, strip_out, high_out, low_out, ext, acc
):
    p = pl.program_id(0)
    size = psi.shape[2]

    @pl.when(p == 0)
    def _():
        assemble(ext, tile, rows, high.at[1], low.at[1], corners.at[0], corners.at[1])
        acc[...] = jnp.zeros_like(acc)

    wr, wi = window(ext, off, p, 0, size), window(ext, off, p, 1, size)
    fr, fi = forward(t, *times(psi[0, 0], psi[0, 1], wr, wi))
    magnitude = jnp.sqrt(fr * fr + fi * fi)
    keep = 1.0 - amp[0] / jnp.maximum(magnitude, 0.5)
    br, bi = inverse(t, fr * keep, fi * keep)
    ur, ui = conj_times(window(ext, off, p, 0, size), window(ext, off, p, 1, size), br, bi)
    u_out[0, 0] = ur
    u_out[0, 1] = ui
    gr, gi = conj_times(psi[0, 0], psi[0, 1], br, bi)
    add_window(acc, off, p, 0, gr)
    add_window(acc, off, p, 1, gi)

    @pl.when(p == pl.num_programs(0) - 1)
    def _():
        leave(acc, tile_out, strip_out, high_out, low_out)


def third_kernel(up, u, w, prop, t, beta_out, mine_out, other_out, acc):
    p = pl.program_id(0)

    @pl.when(p == 0)
    def _():
        acc[...] = jnp.zeros_like(acc)

    fr, fi = forward(t, u[0, 0], u[0, 1])
    br, bi = inverse(t, *conj_times(prop[0], prop[1], fr, fi))
    beta_out[0, 0] = br
    beta_out[0, 1] = bi
    sr, si = conj_times(w[0, 0], w[0, 1], br, bi)
    acc[0] += sr
    acc[1] += si

    @pl.when(p == pl.num_programs(0) - 1)
    def _():
        mine_out[...] = acc[up[0]]
        other_out[...] = acc[1 - up[0]]


def spread_kernel(off, beta, probe, tile_out, strip_out, high_out, low_out, acc):
    p = pl.program_id(0)

    @pl.when(p == 0)
    def _():
        acc[...] = jnp.zeros_like(acc)

    gr, gi = conj_times(probe[0], probe[1], beta[0, 0], beta[0, 1])
    add_window(acc, off, p, 0, gr)
    add_window(acc, off, p, 1, gi)

    @pl.when(p == pl.num_programs(0) - 1)
    def _():
        leave(acc, tile_out, strip_out, high_out, low_out)


def rim_parts(from_right, from_left, c):
    h, w = from_right, from_left
    if c:
        h, w = pltpu.roll(h, HALO, 1), pltpu.roll(w, HALO, 1)
    lane = lax.broadcasted_iota(jnp.int32, h.shape, 1)
    return jnp.where(lane < HALO, 0.0, h), jnp.where(lane < HALO, w, 0.0)


def merge_kernel(x_ref, from_right, from_left, strip_ref):
    end = from_right.shape[0] - HALO
    for c in range(2):
        for i, start in enumerate((0, end)):
            here = pl.ds(i * HALO, HALO)
            h, w = rim_parts(from_right[pl.ds(start, HALO)], from_left[pl.ds(start, HALO)], c)
            strip_ref[c, here, :LANES] = x_ref[c, here, :LANES] + w
            strip_ref[c, here, LANES:-LANES] = x_ref[c, here, LANES:-LANES]
            strip_ref[c, here, -LANES:] = x_ref[c, here, -LANES:] + h


def finish_kernel(*refs):
    out_ref = refs[-1]
    size = out_ref.shape[2]
    for s in range(out_ref.shape[0]):
        inner, from_right, from_left, strip = refs[4 * s : 4 * s + 4]
        middle = pl.ds(HALO, size)
        for c in range(2):
            h, w = rim_parts(from_right[middle], from_left[middle], c)
            out_ref[s, c, :, :LANES] = inner[c, :, :LANES] + w
            out_ref[s, c, :, LANES:-LANES] = inner[c, :, LANES:-LANES]
            out_ref[s, c, :, -LANES:] = inner[c, :, -LANES:] + h
            out_ref[s, c, 0:HALO] += strip[c, HALO:]
            out_ref[s, c, size - HALO :] += strip[c, 0:HALO]


def shift(x, axis, by):
    count = lax.axis_size(axis)
    return lax.ppermute(x, axis, [(i, (i + by) % count) for i in range(count)])


def to_both(strips, axis, width, by):
    if lax.axis_size(axis) == 2:
        return shift(strips, axis, 1)
    return jnp.concatenate(
        [shift(strips[:, :width], axis, by), shift(strips[:, width:], axis, -by)], axis=1
    )


def halving_kernel(at, up, mine, came, mine_out, other_out):
    half = mine_out.shape[0]
    here = pl.ds(pl.multiple_of(up[at] * half, half), half)
    there = pl.ds(pl.multiple_of((1 - up[at]) * half, half), half)
    mine_out[...] = mine[here] + came[here]
    other_out[...] = mine[there] + came[there]


def adding_kernel(mine, came, out):
    out[...] = mine[...] + came[...]


def joining_kernel(at, factor, up, mine, came, out):
    half = mine.shape[0]
    out[pl.ds(pl.multiple_of(up[at] * half, half), half)] = mine[...] * factor
    out[pl.ds(pl.multiple_of((1 - up[at]) * half, half), half)] = came[...] * factor


def halvings():
    return [("col", bit) for bit in (1, 2, 4) if bit < lax.axis_size("col")]


def sides():
    return jnp.stack([lax.axis_index(axis) // bit % 2 for axis, bit in halvings()])


def total(up, mine, other, factor):
    sizes = {axis: lax.axis_size(axis) for axis in ("row", "col")}
    halves = halvings()
    rest = []
    for axis in ("row", "col"):
        bit = 1
        while bit < sizes[axis]:
            if (axis, bit) not in halves:
                rest.append((axis, bit))
            bit *= 2

    def swap(y, axis, bit):
        return lax.ppermute(y, axis, [(i, i ^ bit) for i in range(sizes[axis])])

    def add(x, came):
        return call(
            adding_kernel, shaped(*x.shape), in_specs=[VMEM] * 2, out_specs=VMEM, name="adding"
        )(x, came)

    for at, (axis, bit) in enumerate(halves):
        came = swap(other, axis, bit)
        if at + 1 == len(halves):
            x = add(mine, came)
            break
        out = shaped(mine.shape[0] // 2, mine.shape[1])
        mine, other = call(
            functools.partial(halving_kernel, at + 1),
            (out, out),
            in_specs=[SMEM, VMEM, VMEM],
            out_specs=(VMEM, VMEM),
            name="halving",
        )(up, mine, came)
    for axis, bit in rest:
        x = add(x, swap(x, axis, bit))
    for at, (axis, bit) in reversed(list(enumerate(halves))):
        x = call(
            functools.partial(joining_kernel, at, 1.0 if at else factor),
            shaped(2 * x.shape[0], x.shape[1]),
            in_specs=[SMEM, VMEM, VMEM],
            out_specs=VMEM,
            name="joining",
        )(up, x, swap(x, axis, bit))
    return x


def local(object_field, offsets, amplitudes, probe, phase):
    tile = object_field.shape[2]
    size = probe.shape[1]
    count = offsets.shape[0]
    off = offsets[:, 0]
    span = tile + 2 * HALO
    ext = pltpu.VMEM((2, tile // LANES + 2, span, LANES), F32)
    t = jnp.asarray(tables(size))
    flops = count * 2 * 4 * 3 * 2 * size**3

    up = sides()
    edges0, edges1, last, first = cut(object_field)
    rows0 = to_both(edges0, "row", HALO, 1)
    high = shift(last, "col", 1)
    low = shift(first, "col", -1)
    prop, amp = prepare(phase, amplitudes[:, 0])
    rows1 = to_both(edges1, "row", HALO, 1)
    corner_high, corner_low = row_corners(rows0)
    corner_high = shift(corner_high, "col", 1)
    corner_low = shift(corner_low, "col", -1)
    corners1 = rim_corners(high, low, 1)
    corners1 = to_both(corners1, "row", HALO, 1)

    def block(*shape):
        return pl.BlockSpec((1, *shape), lambda p: (p,) + (0,) * len(shape))

    def slice_of(s):
        return pl.BlockSpec((1, 2, tile, tile), lambda p: (s, 0, 0, 0), pipeline_mode=pl.Buffered(1))

    one = block(2, size, size)
    field = shaped(count, 2, size, size)
    psi, w0 = call(
        first_kernel,
        (field, field),
        flops=flops,
        room=ROOM,
        grid=(count,),
        in_specs=[SMEM, slice_of(0)] + [VMEM] * 8,
        out_specs=(one, one),
        scratch_shapes=[ext],
        name="first",
    )(off, object_field, rows0, high, low, corner_high, corner_low, probe, prop, t)
    left_over = (
        shaped(2, tile, tile),
        shaped(2, 2 * HALO, tile),
        shaped(span, LANES),
        shaped(span, LANES),
    )
    u, tile1, strip1, high1, low1 = call(
        second_kernel,
        (field, *left_over),
        flops=flops,
        room=ROOM,
        grid=(count,),
        in_specs=[SMEM, slice_of(1)] + [VMEM] * 4 + [one, block(size, size), VMEM],
        out_specs=(one, VMEM, VMEM, VMEM, VMEM),
        scratch_shapes=[ext, ext],
        name="second",
    )(off, object_field, rows1, high, low, corners1, psi, amp, t)
    right1 = shift(high1, "col", -1)
    left1 = shift(low1, "col", 1)
    beta, mine, other = call(
        third_kernel,
        (field, shaped(size, size), shaped(size, size)),
        flops=flops,
        room=ROOM,
        grid=(count,),
        in_specs=[SMEM, one, one, VMEM, VMEM],
        out_specs=(one, VMEM, VMEM),
        scratch_shapes=[pltpu.VMEM((2, size, size), F32)],
        name="third",
    )(up, u, w0, prop, t)
    tile0, strip0, high0, low0 = call(
        spread_kernel,
        left_over,
        room=ROOM,
        grid=(count,),
        in_specs=[SMEM, one, VMEM],
        out_specs=(VMEM,) * 4,
        scratch_shapes=[ext],
        name="spread",
    )(off, beta, probe)
    merge = call(
        merge_kernel,
        shaped(2, 2 * HALO, tile),
        in_specs=[VMEM] * 3,
        out_specs=VMEM,
        name="merge",
    )
    strip1 = merge(strip1, right1, left1)
    back1 = to_both(strip1, "row", HALO, -1)
    right0 = shift(high0, "col", -1)
    left0 = shift(low0, "col", 1)
    strip0 = merge(strip0, right0, left0)
    back0 = to_both(strip0, "row", HALO, -1)
    grad = call(
        finish_kernel,
        shaped(2, 2, tile, tile),
        room=16,
        in_specs=[VMEM] * 8,
        out_specs=VMEM,
        name="finish",
    )(tile0, right0, left0, back0, tile1, right1, left1, back1)
    everyone = count * lax.axis_size("row") * lax.axis_size("col")
    summed = total(up, mine, other, 1.0 / math.sqrt(everyone))
    return grad, summed.reshape(2, size, size)


def solution(mesh):
    in_specs = (
        P(None, None, "row", "col"),
        P("row", "col", None),
        P("row", "col", None, None),
        P(),
        P(),
    )
    out_specs = (P(None, None, "row", "col"), P())

    return jax.shard_map(local, mesh=mesh, in_specs=in_specs, out_specs=out_specs, check_vma=False)
```

time: 139 us -> 104 us (0.75)
  the two profiles are of different devices: /device:TPU:0 before, /device:TPU:10 now
where the time goes in v2:
time: 104 us
  Pallas kernels  43.2 us (42%)
  waiting for transfers between devices  34.5 us (33%)
  starting transfers between devices  22.6 us (22%)
  local copies, waits for them, and re-layouts  2.38 us (2%)
    ppermute x13, waiting for transfers between devices, shift(): return lax.ppermute(x, axis, [(i, (i + by) % count) for i in range(count)])  19.3 us
    ppermute x8, waiting for transfers between devices, swap(): return lax.ppermute(y, axis, [(i, i ^ bit) for i in range(sizes[axis])])  15.2 us
    ppermute x8, starting transfers between devices, swap(): return lax.ppermute(y, axis, [(i, i ^ bit) for i in range(sizes[axis])])  12.1 us
    ppermute x13, starting transfers between devices, shift(): return lax.ppermute(x, axis, [(i, (i + by) % count) for i in range(count)])  10.5 us
    pallas_call x1, Pallas kernels, local(): call(second_kernel, (field, *left_over), flops=flops, room=ROOM, grid=(co...  9.93 us
    pallas_call x1, Pallas kernels, local(): call(first_kernel, (field, field), flops=flops, room=ROOM, grid=(count,),...  8.34 us
    pallas_call x1, Pallas kernels, local(): call(third_kernel, (field, shaped(size, size), shaped(size, size)), flops...  6.95 us
    pallas_call x1, Pallas kernels, prepare(): call(prepare_kernel, (shaped(2, size, size), shaped(count, size, size)),...  5.15 us
  transfers between devices with their start and end apart: 21, of which 9 were waited for; matrix products, arithmetic and copies ran while one was open for 0% of the time, Pallas kernels for 21%

profile of v2, /device:TPU:10, one launch (start us, length us, event | category | flops | bytes accessed | tf_op | source)
XLA Modules:
  0.0 103.6 jit_solution(15105186509423139011)
XLA Ops:
  0.6 2.9 %cut.1 = (f32[2,128,384]{2,1,0:T(8,128)}, f32[2,128,384]{2,1,0:T(8,128)}, f32[2,384,128]{2,1,0:T(8,128)}, f32[2,384,128]{2,1,0:T(8,128)}) custom-call(f32[2,2,384,384]{3,2,1,0:T(8,128)} %tile.3), custom_call_target="tpu_custom_call" | custom-call | bytes 4194304 | tf_op jit(solution)/shard_map/cut/pallas_call | solution.py:150
  3.6 1.6 %collective-permute-start.4 = (f32[2,128,384]{2,1,0:T(8,128)}, f32[2,128,384]{2,1,0:T(8,128)}, u32[]{:S(2)}, u32[]{:S(2)}) collective-permute-start(f32[2,128,384]{2,1,0:T(8,128)} %get-tuple-element.31), channel_id=1, source_target_pairs={{0,16},{16,0},{1,17},{17,1},{2,18},{18,2},{3,19},{19,3},{4,20},{20... | collective-permute-start | bytes 1179656 | tf_op jit(solution)/shard_map/ppermute | solution.py:430
  5.2 1.7 %collective-permute-start.2 = (f32[2,384,128]{2,1,0:T(8,128)}, f32[2,384,128]{2,1,0:T(8,128)}, u32[]{:S(2)}, u32[]{:S(2)}) collective-permute-start(f32[2,384,128]{2,1,0:T(8,128)} %get-tuple-element.30), channel_id=1, source_target_pairs={{0,15},{1,0},{2,1},{3,2},{4,3},{5,4},{6,5},{7,6},{8,7},{9,8},{10,9... | collective-permute-start | bytes 1179656 | tf_op jit(solution)/shard_map/ppermute | solution.py:430
  7.4 8.5 %collective-permute-done.4.rows_ref.rows = f32[2,128,384]{2,1,0:T(8,128)} collective-permute-done((f32[2,128,384]{2,1,0:T(8,128)}, f32[2,128,384]{2,1,0:T(8,128)}, u32[]{:S(2)}, u32[]{:S(2)}) %collective-permute-start.4) | collective-permute-done | bytes 393248 | tf_op jit(solution)/shard_map/ppermute | solution.py:430
  17.1 1.7 %collective-permute-start.6 = (f32[128,128]{1,0:T(8,128)S(1)}, f32[128,128]{1,0:T(8,128)S(1)}, u32[]{:S(2)}, u32[]{:S(2)}) collective-permute-start(f32[128,128]{1,0:T(8,128)S(1)} %get-tuple-element.33), channel_id=1, source_target_pairs={{0,15},{1,0},{2,1},{3,2},{4,3},{5,4},{6,5},{7,6},{8,7},{9,8},{10,9... | collective-permute-start | bytes 196616 | tf_op jit(solution)/shard_map/ppermute | solution.py:430
  19.0 5.1 %prepare.1 = (f32[2,256,256]{2,1,0:T(8,128)}, f32[4,256,256]{2,1,0:T(8,128)}) custom-call(f32[256,256]{1,0:T(8,128)} %phase_ref.1, f32[4,256,256]{2,1,0:T(8,128)} %bitcast.8), custom_call_target="tpu_custom_call" | custom-call | flops 536870912 | bytes 4194304 | tf_op jit(solution)/shard_map/prepare/pallas_call | solution.py:226
  25.2 1.6 %collective-permute-start.3 = (f32[2,128,128]{2,1,0:T(8,128)S(1)}, f32[2,128,128]{2,1,0:T(8,128)S(1)}, u32[]{:S(2)}, u32[]{:S(2)}) collective-permute-start(f32[2,128,128]{2,1,0:T(8,128)S(1)} %corners.2), channel_id=1, source_target_pairs={{0,16},{16,0},{1,17},{17,1},{2,18},{18,2},{3,19},{19,3},{4,20},{20... | collective-permute-start | bytes 393224 | tf_op jit(solution)/shard_map/ppermute | solution.py:430
  29.1 8.3 %first.1 = (f32[4,2,256,256]{3,2,1,0:T(8,128)S(1)}, f32[4,2,256,256]{3,2,1,0:T(8,128)S(1)}) custom-call(s32[4,2]{1,0:T(4,128)S(1)} %copy.10.off, f32[2,2,384,384]{3,2,1,0:T(8,128)S(1)} %copy-done, f32[2,128,384]{2,1,0:T(8,128)} %collective-permute-done.4.rows_ref.rows, f32[2,384,128]{2,1,0:T(8,128)S(1)} %collective-permute-done.1.high_ref.high, ...), custom_call_target="tpu_custom_call" | custom-call | flops 3221225472 | bytes 4194304 | tf_op jit(solution)/shard_map/first/pallas_call | solution.py:543
  37.5 9.9 %second.1 = (f32[4,2,256,256]{3,2,1,0:T(8,128)S(1)}, f32[2,384,384]{2,1,0:T(8,128)S(1)}, f32[2,128,384]{2,1,0:T(8,128)S(1)}, f32[512,128]{1,0:T(8,128)S(1)}, f32[512,128]{1,0:T(8,128)S(1)}) custom-call(s32[4,2]{1,0:T(4,128)S(1)} %copy.10.off, f32[2,2,384,384]{3,2,1,0:T(8,128)S(1)} %copy-done, f32[2,128,384]{2,1,0:T(8,128)} %collective-permute-done.rows, ...), custom_call_target="tpu_custom_call" | custom-call | flops 3221225472 | bytes 4194304 | tf_op jit(solution)/shard_map/second/pallas_call | solution.py:560
  47.4 7.0 %third.1 = (f32[4,2,256,256]{3,2,1,0:T(8,128)S(1)}, f32[256,256]{1,0:T(8,128)S(1)}, f32[256,256]{1,0:T(8,128)S(1)}) custom-call(s32[3]{0:T(128)S(1)} %pad_add_fusion.up, f32[4,2,256,256]{3,2,1,0:T(8,128)S(1)} %get-tuple-element.37.u, f32[4,2,256,256]{3,2,1,0:T(8,128)S(1)} %get-tuple-element.38.w, f32[2,256,256]{2,1,0:T(8,128)S(1)} %copy-done.6, ...), custom_call_target="tpu_custom_call" | custom-call | flops 3221225472 | bytes 4194304 | tf_op jit(solution)/shard_map/third/pallas_call | solution.py:573
  54.5 1.5 %collective-permute-done.13.came = f32[256,256]{1,0:T(8,128)S(1)} collective-permute-done((f32[256,256]{1,0:T(8,128)S(1)}, f32[256,256]{1,0:T(8,128)S(1)}, u32[]{:S(2)}, u32[]{:S(2)}) %collective-permute-start.13) | collective-permute-done | bytes 262176 | tf_op jit(solution)/shard_map/ppermute | solution.py:479
  58.1 2.1 %spread.1 = (f32[2,384,384]{2,1,0:T(8,128)S(1)}, f32[2,128,384]{2,1,0:T(8,128)S(1)}, f32[512,128]{1,0:T(8,128)S(1)}, f32[512,128]{1,0:T(8,128)S(1)}) custom-call(s32[4,2]{1,0:T(4,128)S(1)} %copy.10.off, f32[4,2,256,256]{3,2,1,0:T(8,128)S(1)} %get-tuple-element.39.beta, f32[2,256,256]{2,1,0:T(8,128)S(1)} %copy-done.1), custom_call_target="tpu_custom_call" | custom-call | bytes 4194304 | tf_op jit(solution)/shard_map/spread/pallas_call | solution.py:584
  62.8 2.0 %collective-permute-start.15 = (f32[64,256]{1,0:T(8,128)S(1)}, f32[64,256]{1,0:T(8,128)S(1)}, u32[]{:S(2)}, u32[]{:S(2)}) collective-permute-start(f32[64,256]{1,0:T(8,128)S(1)} %get-tuple-element.53), channel_id=1, source_target_pairs={{0,4},{1,5},{2,6},{3,7},{4,0},{5,1},{6,2},{7,3},{8,12},{9,13},{10,... | collective-permute-start | bytes 196616 | tf_op jit(solution)/shard_map/ppermute | solution.py:479
  65.3 2.5 %collective-permute-done.15.came = f32[64,256]{1,0:T(8,128)S(1)} collective-permute-done((f32[64,256]{1,0:T(8,128)S(1)}, f32[64,256]{1,0:T(8,128)S(1)}, u32[]{:S(2)}, u32[]{:S(2)}) %collective-permute-start.15) | collective-permute-done | bytes 65568 | tf_op jit(solution)/shard_map/ppermute | solution.py:479
  68.3 3.8 %collective-permute-done.16.came = f32[64,256]{1,0:T(8,128)S(1)} collective-permute-done((f32[64,256]{1,0:T(8,128)S(1)}, f32[64,256]{1,0:T(8,128)S(1)}, u32[]{:S(2)}, u32[]{:S(2)}) %collective-permute-start.16) | collective-permute-done | bytes 65568 | tf_op jit(solution)/shard_map/ppermute | solution.py:479
  72.1 2.5 %collective-permute-start.17 = (f32[64,256]{1,0:T(8,128)S(1)}, f32[64,256]{1,0:T(8,128)S(1)}, u32[]{:S(2)}, u32[]{:S(2)}) collective-permute-start(f32[64,256]{1,0:T(8,128)S(1)} %adding.4.mine), channel_id=1, source_target_pairs={{0,8},{1,9},{2,10},{3,11},{4,12},{5,13},{6,14},{7,15},{8,0},{9,1},... | collective-permute-start | bytes 196616 | tf_op jit(solution)/shard_map/ppermute | solution.py:479
  74.6 3.0 %collective-permute-done.17.came = f32[64,256]{1,0:T(8,128)S(1)} collective-permute-done((f32[64,256]{1,0:T(8,128)S(1)}, f32[64,256]{1,0:T(8,128)S(1)}, u32[]{:S(2)}, u32[]{:S(2)}) %collective-permute-start.17) | collective-permute-done | bytes 65568 | tf_op jit(solution)/shard_map/ppermute | solution.py:479
  77.6 3.4 %collective-permute-start.18 = (f32[64,256]{1,0:T(8,128)S(1)}, f32[64,256]{1,0:T(8,128)S(1)}, u32[]{:S(2)}, u32[]{:S(2)}) collective-permute-start(f32[64,256]{1,0:T(8,128)S(1)} %adding.5.mine), channel_id=1, source_target_pairs={{0,4},{1,5},{2,6},{3,7},{4,0},{5,1},{6,2},{7,3},{8,12},{9,13},{10,... | collective-permute-start | bytes 196616 | tf_op jit(solution)/shard_map/ppermute | solution.py:479
  81.8 1.6 %collective-permute-start.9 = (f32[2,128,384]{2,1,0:T(8,128)S(1)}, f32[2,128,384]{2,1,0:T(8,128)S(1)}, u32[]{:S(2)}, u32[]{:S(2)}) collective-permute-start(f32[2,128,384]{2,1,0:T(8,128)S(1)} %merge.2), channel_id=1, source_target_pairs={{0,16},{16,0},{1,17},{17,1},{2,18},{18,2},{3,19},{19,3},{4,20},{20... | collective-permute-start | bytes 1179656 | tf_op jit(solution)/shard_map/ppermute | solution.py:430
  84.0 2.1 %collective-permute-start.19 = (f32[128,256]{1,0:T(8,128)S(1)}, f32[128,256]{1,0:T(8,128)S(1)}, u32[]{:S(2)}, u32[]{:S(2)}) collective-permute-start(f32[128,256]{1,0:T(8,128)S(1)} %joining.3.mine), channel_id=1, source_target_pairs={{0,2},{1,3},{2,0},{3,1},{4,6},{5,7},{6,4},{7,5},{8,10},{9,11},{10,... | collective-permute-start | bytes 393224 | tf_op jit(solution)/shard_map/ppermute | solution.py:479
  86.0 3.0 %collective-permute-done.19.came = f32[128,256]{1,0:T(8,128)S(1)} collective-permute-done((f32[128,256]{1,0:T(8,128)S(1)}, f32[128,256]{1,0:T(8,128)S(1)}, u32[]{:S(2)}, u32[]{:S(2)}) %collective-permute-start.19) | collective-permute-done | bytes 131104 | tf_op jit(solution)/shard_map/ppermute | solution.py:479
  89.7 3.5 %collective-permute-done.12.refs_7_ = f32[2,128,384]{2,1,0:T(8,128)S(1)} collective-permute-done((f32[2,128,384]{2,1,0:T(8,128)S(1)}, f32[2,128,384]{2,1,0:T(8,128)S(1)}, u32[]{:S(2)}, u32[]{:S(2)}) %collective-permute-start.12) | collective-permute-done | bytes 393248 | tf_op jit(solution)/shard_map/ppermute | solution.py:430
  93.2 7.2 %collective-permute-done.9.refs_3_ = f32[2,128,384]{2,1,0:T(8,128)S(1)} collective-permute-done((f32[2,128,384]{2,1,0:T(8,128)S(1)}, f32[2,128,384]{2,1,0:T(8,128)S(1)}, u32[]{:S(2)}, u32[]{:S(2)}) %collective-permute-start.9) | collective-permute-done | bytes 393248 | tf_op jit(solution)/shard_map/ppermute | solution.py:430
  100.4 1.8 %finish.1 = f32[2,2,384,384]{3,2,1,0:T(8,128)} custom-call(f32[2,384,384]{2,1,0:T(8,128)S(1)} %get-tuple-element.40.refs_0_, f32[512,128]{1,0:T(8,128)S(1)} %collective-permute-done.7.from_right.refs_1_, f32[512,128]{1,0:T(8,128)S(1)} %collective-permute-done.8.from_left.refs_2_, f32[2,128,384]{2,1,0:T(8,128)S(1)} %collective-permute-done.9.refs_3_, ...), custom_call_target="tpu_custom_call" | custom-call | bytes 4194304 | tf_op jit(solution)/shard_map/finish/pallas_call | solution.py:607
  (55 shorter events, 14.3 us)
Async XLA Ops:
  0.6 18.3 %copy-start.7 = (s32[4,1,2]{0,2,1:T(2,128)S(1)}, s32[4,1,2]{0,2,1:T(2,128)}, u32[]{:S(2)}) copy-start(s32[4,1,2]{0,2,1:T(2,128)} %param.7) | copy-start | bytes 100
  3.6 23.2 %copy-start = (f32[2,2,384,384]{3,2,1,0:T(8,128)S(1)}, f32[2,2,384,384]{3,2,1,0:T(8,128)}, u32[]{:S(2)}) copy-start(f32[2,2,384,384]{3,2,1,0:T(8,128)} %tile.3) | copy-start | bytes 7077892
  3.6 23.2 %copy-start.1 = (f32[2,256,256]{2,1,0:T(8,128)S(1)}, f32[2,256,256]{2,1,0:T(8,128)}, u32[]{:S(2)}) copy-start(f32[2,256,256]{2,1,0:T(8,128)} %probe.3) | copy-start | bytes 1572868
  3.6 12.4 %collective-permute-start.4 = (f32[2,128,384]{2,1,0:T(8,128)}, f32[2,128,384]{2,1,0:T(8,128)}, u32[]{:S(2)}, u32[]{:S(2)}) collective-permute-start(f32[2,128,384]{2,1,0:T(8,128)} %get-tuple-element.31), channel_id=1, source_target_pairs={{0,16},{16,0},{1,17},{17,1},{2,18},{18,2},{3,19},{19,3},{4,20},{20... | collective-permute-start | bytes 1179656 | tf_op jit(solution)/shard_map/ppermute | solution.py:430
  5.2 19.0 %collective-permute-start.1 = (f32[2,384,128]{2,1,0:T(8,128)}, f32[2,384,128]{2,1,0:T(8,128)S(1)}, u32[]{:S(2)}, u32[]{:S(2)}) collective-permute-start(f32[2,384,128]{2,1,0:T(8,128)} %get-tuple-element.29), channel_id=1, source_target_pairs={{0,1},{1,2},{2,3},{3,4},{4,5},{5,6},{6,7},{7,8},{8,9},{9,10},{10,1... | collective-permute-start | bytes 1179656 | tf_op jit(solution)/shard_map/ppermute | solution.py:430
  5.2 19.0 %collective-permute-start.2 = (f32[2,384,128]{2,1,0:T(8,128)}, f32[2,384,128]{2,1,0:T(8,128)}, u32[]{:S(2)}, u32[]{:S(2)}) collective-permute-start(f32[2,384,128]{2,1,0:T(8,128)} %get-tuple-element.30), channel_id=1, source_target_pairs={{0,15},{1,0},{2,1},{3,2},{4,3},{5,4},{6,5},{7,6},{8,7},{9,8},{10,9... | collective-permute-start | bytes 1179656 | tf_op jit(solution)/shard_map/ppermute | solution.py:430
  6.9 30.5 %collective-permute-start = (f32[2,128,384]{2,1,0:T(8,128)}, f32[2,128,384]{2,1,0:T(8,128)}, u32[]{:S(2)}, u32[]{:S(2)}) collective-permute-start(f32[2,128,384]{2,1,0:T(8,128)} %get-tuple-element.28), channel_id=1, source_target_pairs={{0,16},{16,0},{1,17},{17,1},{2,18},{18,2},{3,19},{19,3},{4,20},{20... | collective-permute-start | bytes 1179656 | tf_op jit(solution)/shard_map/ppermute | solution.py:430
  17.1 9.7 %collective-permute-start.5 = (f32[128,128]{1,0:T(8,128)S(1)}, f32[128,128]{1,0:T(8,128)S(1)}, u32[]{:S(2)}, u32[]{:S(2)}) collective-permute-start(f32[128,128]{1,0:T(8,128)S(1)} %get-tuple-element.32), channel_id=1, source_target_pairs={{0,1},{1,2},{2,3},{3,4},{4,5},{5,6},{6,7},{7,8},{8,9},{9,10},{10,1... | collective-permute-start | bytes 196616 | tf_op jit(solution)/shard_map/ppermute | solution.py:430
  17.1 9.7 %collective-permute-start.6 = (f32[128,128]{1,0:T(8,128)S(1)}, f32[128,128]{1,0:T(8,128)S(1)}, u32[]{:S(2)}, u32[]{:S(2)}) collective-permute-start(f32[128,128]{1,0:T(8,128)S(1)} %get-tuple-element.33), channel_id=1, source_target_pairs={{0,15},{1,0},{2,1},{3,2},{4,3},{5,4},{6,5},{7,6},{8,7},{9,8},{10,9... | collective-permute-start | bytes 196616 | tf_op jit(solution)/shard_map/ppermute | solution.py:430
  25.2 12.2 %collective-permute-start.3 = (f32[2,128,128]{2,1,0:T(8,128)S(1)}, f32[2,128,128]{2,1,0:T(8,128)S(1)}, u32[]{:S(2)}, u32[]{:S(2)}) collective-permute-start(f32[2,128,128]{2,1,0:T(8,128)S(1)} %corners.2), channel_id=1, source_target_pairs={{0,16},{16,0},{1,17},{17,1},{2,18},{18,2},{3,19},{19,3},{4,20},{20... | collective-permute-start | bytes 393224 | tf_op jit(solution)/shard_map/ppermute | solution.py:430
  54.4 1.6 %collective-permute-start.13 = (f32[256,256]{1,0:T(8,128)S(1)}, f32[256,256]{1,0:T(8,128)S(1)}, u32[]{:S(2)}, u32[]{:S(2)}) collective-permute-start(f32[256,256]{1,0:T(8,128)S(1)} %get-tuple-element.49), channel_id=1, source_target_pairs={{0,1},{1,0},{2,3},{3,2},{4,5},{5,4},{6,7},{7,6},{8,9},{9,8},{10,11... | collective-permute-start | bytes 786440 | tf_op jit(solution)/shard_map/ppermute | solution.py:479
  56.6 5.6 %collective-permute-start.14 = (f32[128,256]{1,0:T(8,128)S(1)}, f32[128,256]{1,0:T(8,128)S(1)}, u32[]{:S(2)}, u32[]{:S(2)}) collective-permute-start(f32[128,256]{1,0:T(8,128)S(1)} %get-tuple-element.51), channel_id=1, source_target_pairs={{0,2},{1,3},{2,0},{3,1},{4,6},{5,7},{6,4},{7,5},{8,10},{9,11},{10,... | collective-permute-start | bytes 393224 | tf_op jit(solution)/shard_map/ppermute | solution.py:479
  60.2 20.9 %collective-permute-start.10 = (f32[512,128]{1,0:T(8,128)S(1)}, f32[512,128]{1,0:T(8,128)S(1)}, u32[]{:S(2)}, u32[]{:S(2)}) collective-permute-start(f32[512,128]{1,0:T(8,128)S(1)} %get-tuple-element.45), channel_id=1, source_target_pairs={{0,15},{1,0},{2,1},{3,2},{4,3},{5,4},{6,5},{7,6},{8,7},{9,8},{10,9... | collective-permute-start | bytes 786440 | tf_op jit(solution)/shard_map/ppermute | solution.py:430
  60.3 20.8 %collective-permute-start.11 = (f32[512,128]{1,0:T(8,128)S(1)}, f32[512,128]{1,0:T(8,128)S(1)}, u32[]{:S(2)}, u32[]{:S(2)}) collective-permute-start(f32[512,128]{1,0:T(8,128)S(1)} %get-tuple-element.46), channel_id=1, source_target_pairs={{0,1},{1,2},{2,3},{3,4},{4,5},{5,6},{6,7},{7,8},{8,9},{9,10},{10,1... | collective-permute-start | bytes 786440 | tf_op jit(solution)/shard_map/ppermute | solution.py:430
  62.8 5.0 %collective-permute-start.15 = (f32[64,256]{1,0:T(8,128)S(1)}, f32[64,256]{1,0:T(8,128)S(1)}, u32[]{:S(2)}, u32[]{:S(2)}) collective-permute-start(f32[64,256]{1,0:T(8,128)S(1)} %get-tuple-element.53), channel_id=1, source_target_pairs={{0,4},{1,5},{2,6},{3,7},{4,0},{5,1},{6,2},{7,3},{8,12},{9,13},{10,... | collective-permute-start | bytes 196616 | tf_op jit(solution)/shard_map/ppermute | solution.py:479
  64.7 16.9 %collective-permute-start.7 = (f32[512,128]{1,0:T(8,128)S(1)}, f32[512,128]{1,0:T(8,128)S(1)}, u32[]{:S(2)}, u32[]{:S(2)}) collective-permute-start(f32[512,128]{1,0:T(8,128)S(1)} %get-tuple-element.41), channel_id=1, source_target_pairs={{0,15},{1,0},{2,1},{3,2},{4,3},{5,4},{6,5},{7,6},{8,7},{9,8},{10,9... | collective-permute-start | bytes 786440 | tf_op jit(solution)/shard_map/ppermute | solution.py:430
  65.1 16.6 %collective-permute-start.8 = (f32[512,128]{1,0:T(8,128)S(1)}, f32[512,128]{1,0:T(8,128)S(1)}, u32[]{:S(2)}, u32[]{:S(2)}) collective-permute-start(f32[512,128]{1,0:T(8,128)S(1)} %get-tuple-element.42), channel_id=1, source_target_pairs={{0,1},{1,2},{2,3},{3,4},{4,5},{5,6},{6,7},{7,8},{8,9},{9,10},{10,1... | collective-permute-start | bytes 786440 | tf_op jit(solution)/shard_map/ppermute | solution.py:430
  67.8 4.3 %collective-permute-start.16 = (f32[64,256]{1,0:T(8,128)S(1)}, f32[64,256]{1,0:T(8,128)S(1)}, u32[]{:S(2)}, u32[]{:S(2)}) collective-permute-start(f32[64,256]{1,0:T(8,128)S(1)} %adding.3.mine), channel_id=1, source_target_pairs={{0,16},{16,0},{1,17},{17,1},{2,18},{18,2},{3,19},{19,3},{4,20},{20... | collective-permute-start | bytes 196616 | tf_op jit(solution)/shard_map/ppermute | solution.py:479
  72.1 5.5 %collective-permute-start.17 = (f32[64,256]{1,0:T(8,128)S(1)}, f32[64,256]{1,0:T(8,128)S(1)}, u32[]{:S(2)}, u32[]{:S(2)}) collective-permute-start(f32[64,256]{1,0:T(8,128)S(1)} %adding.4.mine), channel_id=1, source_target_pairs={{0,8},{1,9},{2,10},{3,11},{4,12},{5,13},{6,14},{7,15},{8,0},{9,1},... | collective-permute-start | bytes 196616 | tf_op jit(solution)/shard_map/ppermute | solution.py:479
  77.6 5.8 %collective-permute-start.18 = (f32[64,256]{1,0:T(8,128)S(1)}, f32[64,256]{1,0:T(8,128)S(1)}, u32[]{:S(2)}, u32[]{:S(2)}) collective-permute-start(f32[64,256]{1,0:T(8,128)S(1)} %adding.5.mine), channel_id=1, source_target_pairs={{0,4},{1,5},{2,6},{3,7},{4,0},{5,1},{6,2},{7,3},{8,12},{9,13},{10,... | collective-permute-start | bytes 196616 | tf_op jit(solution)/shard_map/ppermute | solution.py:479
  81.1 12.1 %collective-permute-start.12 = (f32[2,128,384]{2,1,0:T(8,128)S(1)}, f32[2,128,384]{2,1,0:T(8,128)S(1)}, u32[]{:S(2)}, u32[]{:S(2)}) collective-permute-start(f32[2,128,384]{2,1,0:T(8,128)S(1)} %merge.3), channel_id=1, source_target_pairs={{0,16},{16,0},{1,17},{17,1},{2,18},{18,2},{3,19},{19,3},{4,20},{20... | collective-permute-start | bytes 1179656 | tf_op jit(solution)/shard_map/ppermute | solution.py:430
  81.8 18.6 %collective-permute-start.9 = (f32[2,128,384]{2,1,0:T(8,128)S(1)}, f32[2,128,384]{2,1,0:T(8,128)S(1)}, u32[]{:S(2)}, u32[]{:S(2)}) collective-permute-start(f32[2,128,384]{2,1,0:T(8,128)S(1)} %merge.2), channel_id=1, source_target_pairs={{0,16},{16,0},{1,17},{17,1},{2,18},{18,2},{3,19},{19,3},{4,20},{20... | collective-permute-start | bytes 1179656 | tf_op jit(solution)/shard_map/ppermute | solution.py:430
  84.0 5.0 %collective-permute-start.19 = (f32[128,256]{1,0:T(8,128)S(1)}, f32[128,256]{1,0:T(8,128)S(1)}, u32[]{:S(2)}, u32[]{:S(2)}) collective-permute-start(f32[128,256]{1,0:T(8,128)S(1)} %joining.3.mine), channel_id=1, source_target_pairs={{0,2},{1,3},{2,0},{3,1},{4,6},{5,7},{6,4},{7,5},{8,10},{9,11},{10,... | collective-permute-start | bytes 393224 | tf_op jit(solution)/shard_map/ppermute | solution.py:479
  89.6 12.6 %collective-permute-start.20 = (f32[256,256]{1,0:T(8,128)S(1)}, f32[256,256]{1,0:T(8,128)S(1)}, u32[]{:S(2)}, u32[]{:S(2)}) collective-permute-start(f32[256,256]{1,0:T(8,128)S(1)} %joining.4.mine), channel_id=1, source_target_pairs={{0,1},{1,0},{2,3},{3,2},{4,5},{5,4},{6,7},{7,6},{8,9},{9,8},{10,11... | collective-permute-start | bytes 786440 | tf_op jit(solution)/shard_map/ppermute | solution.py:479
  (5 other events, 29.0 us)

commit v3 on v2

v3 whole, which is shorter than its diff:
```python
import functools
import math

import jax
import jax.numpy as jnp
from jax import lax
from jax.experimental import pallas as pl
from jax.experimental.pallas import tpu as pltpu
from jax.sharding import PartitionSpec as P

HALO = 64
ROOM = 20
CUT_ROOM = 61
LANES = 128
F32 = jnp.float32
BF16 = jnp.bfloat16
VMEM = pl.BlockSpec(memory_space=pltpu.VMEM)
SMEM = pl.BlockSpec(memory_space=pltpu.SMEM)


def split(x):
    high = x.astype(BF16)
    return high, (x - high.astype(F32)).astype(BF16)


def dot(a, b):
    return jnp.dot(a, b, preferred_element_type=F32)


class Stage:
    def __init__(self, t, high, low, product):
        self.t, self.high, self.low, self.product = t, high, low, product
        self.group = range(high.shape[0])
        self.half = high.shape[2] // 2

    def put(self, q, e, x):
        self.high[q, e], self.low[q, e] = split(x)

    def right(self, q, e, which):
        th, tl = self.t[2 * which], self.t[2 * which + 1]
        high, low = self.high[q, e], self.low[q, e]
        return dot(high, th) + dot(low, th) + dot(high, tl)

    def left(self, q, e, which):
        th, tl = self.t[2 * which], self.t[2 * which + 1]
        high, low = self.high[q, e], self.low[q, e]
        return dot(th, high) + dot(th, low) + dot(tl, high)

    def forward(self, source):
        h = self.half
        for q in self.group:
            x = source(q)
            self.put(q, 0, jnp.concatenate([y[:, :h] + y[:, h:] for y in x], 1))
            self.put(q, 1, jnp.concatenate([y[:, :h] - y[:, h:] for y in x], 1))
        for q in self.group:
            self.product[q, 0] = self.right(q, 0, 0)
            self.product[q, 1] = self.right(q, 1, 2)
        for q in self.group:
            top = self.product[q, :, :h, :]
            bottom = self.product[q, :, h:, :]
            for e, y in enumerate((top + bottom, top - bottom)):
                parts = [
                    jnp.concatenate([y[k, :, c * h : (c + 1) * h] for k in (0, 1)], 1) for c in (0, 1)
                ]
                self.put(q, e, jnp.concatenate(parts, 0))
        for q in self.group:
            self.product[q, 0] = self.left(q, 0, 1)
            self.product[q, 1] = self.left(q, 1, 3)

    def inverse(self, change, sink):
        h = self.half
        for q in self.group:
            for e in (0, 1):
                z = change(q, e, self.product[q, e, :h], self.product[q, e, h:])
                self.put(q, e, jnp.concatenate(z, 0))
        for q in self.group:
            self.product[q, 0] = self.left(q, 0, 0)
            self.product[q, 1] = self.left(q, 1, 2)
        for q in self.group:
            even, odd = self.product[q, 0], self.product[q, 1]
            p, m = even + odd, even - odd
            parts = [jnp.concatenate([p[c * h : (c + 1) * h], m[c * h : (c + 1) * h]], 0) for c in (0, 1)]
            self.put(q, 0, jnp.concatenate([y[:, :h] for y in parts], 1))
            self.put(q, 1, jnp.concatenate([y[:, h:] for y in parts], 1))
        for q in self.group:
            even, odd = self.right(q, 0, 1), self.right(q, 1, 3)
            p, m = even + odd, even - odd
            sink(q, *[jnp.concatenate([y[:, c * h : (c + 1) * h] for y in (p, m)], 1) for c in (0, 1)])


def group_of(count):
    return 2 if count % 2 == 0 else 1


def stage_scratch(count, size):
    shape = (group_of(count), 2, size, size)
    return [pltpu.VMEM(shape, BF16), pltpu.VMEM(shape, BF16), pltpu.VMEM(shape, F32)]


def call(kernel, out_shape, flops=0, room=8, **kwargs):
    return pl.pallas_call(
        kernel,
        out_shape=out_shape,
        cost_estimate=pl.CostEstimate(flops=flops, bytes_accessed=4 << 20, transcendentals=0),
        compiler_params=pltpu.CompilerParams(vmem_limit_bytes=room << 20),
        **kwargs,
    )


def shaped(*shape):
    return jax.ShapeDtypeStruct(shape, F32)


def side_by_side(re, im):
    lane = lax.broadcasted_iota(jnp.int32, re.shape, 1)
    turned = pltpu.roll(im, HALO, 1)
    return lane < HALO, turned


def high_rim(re, im):
    low, turned = side_by_side(re, im)
    return jnp.where(low, turned, re)


def low_rim(re, im):
    low, turned = side_by_side(re, im)
    return jnp.where(low, re, turned)


def upper(at):
    axis, bit = halvings()[at]
    return lax.axis_index(axis) // bit % 2


def on_odd():
    return lax.axis_index("col") % 2 == 1


def swapped(odd, a, b):
    return jnp.where(odd, b, a), jnp.where(odd, a, b)


def row_copies(x_ref, s, out, sem):
    size = x_ref.shape[2]
    return [
        pltpu.make_async_copy(
            x_ref.at[s, :, pl.ds(start, HALO), :], out.at[:, pl.ds(i * HALO, HALO), :], sem.at[i]
        )
        for i, start in enumerate((size - HALO, 0))
    ]


def cut_rows_kernel(s, x_ref, out, sem):
    copies = row_copies(x_ref, s, out, sem)
    for copy in copies:
        copy.start()
    for copy in copies:
        copy.wait()


def cut_rows(x, s):
    size = x.shape[2]
    return call(
        functools.partial(cut_rows_kernel, s),
        shaped(2, 2 * HALO, size),
        room=CUT_ROOM + 1,
        in_specs=[pl.BlockSpec(memory_space=pltpu.HBM)],
        out_specs=VMEM,
        scratch_shapes=[pltpu.SemaphoreType.DMA((2,))],
        name="cut",
    )(x)


def cut_kernel(off, x_ref, edge, near, far, columns, sem, col_sem):
    odd = on_odd()
    slices, _, size, _ = x_ref.shape
    rows = row_copies(x_ref, slices - 1, edge, sem)
    cols = [
        pltpu.make_async_copy(
            x_ref.at[s, :, :, pl.ds(start, LANES)], columns.at[s, i], col_sem.at[s, i]
        )
        for s in range(slices)
        for i, start in enumerate((size - LANES, 0))
    ]
    for copy in cols + rows:
        copy.start()
    for s in range(slices):
        cols[2 * s].wait()
        cols[2 * s + 1].wait()
        near[s], far[s] = swapped(
            odd,
            high_rim(columns[s, 0, 0], columns[s, 0, 1]),
            low_rim(columns[s, 1, 0], columns[s, 1, 1]),
        )
    for copy in rows:
        copy.wait()


def cut(off, x):
    slices, _, size, _ = x.shape
    rim = shaped(slices, size, LANES)
    return call(
        cut_kernel,
        (shaped(2, 2 * HALO, size), rim, rim),
        room=CUT_ROOM,
        in_specs=[SMEM, pl.BlockSpec(memory_space=pltpu.HBM)],
        out_specs=(VMEM,) * 3,
        scratch_shapes=[
            pltpu.VMEM((slices, 2, 2, size, LANES), F32),
            pltpu.SemaphoreType.DMA((2,)),
            pltpu.SemaphoreType.DMA((slices, 2)),
        ],
        name="cut",
    )(off, x)


def row_corners_kernel(rows_ref, near, far):
    near[...], far[...] = swapped(
        on_odd(),
        high_rim(rows_ref[0, :, -LANES:], rows_ref[1, :, -LANES:]),
        low_rim(rows_ref[0, :, :LANES], rows_ref[1, :, :LANES]),
    )


def row_corners(rows):
    out = shaped(2 * HALO, LANES)
    return call(
        row_corners_kernel,
        (out, out),
        in_specs=[VMEM],
        out_specs=(VMEM, VMEM),
        name="corners",
    )(rows)


def rim_corners_kernel(s, near, far, out_ref):
    for i, ref in enumerate((near, far)):
        out_ref[i, 0:HALO] = ref[s, -HALO:]
        out_ref[i, HALO:] = ref[s, 0:HALO]


def rim_corners(near, far, s):
    return call(
        functools.partial(rim_corners_kernel, s),
        shaped(2, 2 * HALO, LANES),
        in_specs=[VMEM, VMEM],
        out_specs=VMEM,
        name="corners",
    )(near, far)


def chooser(size):
    half = size // 2
    i = lax.broadcasted_iota(jnp.int32, (size, size), 0)
    j = lax.broadcasted_iota(jnp.int32, (size, size), 1)
    picked = jnp.where(j < half, 2 * j, 2 * (j - half) + 1)
    return jnp.where(i == picked, 1.0, 0.0).astype(BF16)


def unmixed(across, turned):
    size = across.shape[1]
    for k in range(size // LANES):
        turned[k] = across[:, k * LANES : (k + 1) * LANES]
    rows = []
    for odd in (0, 1):
        here = pl.ds(odd, across.shape[0] // 2, stride=2)
        rows.append(jnp.concatenate([turned[k, here, :] for k in range(size // LANES)], 1))
    return jnp.concatenate(rows, 0)


def write_tables(t_out):
    size = t_out.shape[1]
    half = size // 2
    i = lax.broadcasted_iota(jnp.int32, (half, half), 0)
    j = lax.broadcasted_iota(jnp.int32, (half, half), 1)
    products = (2 * i * j, 2 * j * i, i * (2 * j + 1), j * (2 * i + 1))
    for which, product in enumerate(products):
        angle = (product % size).astype(F32) * (2.0 * math.pi / size)
        re = jnp.cos(angle) * (1.0 / math.sqrt(size))
        im = jnp.sin(angle) * (-1.0 / math.sqrt(size))
        if which % 2:
            im = -im
        for r, row in enumerate(((re, im), (-im, re))):
            for c, part in enumerate(row):
                at = (slice(r * half, (r + 1) * half), slice(c * half, (c + 1) * half))
                t_out[(2 * which, *at)], t_out[(2 * which + 1, *at)] = split(part)


def prepare_kernel(phase_ref, prop_ref, t_out, turned):
    write_tables(t_out)
    x = phase_ref[...]
    choose = chooser(x.shape[0])
    first, rest = split(x)
    third = (x - first.astype(F32) - rest.astype(F32)).astype(BF16)
    phase = unmixed(dot(first, choose) + dot(rest, choose) + dot(third, choose), turned)
    prop_ref[0] = jnp.cos(phase)
    prop_ref[1] = jnp.sin(phase)


def prepare(phase):
    size = phase.shape[0]
    return call(
        prepare_kernel,
        (shaped(2, size, size), jax.ShapeDtypeStruct((8, size, size), BF16)),
        flops=1 << 28,
        in_specs=[VMEM],
        out_specs=(VMEM, VMEM),
        scratch_shapes=[pltpu.VMEM((size // LANES, size, LANES), F32)],
        name="prepare",
    )(phase)


def assemble(ext, tile, rows, near, far, corner_near, corner_far, odd):
    size = tile.shape[1]
    tiles = size // LANES
    spans = ((0, rows, 0, HALO), (HALO, None, 0, size), (HALO + size, rows, HALO, HALO))
    for top, strip, source, length in spans:
        here = pl.ds(top, length)
        there = pl.ds(source, length)
        for c in range(2):
            for j in range(tiles):
                across = slice(j * LANES, (j + 1) * LANES)
                ext[c, j + 1, here] = (
                    tile[c, :, across] if strip is None else strip[c, there, across]
                )
        w, h = swapped(
            odd,
            near[...] if strip is None else corner_near[there, :],
            far[...] if strip is None else corner_far[there, :],
        )
        ext[0, 0, here] = h
        ext[1, 0, here] = pltpu.roll(h, HALO, 1)
        ext[0, tiles + 1, here] = w
        ext[1, tiles + 1, here] = pltpu.roll(w, HALO, 1)


def place(off_ref, p):
    col = off_ref[p, 1] + HALO
    return off_ref[p, 0], col // LANES, col % LANES


def window(ext, off_ref, p, c, size):
    row, tile, turn = place(off_ref, p)
    keep = lax.broadcasted_iota(jnp.int32, (size, LANES), 1) < LANES - turn
    turned = [
        pltpu.roll(ext[c, tile + j, pl.ds(row, size), :], LANES - turn, 1)
        for j in range(size // LANES + 1)
    ]
    return jnp.concatenate(
        [jnp.where(keep, turned[j], turned[j + 1]) for j in range(size // LANES)], 1
    )


def add_window(acc, off_ref, p, c, value):
    size = value.shape[0]
    row, tile, turn = place(off_ref, p)
    keep = lax.broadcasted_iota(jnp.int32, (size, LANES), 1) >= turn
    count = size // LANES
    turned = [pltpu.roll(value[:, j * LANES : (j + 1) * LANES], turn, 1) for j in range(count)]
    zero = jnp.zeros((size, LANES), F32)
    before = [zero] + turned
    after = turned + [zero]
    for j in range(count + 1):
        at = (c, tile + j, pl.ds(row, size))
        acc[at] = acc[at] + jnp.where(keep, after[j], before[j])


def times(ar, ai, br, bi):
    return ar * br - ai * bi, ar * bi + ai * br


def conj_times(ar, ai, br, bi):
    return ar * br + ai * bi, ar * bi - ai * br


def first_kernel(off, x, rows, near, far, cn, cf, probe, prop, t, psi_out, w_out, ext, *buffers):
    stage = Stage(t, *buffers)
    count, _, size, _ = psi_out.shape
    many = len(stage.group)
    h = stage.half
    assemble(ext, x.at[0], rows, near.at[0], far.at[0], cn, cf, on_odd())

    @pl.loop(0, count // many)
    def _(i):
        first = i * many

        def source(q):
            w = [window(ext, off, first + q, c, size) for c in (0, 1)]
            w_out[first + q, 0], w_out[first + q, 1] = w
            return times(probe[0], probe[1], *w)

        def change(q, e, re, im):
            here = slice(e * h, (e + 1) * h)
            return times(prop[0, here], prop[1, here], re, im)

        def sink(q, re, im):
            psi_out[first + q, 0], psi_out[first + q, 1] = re, im

        stage.forward(source)
        stage.inverse(change, sink)


def leave(acc, near, far, odd):
    last = acc.shape[1] - 1
    near[...], far[...] = swapped(
        odd, low_rim(acc[0, last], acc[1, last]), high_rim(acc[0, 0], acc[1, 0])
    )


def second_kernel(
    off,
    x,
    rows,
    near,
    far,
    corners,
    psi,
    amp,
    t,
    u_out,
    acc,
    near_out,
    far_out,
    ext,
    kept,
    choose,
    turned,
    level,
    *buffers,
):
    stage = Stage(t, *buffers)
    count, _, size, _ = psi.shape
    many = len(stage.group)
    h = stage.half
    odd = on_odd()
    assemble(ext, x.at[1], rows, near.at[1], far.at[1], corners.at[0], corners.at[1], odd)
    acc[...] = jnp.zeros_like(acc)
    choose[...] = chooser(size)

    @pl.loop(0, count // many)
    def _(i):
        first = i * many
        for q in stage.group:
            top, rest = split(amp[first + q])
            level[q] = unmixed(dot(top, choose[...]) + dot(rest, choose[...]), turned.at[q])

        def source(q):
            w = [window(ext, off, first + q, c, size) for c in (0, 1)]
            kept[q, 0], kept[q, 1] = w
            return times(psi[first + q, 0], psi[first + q, 1], *w)

        def change(q, e, re, im):
            magnitude = jnp.sqrt(re * re + im * im)
            keep = 1.0 - level[q, e * h : (e + 1) * h] / jnp.maximum(magnitude, 0.5)
            return re * keep, im * keep

        def sink(q, re, im):
            p = first + q
            u_out[p, 0], u_out[p, 1] = conj_times(kept[q, 0], kept[q, 1], re, im)
            for c, g in enumerate(conj_times(psi[p, 0], psi[p, 1], re, im)):
                add_window(acc, off, p, c, g)

        stage.forward(source)
        stage.inverse(change, sink)

    leave(acc, near_out, far_out, odd)


def third_kernel(factor, u, w, prop, t, beta_out, mine_out, other_out, acc, *buffers):
    stage = Stage(t, *buffers)
    count = u.shape[0]
    many = len(stage.group)
    h = stage.half
    acc[...] = jnp.zeros_like(acc)

    @pl.loop(0, count // many)
    def _(i):
        first = i * many

        def source(q):
            return u[first + q, 0], u[first + q, 1]

        def change(q, e, re, im):
            here = slice(e * h, (e + 1) * h)
            return conj_times(prop[0, here], prop[1, here], re, im)

        def sink(q, re, im):
            p = first + q
            beta_out[p, 0], beta_out[p, 1] = re, im
            for c, g in enumerate(conj_times(w[p, 0], w[p, 1], re, im)):
                acc[c] += g

        stage.forward(source)
        stage.inverse(change, sink)

    mine_out[...] = acc[upper(0)] * factor
    other_out[...] = acc[1 - upper(0)] * factor


def spread_kernel(off, beta, probe, acc, near_out, far_out):
    acc[...] = jnp.zeros_like(acc)

    @pl.loop(0, beta.shape[0])
    def _(p):
        for c, g in enumerate(conj_times(probe[0], probe[1], beta[p, 0], beta[p, 1])):
            add_window(acc, off, p, c, g)

    leave(acc, near_out, far_out, on_odd())


def rim_parts(near, far, odd, c):
    h, w = swapped(odd, near, far)
    if c:
        h, w = pltpu.roll(h, HALO, 1), pltpu.roll(w, HALO, 1)
    lane = lax.broadcasted_iota(jnp.int32, h.shape, 1)
    return jnp.where(lane < HALO, 0.0, h), jnp.where(lane < HALO, w, 0.0)


def merge_kernel(acc, near, far, strip_ref):
    tiles = acc.shape[1] - 2
    end = near.shape[0] - HALO
    for c in range(2):
        for i, start in enumerate((0, end)):
            here, there = pl.ds(i * HALO, HALO), pl.ds(start, HALO)
            h, w = rim_parts(near[there], far[there], on_odd(), c)
            for j in range(tiles):
                value = acc[c, j + 1, there]
                if j == 0:
                    value += w
                if j == tiles - 1:
                    value += h
                strip_ref[c, here, j * LANES : (j + 1) * LANES] = value


def finish_kernel(*refs):
    out_ref = refs[-1]
    size = out_ref.shape[2]
    tiles = size // LANES
    middle = pl.ds(HALO, size)
    for s in range(out_ref.shape[0]):
        acc, near, far, strip = refs[4 * s : 4 * s + 4]
        for c in range(2):
            h, w = rim_parts(near[middle], far[middle], on_odd(), c)
            for j in range(tiles):
                value = acc[c, j + 1, middle]
                if j == 0:
                    value += w
                if j == tiles - 1:
                    value += h
                across = slice(j * LANES, (j + 1) * LANES)
                out_ref[s, c, HALO:-HALO, across] = value[HALO:-HALO]
                out_ref[s, c, :HALO, across] = value[:HALO] + strip[c, HALO:, across]
                out_ref[s, c, -HALO:, across] = value[-HALO:] + strip[c, :HALO, across]


def shift(x, axis, by):
    count = lax.axis_size(axis)
    return lax.ppermute(x, axis, [(i, (i + by) % count) for i in range(count)])


def exchange(near, far):
    count = lax.axis_size("col")
    near = lax.ppermute(near, "col", [(i, i ^ 1) for i in range(count)])
    far = lax.ppermute(far, "col", [(i, (i + i % 2 * 2 - 1) % count) for i in range(count)])
    return near, far


def to_both(strips, axis, width, by):
    if lax.axis_size(axis) == 2:
        return shift(strips, axis, 1)
    return jnp.concatenate(
        [shift(strips[:, :width], axis, by), shift(strips[:, width:], axis, -by)], axis=1
    )


def halving_kernel(at, mine, came, mine_out, other_out):
    half = mine_out.shape[0]
    here = pl.ds(pl.multiple_of(upper(at) * half, half), half)
    there = pl.ds(pl.multiple_of((1 - upper(at)) * half, half), half)
    mine_out[...] = mine[here] + came[here]
    other_out[...] = mine[there] + came[there]


def adding_kernel(mine, came, out):
    out[...] = mine[...] + came[...]


def joining_kernel(at, mine, came, out):
    half = mine.shape[0]
    out[pl.ds(pl.multiple_of(upper(at) * half, half), half)] = mine[...]
    out[pl.ds(pl.multiple_of((1 - upper(at)) * half, half), half)] = came[...]


def ending_kernel(mine, came, out, sem):
    copies = [
        pltpu.make_async_copy(mine, out.at[upper(0)], sem.at[0]),
        pltpu.make_async_copy(came, out.at[1 - upper(0)], sem.at[1]),
    ]
    for copy in copies:
        copy.start()
    for copy in copies:
        copy.wait()


def halvings():
    return [("col", bit) for bit in (1, 2, 4) if bit < lax.axis_size("col")]


def total(mine, other):
    sizes = {axis: lax.axis_size(axis) for axis in ("row", "col")}
    halves = halvings()
    rest = []
    for axis in ("row", "col"):
        bit = 1
        while bit < sizes[axis]:
            if (axis, bit) not in halves:
                rest.append((axis, bit))
            bit *= 2

    def swap(y, axis, bit):
        return lax.ppermute(y, axis, [(i, i ^ bit) for i in range(sizes[axis])])

    def add(x, came):
        return call(
            adding_kernel, shaped(*x.shape), in_specs=[VMEM] * 2, out_specs=VMEM, name="adding"
        )(x, came)

    for at, (axis, bit) in enumerate(halves):
        came = swap(other, axis, bit)
        if at + 1 == len(halves):
            x = add(mine, came)
            break
        out = shaped(mine.shape[0] // 2, mine.shape[1])
        mine, other = call(
            functools.partial(halving_kernel, at + 1),
            (out, out),
            in_specs=[VMEM, VMEM],
            out_specs=(VMEM, VMEM),
            name="halving",
        )(mine, came)
    for axis, bit in rest:
        x = add(x, swap(x, axis, bit))
    for at, (axis, bit) in reversed(list(enumerate(halves))):
        came = swap(x, axis, bit)
        if at == 0:
            return call(
                ending_kernel,
                shaped(2, *x.shape),
                in_specs=[VMEM, VMEM],
                out_specs=pl.BlockSpec(memory_space=pltpu.HBM),
                scratch_shapes=[pltpu.SemaphoreType.DMA((2,))],
                name="ending",
            )(x, came)
        x = call(
            functools.partial(joining_kernel, at),
            shaped(2 * x.shape[0], x.shape[1]),
            in_specs=[VMEM, VMEM],
            out_specs=VMEM,
            name="joining",
        )(x, came)


def local(object_field, offsets, amplitudes, probe, phase):
    tile = object_field.shape[2]
    size = probe.shape[1]
    count = offsets.shape[0]
    off = offsets[:, 0]
    span = tile + 2 * HALO
    ext = pltpu.VMEM((2, tile // LANES + 2, span, LANES), F32)
    flops = count * 2 * 4 * 3 * 2 * size**3

    edges0 = cut_rows(object_field, 0)
    edges1, near, far = cut(off, object_field)
    rows0 = to_both(edges0, "row", HALO, 1)
    near, far = exchange(near, far)
    prop, t = prepare(phase)
    rows1 = to_both(edges1, "row", HALO, 1)
    corner_near, corner_far = row_corners(rows0)
    corner_near, corner_far = exchange(corner_near, corner_far)
    corners1 = rim_corners(near, far, 1)
    corners1 = to_both(corners1, "row", HALO, 1)

    field = shaped(count, 2, size, size)
    buffers = stage_scratch(count, size)
    many = group_of(count)
    everyone = count * lax.axis_size("row") * lax.axis_size("col")
    factor = 1.0 / math.sqrt(everyone)
    psi, w0 = call(
        first_kernel,
        (field, field),
        flops=flops,
        room=ROOM,
        in_specs=[SMEM] + [VMEM] * 9,
        out_specs=(VMEM,) * 2,
        scratch_shapes=[ext, *buffers],
        name="first",
    )(off, object_field, rows0, near, far, corner_near, corner_far, probe, prop, t)
    left_over = (shaped(*ext.shape), shaped(span, LANES), shaped(span, LANES))
    u, sum1, near1, far1 = call(
        second_kernel,
        (field, *left_over),
        flops=flops,
        room=ROOM,
        in_specs=[SMEM] + [VMEM] * 8,
        out_specs=(VMEM,) * 4,
        scratch_shapes=[
            ext,
            pltpu.VMEM((many, 2, size, size), F32),
            pltpu.VMEM((size, size), BF16),
            pltpu.VMEM((many, size // LANES, size, LANES), F32),
            pltpu.VMEM((many, size, size), F32),
            *buffers,
        ],
        name="second",
    )(off, object_field, rows1, near, far, corners1, psi, amplitudes[:, 0], t)
    near1, far1 = exchange(near1, far1)
    beta, mine, other = call(
        functools.partial(third_kernel, factor),
        (field, shaped(size, size), shaped(size, size)),
        flops=flops,
        room=ROOM,
        in_specs=[VMEM] * 4,
        out_specs=(VMEM,) * 3,
        scratch_shapes=[pltpu.VMEM((2, size, size), F32), *buffers],
        name="third",
    )(u, w0, prop, t)
    sum0, near0, far0 = call(
        spread_kernel,
        left_over,
        room=ROOM,
        in_specs=[SMEM] + [VMEM] * 2,
        out_specs=(VMEM,) * 3,
        name="spread",
    )(off, beta, probe)
    near0, far0 = exchange(near0, far0)
    merge = call(
        merge_kernel,
        shaped(2, 2 * HALO, tile),
        in_specs=[VMEM] * 3,
        out_specs=VMEM,
        name="merge",
    )
    strip1 = merge(sum1, near1, far1)
    back1 = to_both(strip1, "row", HALO, -1)
    strip0 = merge(sum0, near0, far0)
    back0 = to_both(strip0, "row", HALO, -1)
    grad = call(
        finish_kernel,
        shaped(2, 2, tile, tile),
        room=16,
        in_specs=[VMEM] * 8,
        out_specs=VMEM,
        name="finish",
    )(sum0, near0, far0, back0, sum1, near1, far1, back1)
    return grad, total(mine, other)


def solution(mesh):
    in_specs = (
        P(None, None, "row", "col"),
        P("row", "col", None),
        P("row", "col", None, None),
        P(),
        P(),
    )
    out_specs = (P(None, None, "row", "col"), P())

    return jax.shard_map(local, mesh=mesh, in_specs=in_specs, out_specs=out_specs, check_vma=False)
```

time: 104 us -> 85.2 us (0.82)
  the two profiles are of different devices: /device:TPU:10 before, /device:TPU:0 now
where the time goes in v3:
time: 85.2 us; the launch traced here: 84.9 us
  Pallas kernels  29.7 us (35%)
  starting transfers between devices  27.8 us (33%)
  waiting for transfers between devices  24.7 us (29%)
  local copies, waits for them, and re-layouts  1.64 us (2%)
  between operations  1.08 us (1%)
    ppermute x8, waiting for transfers between devices, swap(): return lax.ppermute(y, axis, [(i, i ^ bit) for i in range(sizes[axis])])  16.9 us
    ppermute x4, starting transfers between devices, exchange(): lax.ppermute(far, 'col', [(i, (i + i % 2 * 2 - 1) % count) for i in range...  16.4 us
    ppermute x5, waiting for transfers between devices, shift(): return lax.ppermute(x, axis, [(i, (i + by) % count) for i in range(count)])  7.77 us
    ppermute x5, starting transfers between devices, shift(): return lax.ppermute(x, axis, [(i, (i + by) % count) for i in range(count)])  7.31 us
    pallas_call x1, Pallas kernels, local(): call(second_kernel, (field, *left_over), flops=flops, room=ROOM, in_specs...  6.35 us
    pallas_call x1, Pallas kernels, local(): call(first_kernel, (field, field), flops=flops, room=ROOM, in_specs=[SMEM...  5.74 us
    pallas_call x1, Pallas kernels, local(): call(functools.partial(third_kernel, factor), (field, shaped(size, size),...  4 us
    ppermute x8, starting transfers between devices, swap(): return lax.ppermute(y, axis, [(i, i ^ bit) for i in range(sizes[axis])])  3.74 us
  transfers between devices with their start and end apart: 21, of which 9 were waited for; matrix products, arithmetic and copies ran while one was open for 1% of the time, Pallas kernels for 20%

profile of v3, /device:TPU:0, one launch (start us, length us, event | category | flops | bytes accessed | tf_op | source)
XLA Modules:
  0.0 84.9 jit_solution(14880144959641139870)
XLA Ops:
  0.6 1.8 %cut.3 = f32[2,128,384]{2,1,0:T(8,128)} custom-call(f32[2,2,384,384]{3,2,1,0:T(8,128)} %x.3), custom_call_target="tpu_custom_call" | custom-call | bytes 4194304 | tf_op jit(solution)/shard_map/cut/pallas_call | solution.py:163
  2.5 3.1 %collective-permute-start.4 = (f32[2,128,384]{2,1,0:T(8,128)}, f32[2,128,384]{2,1,0:T(8,128)}, u32[]{:S(2)}, u32[]{:S(2)}) collective-permute-start(f32[2,128,384]{2,1,0:T(8,128)} %cut.3), channel_id=1, source_target_pairs={{0,16},{16,0},{1,17},{17,1},{2,18},{18,2},{3,19},{19,3},{4,20},{20... | collective-permute-start | bytes 1179656 | tf_op jit(solution)/shard_map/ppermute | solution.py:558
  6.2 3.5 %cut.2 = (f32[2,128,384]{2,1,0:T(8,128)}, f32[2,384,128]{2,1,0:T(8,128)}, f32[2,384,128]{2,1,0:T(8,128)}) custom-call(s32[4,2]{1,0:T(4,128)} %copy.10.off, f32[2,2,384,384]{3,2,1,0:T(8,128)} %x.3), custom_call_target="tpu_custom_call" | custom-call | bytes 4194304 | tf_op jit(solution)/shard_map/cut/pallas_call | solution.py:202
  9.8 4.6 %collective-permute-start.2 = (f32[2,384,128]{2,1,0:T(8,128)}, f32[2,384,128]{2,1,0:T(8,128)S(1)}, u32[]{:S(2)}, u32[]{:S(2)}) collective-permute-start(f32[2,384,128]{2,1,0:T(8,128)} %get-tuple-element.27), channel_id=1, source_target_pairs={{0,15},{1,2},{2,1},{3,4},{4,3},{5,6},{6,5},{7,8},{8,7},{9,10},{10,... | collective-permute-start | bytes 1179656 | tf_op jit(solution)/shard_map/ppermute | solution.py:564
  16.7 5.4 %collective-permute-start.6 = (f32[128,128]{1,0:T(8,128)S(1)}, f32[128,128]{1,0:T(8,128)S(1)}, u32[]{:S(2)}, u32[]{:S(2)}) collective-permute-start(f32[128,128]{1,0:T(8,128)S(1)} %get-tuple-element.29), channel_id=1, source_target_pairs={{0,15},{1,2},{2,1},{3,4},{4,3},{5,6},{6,5},{7,8},{8,7},{9,10},{10,... | collective-permute-start | bytes 196616 | tf_op jit(solution)/shard_map/ppermute | solution.py:564
  23.1 2.3 %prepare.1 = (f32[2,256,256]{2,1,0:T(8,128)S(1)}, bf16[8,256,256]{2,1,0:T(8,128)(2,1)S(1)}) custom-call(f32[256,256]{1,0:T(8,128)S(1)} %copy-done.4), custom_call_target="tpu_custom_call" | custom-call | flops 268435456 | bytes 4194304 | tf_op jit(solution)/shard_map/prepare/pallas_call | solution.py:302
  25.4 1.6 %collective-permute-start.3 = (f32[2,128,128]{2,1,0:T(8,128)S(1)}, f32[2,128,128]{2,1,0:T(8,128)S(1)}, u32[]{:S(2)}, u32[]{:S(2)}) collective-permute-start(f32[2,128,128]{2,1,0:T(8,128)S(1)} %corners.2), channel_id=1, source_target_pairs={{0,16},{16,0},{1,17},{17,1},{2,18},{18,2},{3,19},{19,3},{4,20},{20... | collective-permute-start | bytes 393224 | tf_op jit(solution)/shard_map/ppermute | solution.py:558
  27.0 5.7 %first.1 = (f32[4,2,256,256]{3,2,1,0:T(8,128)S(1)}, f32[4,2,256,256]{3,2,1,0:T(8,128)S(1)}) custom-call(s32[4,2]{1,0:T(4,128)S(1)} %copy-done.2, f32[2,2,384,384]{3,2,1,0:T(8,128)S(1)} %copy-done, f32[2,128,384]{2,1,0:T(8,128)} %collective-permute-done.4.rows_ref.rows, f32[2,384,128]{2,1,0:T(8,128)S(1)} %collective-permute-done.1.near, ...), custom_call_target="tpu_custom_call" | custom-call | flops 3221225472 | bytes 4194304 | tf_op jit(solution)/shard_map/first/pallas_call | solution.py:688
  32.8 6.3 %second.1 = (f32[4,2,256,256]{3,2,1,0:T(8,128)S(1)}, f32[2,5,512,128]{3,2,1,0:T(8,128)S(1)}, f32[512,128]{1,0:T(8,128)S(1)}, f32[512,128]{1,0:T(8,128)S(1)}) custom-call(s32[4,2]{1,0:T(4,128)S(1)} %copy-done.2, f32[2,2,384,384]{3,2,1,0:T(8,128)S(1)} %copy-done, f32[2,128,384]{2,1,0:T(8,128)S(1)} %collective-permute-done.rows, ...), custom_call_target="tpu_custom_call" | custom-call | flops 3221225472 | bytes 4194304 | tf_op jit(solution)/shard_map/second/pallas_call | solution.py:699
  39.2 4.0 %third.1 = (f32[4,2,256,256]{3,2,1,0:T(8,128)S(1)}, f32[256,256]{1,0:T(8,128)S(1)}, f32[256,256]{1,0:T(8,128)S(1)}) custom-call(f32[4,2,256,256]{3,2,1,0:T(8,128)S(1)} %get-tuple-element.33.u, f32[4,2,256,256]{3,2,1,0:T(8,128)S(1)} %get-tuple-element.34.w, f32[2,256,256]{2,1,0:T(8,128)S(1)} %get-tuple-element.30.prop, ...), custom_call_target="tpu_custom_call" | custom-call | flops 3221225472 | bytes 4194304 | tf_op jit(solution)/shard_map/third/pallas_call | solution.py:717
  43.3 1.5 %collective-permute-done.13.came = f32[256,256]{1,0:T(8,128)S(1)} collective-permute-done((f32[256,256]{1,0:T(8,128)S(1)}, f32[256,256]{1,0:T(8,128)S(1)}, u32[]{:S(2)}, u32[]{:S(2)}) %collective-permute-start.13) | collective-permute-done | bytes 262176 | tf_op jit(solution)/shard_map/ppermute | solution.py:621
  45.1 1.9 %collective-permute-start.11 = (f32[512,128]{1,0:T(8,128)S(1)}, f32[512,128]{1,0:T(8,128)S(1)}, u32[]{:S(2)}, u32[]{:S(2)}) collective-permute-start(f32[512,128]{1,0:T(8,128)S(1)} %get-tuple-element.41), channel_id=1, source_target_pairs={{0,15},{1,2},{2,1},{3,4},{4,3},{5,6},{6,5},{7,8},{8,7},{9,10},{10,... | collective-permute-start | bytes 786440 | tf_op jit(solution)/shard_map/ppermute | solution.py:564
  47.0 1.9 %spread.1 = (f32[2,5,512,128]{3,2,1,0:T(8,128)S(1)}, f32[512,128]{1,0:T(8,128)S(1)}, f32[512,128]{1,0:T(8,128)S(1)}) custom-call(s32[4,2]{1,0:T(4,128)S(1)} %copy-done.2, f32[4,2,256,256]{3,2,1,0:T(8,128)S(1)} %get-tuple-element.35.beta, f32[2,256,256]{2,1,0:T(8,128)S(1)} %copy-done.1), custom_call_target="tpu_custom_call" | custom-call | bytes 4194304 | tf_op jit(solution)/shard_map/spread/pallas_call | solution.py:727
  49.0 1.5 %collective-permute-done.14.came = f32[128,256]{1,0:T(8,128)S(1)} collective-permute-done((f32[128,256]{1,0:T(8,128)S(1)}, f32[128,256]{1,0:T(8,128)S(1)}, u32[]{:S(2)}, u32[]{:S(2)}) %collective-permute-start.14) | collective-permute-done | bytes 131104 | tf_op jit(solution)/shard_map/ppermute | solution.py:621
  51.3 4.5 %collective-permute-start.8 = (f32[512,128]{1,0:T(8,128)S(1)}, f32[512,128]{1,0:T(8,128)S(1)}, u32[]{:S(2)}, u32[]{:S(2)}) collective-permute-start(f32[512,128]{1,0:T(8,128)S(1)} %get-tuple-element.38), channel_id=1, source_target_pairs={{0,15},{1,2},{2,1},{3,4},{4,3},{5,6},{6,5},{7,8},{8,7},{9,10},{10,... | collective-permute-start | bytes 786440 | tf_op jit(solution)/shard_map/ppermute | solution.py:564
  55.9 4.3 %collective-permute-done.16.came = f32[64,256]{1,0:T(8,128)S(1)} collective-permute-done((f32[64,256]{1,0:T(8,128)S(1)}, f32[64,256]{1,0:T(8,128)S(1)}, u32[]{:S(2)}, u32[]{:S(2)}) %collective-permute-start.16) | collective-permute-done | bytes 65568 | tf_op jit(solution)/shard_map/ppermute | solution.py:621
  60.2 1.4 %collective-permute-start.17 = (f32[64,256]{1,0:T(8,128)S(1)}, f32[64,256]{1,0:T(8,128)S(1)}, u32[]{:S(2)}, u32[]{:S(2)}) collective-permute-start(f32[64,256]{1,0:T(8,128)S(1)} %adding.4.mine), channel_id=1, source_target_pairs={{0,8},{1,9},{2,10},{3,11},{4,12},{5,13},{6,14},{7,15},{8,0},{9,1},... | collective-permute-start | bytes 196616 | tf_op jit(solution)/shard_map/ppermute | solution.py:621
  61.6 3.9 %collective-permute-done.17.came = f32[64,256]{1,0:T(8,128)S(1)} collective-permute-done((f32[64,256]{1,0:T(8,128)S(1)}, f32[64,256]{1,0:T(8,128)S(1)}, u32[]{:S(2)}, u32[]{:S(2)}) %collective-permute-start.17) | collective-permute-done | bytes 65568 | tf_op jit(solution)/shard_map/ppermute | solution.py:621
  66.2 1.8 %collective-permute-start.9 = (f32[2,128,384]{2,1,0:T(8,128)S(1)}, f32[2,128,384]{2,1,0:T(8,128)S(1)}, u32[]{:S(2)}, u32[]{:S(2)}) collective-permute-start(f32[2,128,384]{2,1,0:T(8,128)S(1)} %merge.2), channel_id=1, source_target_pairs={{0,16},{16,0},{1,17},{17,1},{2,18},{18,2},{3,19},{19,3},{4,20},{20... | collective-permute-start | bytes 1179656 | tf_op jit(solution)/shard_map/ppermute | solution.py:558
  68.0 1.8 %collective-permute-done.18.came = f32[64,256]{1,0:T(8,128)S(1)} collective-permute-done((f32[64,256]{1,0:T(8,128)S(1)}, f32[64,256]{1,0:T(8,128)S(1)}, u32[]{:S(2)}, u32[]{:S(2)}) %collective-permute-start.18) | collective-permute-done | bytes 65568 | tf_op jit(solution)/shard_map/ppermute | solution.py:621
  71.0 3.9 %collective-permute-done.19.came = f32[128,256]{1,0:T(8,128)S(1)} collective-permute-done((f32[128,256]{1,0:T(8,128)S(1)}, f32[128,256]{1,0:T(8,128)S(1)}, u32[]{:S(2)}, u32[]{:S(2)}) %collective-permute-start.19) | collective-permute-done | bytes 131104 | tf_op jit(solution)/shard_map/ppermute | solution.py:621
  75.0 2.8 %collective-permute-done.12.refs_7_ = f32[2,128,384]{2,1,0:T(8,128)S(1)} collective-permute-done((f32[2,128,384]{2,1,0:T(8,128)S(1)}, f32[2,128,384]{2,1,0:T(8,128)S(1)}, u32[]{:S(2)}, u32[]{:S(2)}) %collective-permute-start.12) | collective-permute-done | bytes 393248 | tf_op jit(solution)/shard_map/ppermute | solution.py:558
  77.8 4.4 %collective-permute-done.9.refs_3_ = f32[2,128,384]{2,1,0:T(8,128)S(1)} collective-permute-done((f32[2,128,384]{2,1,0:T(8,128)S(1)}, f32[2,128,384]{2,1,0:T(8,128)S(1)}, u32[]{:S(2)}, u32[]{:S(2)}) %collective-permute-start.9) | collective-permute-done | bytes 393248 | tf_op jit(solution)/shard_map/ppermute | solution.py:558
  82.1 1.9 %finish.1 = f32[2,2,384,384]{3,2,1,0:T(8,128)} custom-call(f32[2,5,512,128]{3,2,1,0:T(8,128)S(1)} %get-tuple-element.36.acc.refs_0_, f32[512,128]{1,0:T(8,128)S(1)} %collective-permute-done.7.near.refs_1_, f32[512,128]{1,0:T(8,128)S(1)} %collective-permute-done.8.far.refs_2_, f32[2,128,384]{2,1,0:T(8,128)S(1)} %collective-permute-done.9.refs_3_, ...), custom_call_target="tpu_custom_call" | custom-call | bytes 4194304 | tf_op jit(solution)/shard_map/finish/pallas_call | solution.py:747
  (51 shorter events, 8.1 us)
Async XLA Ops:
  2.4 24.6 %copy-start = (f32[2,2,384,384]{3,2,1,0:T(8,128)S(1)}, f32[2,2,384,384]{3,2,1,0:T(8,128)}, u32[]{:S(2)}) copy-start(f32[2,2,384,384]{3,2,1,0:T(8,128)} %x.3) | copy-start | bytes 7077892
  2.5 24.6 %copy-start.1 = (f32[2,256,256]{2,1,0:T(8,128)S(1)}, f32[2,256,256]{2,1,0:T(8,128)}, u32[]{:S(2)}) copy-start(f32[2,256,256]{2,1,0:T(8,128)} %probe.3) | copy-start | bytes 1572868
  2.5 13.1 %collective-permute-start.4 = (f32[2,128,384]{2,1,0:T(8,128)}, f32[2,128,384]{2,1,0:T(8,128)}, u32[]{:S(2)}, u32[]{:S(2)}) collective-permute-start(f32[2,128,384]{2,1,0:T(8,128)} %cut.3), channel_id=1, source_target_pairs={{0,16},{16,0},{1,17},{17,1},{2,18},{18,2},{3,19},{19,3},{4,20},{20... | collective-permute-start | bytes 1179656 | tf_op jit(solution)/shard_map/ppermute | solution.py:558
  6.2 20.8 %copy-start.2 = (s32[4,2]{1,0:T(4,128)S(1)}, s32[4,2]{1,0:T(4,128)}, u32[]{:S(2)}) copy-start(s32[4,2]{1,0:T(4,128)} %copy.10.off) | copy-start | bytes 100
  9.7 15.7 %collective-permute-start.1 = (f32[2,384,128]{2,1,0:T(8,128)}, f32[2,384,128]{2,1,0:T(8,128)S(1)}, u32[]{:S(2)}, u32[]{:S(2)}) collective-permute-start(f32[2,384,128]{2,1,0:T(8,128)} %get-tuple-element.26), channel_id=1, source_target_pairs={{0,1},{1,0},{2,3},{3,2},{4,5},{5,4},{6,7},{7,6},{8,9},{9,8},{10,11... | collective-permute-start | bytes 1179656 | tf_op jit(solution)/shard_map/ppermute | solution.py:563
  9.8 15.6 %collective-permute-start.2 = (f32[2,384,128]{2,1,0:T(8,128)}, f32[2,384,128]{2,1,0:T(8,128)S(1)}, u32[]{:S(2)}, u32[]{:S(2)}) collective-permute-start(f32[2,384,128]{2,1,0:T(8,128)} %get-tuple-element.27), channel_id=1, source_target_pairs={{0,15},{1,2},{2,1},{3,4},{4,3},{5,6},{6,5},{7,8},{8,7},{9,10},{10,... | collective-permute-start | bytes 1179656 | tf_op jit(solution)/shard_map/ppermute | solution.py:564
  14.4 18.4 %collective-permute-start = (f32[2,128,384]{2,1,0:T(8,128)}, f32[2,128,384]{2,1,0:T(8,128)S(1)}, u32[]{:S(2)}, u32[]{:S(2)}) collective-permute-start(f32[2,128,384]{2,1,0:T(8,128)} %get-tuple-element.25), channel_id=1, source_target_pairs={{0,16},{16,0},{1,17},{17,1},{2,18},{18,2},{3,19},{19,3},{4,20},{20... | collective-permute-start | bytes 1179656 | tf_op jit(solution)/shard_map/ppermute | solution.py:558
  16.7 10.3 %collective-permute-start.5 = (f32[128,128]{1,0:T(8,128)S(1)}, f32[128,128]{1,0:T(8,128)S(1)}, u32[]{:S(2)}, u32[]{:S(2)}) collective-permute-start(f32[128,128]{1,0:T(8,128)S(1)} %get-tuple-element.28), channel_id=1, source_target_pairs={{0,1},{1,0},{2,3},{3,2},{4,5},{5,4},{6,7},{7,6},{8,9},{9,8},{10,11... | collective-permute-start | bytes 196616 | tf_op jit(solution)/shard_map/ppermute | solution.py:563
  16.7 10.3 %collective-permute-start.6 = (f32[128,128]{1,0:T(8,128)S(1)}, f32[128,128]{1,0:T(8,128)S(1)}, u32[]{:S(2)}, u32[]{:S(2)}) collective-permute-start(f32[128,128]{1,0:T(8,128)S(1)} %get-tuple-element.29), channel_id=1, source_target_pairs={{0,15},{1,2},{2,1},{3,4},{4,3},{5,6},{6,5},{7,8},{8,7},{9,10},{10,... | collective-permute-start | bytes 196616 | tf_op jit(solution)/shard_map/ppermute | solution.py:564
  25.4 7.4 %collective-permute-start.3 = (f32[2,128,128]{2,1,0:T(8,128)S(1)}, f32[2,128,128]{2,1,0:T(8,128)S(1)}, u32[]{:S(2)}, u32[]{:S(2)}) collective-permute-start(f32[2,128,128]{2,1,0:T(8,128)S(1)} %corners.2), channel_id=1, source_target_pairs={{0,16},{16,0},{1,17},{17,1},{2,18},{18,2},{3,19},{19,3},{4,20},{20... | collective-permute-start | bytes 393224 | tf_op jit(solution)/shard_map/ppermute | solution.py:558
  43.2 1.6 %collective-permute-start.13 = (f32[256,256]{1,0:T(8,128)S(1)}, f32[256,256]{1,0:T(8,128)S(1)}, u32[]{:S(2)}, u32[]{:S(2)}) collective-permute-start(f32[256,256]{1,0:T(8,128)S(1)} %get-tuple-element.43), channel_id=1, source_target_pairs={{0,1},{1,0},{2,3},{3,2},{4,5},{5,4},{6,7},{7,6},{8,9},{9,8},{10,11... | collective-permute-start | bytes 786440 | tf_op jit(solution)/shard_map/ppermute | solution.py:621
  44.8 5.6 %collective-permute-start.14 = (f32[128,256]{1,0:T(8,128)S(1)}, f32[128,256]{1,0:T(8,128)S(1)}, u32[]{:S(2)}, u32[]{:S(2)}) collective-permute-start(f32[128,256]{1,0:T(8,128)S(1)} %get-tuple-element.45), channel_id=1, source_target_pairs={{0,2},{1,3},{2,0},{3,1},{4,6},{5,7},{6,4},{7,5},{8,10},{9,11},{10,... | collective-permute-start | bytes 393224 | tf_op jit(solution)/shard_map/ppermute | solution.py:621
  44.9 20.7 %collective-permute-start.10 = (f32[512,128]{1,0:T(8,128)S(1)}, f32[512,128]{1,0:T(8,128)S(1)}, u32[]{:S(2)}, u32[]{:S(2)}) collective-permute-start(f32[512,128]{1,0:T(8,128)S(1)} %get-tuple-element.40), channel_id=1, source_target_pairs={{0,1},{1,0},{2,3},{3,2},{4,5},{5,4},{6,7},{7,6},{8,9},{9,8},{10,11... | collective-permute-start | bytes 786440 | tf_op jit(solution)/shard_map/ppermute | solution.py:563
  45.1 20.5 %collective-permute-start.11 = (f32[512,128]{1,0:T(8,128)S(1)}, f32[512,128]{1,0:T(8,128)S(1)}, u32[]{:S(2)}, u32[]{:S(2)}) collective-permute-start(f32[512,128]{1,0:T(8,128)S(1)} %get-tuple-element.41), channel_id=1, source_target_pairs={{0,15},{1,2},{2,1},{3,4},{4,3},{5,6},{6,5},{7,8},{8,7},{9,10},{10,... | collective-permute-start | bytes 786440 | tf_op jit(solution)/shard_map/ppermute | solution.py:564
  50.5 5.4 %collective-permute-start.15 = (f32[64,256]{1,0:T(8,128)S(1)}, f32[64,256]{1,0:T(8,128)S(1)}, u32[]{:S(2)}, u32[]{:S(2)}) collective-permute-start(f32[64,256]{1,0:T(8,128)S(1)} %get-tuple-element.47), channel_id=1, source_target_pairs={{0,4},{1,5},{2,6},{3,7},{4,0},{5,1},{6,2},{7,3},{8,12},{9,13},{10,... | collective-permute-start | bytes 196616 | tf_op jit(solution)/shard_map/ppermute | solution.py:621
  51.3 14.8 %collective-permute-start.7 = (f32[512,128]{1,0:T(8,128)S(1)}, f32[512,128]{1,0:T(8,128)S(1)}, u32[]{:S(2)}, u32[]{:S(2)}) collective-permute-start(f32[512,128]{1,0:T(8,128)S(1)} %get-tuple-element.37), channel_id=1, source_target_pairs={{0,1},{1,0},{2,3},{3,2},{4,5},{5,4},{6,7},{7,6},{8,9},{9,8},{10,11... | collective-permute-start | bytes 786440 | tf_op jit(solution)/shard_map/ppermute | solution.py:563
  51.3 14.8 %collective-permute-start.8 = (f32[512,128]{1,0:T(8,128)S(1)}, f32[512,128]{1,0:T(8,128)S(1)}, u32[]{:S(2)}, u32[]{:S(2)}) collective-permute-start(f32[512,128]{1,0:T(8,128)S(1)} %get-tuple-element.38), channel_id=1, source_target_pairs={{0,15},{1,2},{2,1},{3,4},{4,3},{5,6},{6,5},{7,8},{8,7},{9,10},{10,... | collective-permute-start | bytes 786440 | tf_op jit(solution)/shard_map/ppermute | solution.py:564
  55.8 4.3 %collective-permute-start.16 = (f32[64,256]{1,0:T(8,128)S(1)}, f32[64,256]{1,0:T(8,128)S(1)}, u32[]{:S(2)}, u32[]{:S(2)}) collective-permute-start(f32[64,256]{1,0:T(8,128)S(1)} %adding.3.mine), channel_id=1, source_target_pairs={{0,16},{16,0},{1,17},{17,1},{2,18},{18,2},{3,19},{19,3},{4,20},{20... | collective-permute-start | bytes 196616 | tf_op jit(solution)/shard_map/ppermute | solution.py:621
  60.2 5.3 %collective-permute-start.17 = (f32[64,256]{1,0:T(8,128)S(1)}, f32[64,256]{1,0:T(8,128)S(1)}, u32[]{:S(2)}, u32[]{:S(2)}) collective-permute-start(f32[64,256]{1,0:T(8,128)S(1)} %adding.4.mine), channel_id=1, source_target_pairs={{0,8},{1,9},{2,10},{3,11},{4,12},{5,13},{6,14},{7,15},{8,0},{9,1},... | collective-permute-start | bytes 196616 | tf_op jit(solution)/shard_map/ppermute | solution.py:621
  65.5 4.3 %collective-permute-start.18 = (f32[64,256]{1,0:T(8,128)S(1)}, f32[64,256]{1,0:T(8,128)S(1)}, u32[]{:S(2)}, u32[]{:S(2)}) collective-permute-start(f32[64,256]{1,0:T(8,128)S(1)} %adding.5.mine), channel_id=1, source_target_pairs={{0,4},{1,5},{2,6},{3,7},{4,0},{5,1},{6,2},{7,3},{8,12},{9,13},{10,... | collective-permute-start | bytes 196616 | tf_op jit(solution)/shard_map/ppermute | solution.py:621
  65.7 12.1 %collective-permute-start.12 = (f32[2,128,384]{2,1,0:T(8,128)S(1)}, f32[2,128,384]{2,1,0:T(8,128)S(1)}, u32[]{:S(2)}, u32[]{:S(2)}) collective-permute-start(f32[2,128,384]{2,1,0:T(8,128)S(1)} %merge.3), channel_id=1, source_target_pairs={{0,16},{16,0},{1,17},{17,1},{2,18},{18,2},{3,19},{19,3},{4,20},{20... | collective-permute-start | bytes 1179656 | tf_op jit(solution)/shard_map/ppermute | solution.py:558
  66.2 15.9 %collective-permute-start.9 = (f32[2,128,384]{2,1,0:T(8,128)S(1)}, f32[2,128,384]{2,1,0:T(8,128)S(1)}, u32[]{:S(2)}, u32[]{:S(2)}) collective-permute-start(f32[2,128,384]{2,1,0:T(8,128)S(1)} %merge.2), channel_id=1, source_target_pairs={{0,16},{16,0},{1,17},{17,1},{2,18},{18,2},{3,19},{19,3},{4,20},{20... | collective-permute-start | bytes 1179656 | tf_op jit(solution)/shard_map/ppermute | solution.py:558
  69.8 5.0 %collective-permute-start.19 = (f32[128,256]{1,0:T(8,128)S(1)}, f32[128,256]{1,0:T(8,128)S(1)}, u32[]{:S(2)}, u32[]{:S(2)}) collective-permute-start(f32[128,256]{1,0:T(8,128)S(1)} %joining.2.mine), channel_id=1, source_target_pairs={{0,2},{1,3},{2,0},{3,1},{4,6},{5,7},{6,4},{7,5},{8,10},{9,11},{10,... | collective-permute-start | bytes 393224 | tf_op jit(solution)/shard_map/ppermute | solution.py:621
  74.9 9.1 %collective-permute-start.20 = (f32[256,256]{1,0:T(8,128)S(1)}, f32[256,256]{1,0:T(8,128)S(1)}, u32[]{:S(2)}, u32[]{:S(2)}) collective-permute-start(f32[256,256]{1,0:T(8,128)S(1)} %joining.3.mine), channel_id=1, source_target_pairs={{0,1},{1,0},{2,3},{3,2},{4,5},{5,4},{6,7},{7,6},{8,9},{9,8},{10,11... | collective-permute-start | bytes 786440 | tf_op jit(solution)/shard_map/ppermute | solution.py:621
  (3 other events, 11.6 us)

commit v4 on v3

--- a/solution.py
+++ b/solution.py
@@ -10,7 +10,6 @@
 
 HALO = 64
 ROOM = 20
-CUT_ROOM = 61
 LANES = 128
 F32 = jnp.float32
 BF16 = jnp.bfloat16
@@ -140,78 +139,38 @@
     return jnp.where(odd, b, a), jnp.where(odd, a, b)
 
 
-def row_copies(x_ref, s, out, sem):
+def cut_rows_kernel(s, x_ref, out):
     size = x_ref.shape[2]
-    return [
-        pltpu.make_async_copy(
-            x_ref.at[s, :, pl.ds(start, HALO), :], out.at[:, pl.ds(i * HALO, HALO), :], sem.at[i]
-        )
-        for i, start in enumerate((size - HALO, 0))
-    ]
-
-
-def cut_rows_kernel(s, x_ref, out, sem):
-    copies = row_copies(x_ref, s, out, sem)
-    for copy in copies:
-        copy.start()
-    for copy in copies:
-        copy.wait()
+    for c in range(2):
+        out[c, :HALO] = x_ref[s, c, size - HALO :]
+        out[c, HALO:] = x_ref[s, c, :HALO]
 
 
 def cut_rows(x, s):
-    size = x.shape[2]
     return call(
         functools.partial(cut_rows_kernel, s),
-        shaped(2, 2 * HALO, size),
-        room=CUT_ROOM + 1,
-        in_specs=[pl.BlockSpec(memory_space=pltpu.HBM)],
+        shaped(2, 2 * HALO, x.shape[2]),
+        in_specs=[VMEM],
         out_specs=VMEM,
-        scratch_shapes=[pltpu.SemaphoreType.DMA((2,))],
         name="cut",
     )(x)
 
 
-def cut_kernel(off, x_ref, edge, near, far, columns, sem, col_sem):
-    odd = on_odd()
-    slices, _, size, _ = x_ref.shape
-    rows = row_copies(x_ref, slices - 1, edge, sem)
-    cols = [
-        pltpu.make_async_copy(
-            x_ref.at[s, :, :, pl.ds(start, LANES)], columns.at[s, i], col_sem.at[s, i]
+def cut_kernel(x_ref, near, far):
+    for s in range(x_ref.shape[0]):
+        near[s], far[s] = swapped(
+            on_odd(),
+            high_rim(x_ref[s, 0, :, -LANES:], x_ref[s, 1, :, -LANES:]),
+            low_rim(x_ref[s, 0, :, :LANES], x_ref[s, 1, :, :LANES]),
         )
-        for s in range(slices)
-        for i, start in enumerate((size - LANES, 0))
-    ]
-    for copy in cols + rows:
-        copy.start()
-    for s in range(slices):
-        cols[2 * s].wait()
-        cols[2 * s + 1].wait()
-        near[s], far[s] = swapped(
-            odd,
-            high_rim(columns[s, 0, 0], columns[s, 0, 1]),
-            low_rim(columns[s, 1, 0], columns[s, 1, 1]),
-        )
-    for copy in rows:
-        copy.wait()
-
-
-def cut(off, x):
+
+
+def cut(x):
     slices, _, size, _ = x.shape
     rim = shaped(slices, size, LANES)
     return call(
-        cut_kernel,
-        (shaped(2, 2 * HALO, size), rim, rim),
-        room=CUT_ROOM,
-        in_specs=[SMEM, pl.BlockSpec(memory_space=pltpu.HBM)],
-        out_specs=(VMEM,) * 3,
-        scratch_shapes=[
-            pltpu.VMEM((slices, 2, 2, size, LANES), F32),
-            pltpu.SemaphoreType.DMA((2,)),
-            pltpu.SemaphoreType.DMA((slices, 2)),
-        ],
-        name="cut",
-    )(off, x)
+        cut_kernel, (rim, rim), in_specs=[VMEM], out_specs=(VMEM,) * 2, name="cut"
+    )(x)
 
 
 def row_corners_kernel(rows_ref, near, far):
@@ -335,8 +294,8 @@
 
 
 def place(off_ref, p):
-    col = off_ref[p, 1] + HALO
-    return off_ref[p, 0], col // LANES, col % LANES
+    col = off_ref[1, p] + HALO
+    return off_ref[0, p], col // LANES, col % LANES
 
 
 def window(ext, off_ref, p, c, size):
@@ -560,8 +519,8 @@
 
 def exchange(near, far):
     count = lax.axis_size("col")
+    far = lax.ppermute(far, "col", [(i, (i + i % 2 * 2 - 1) % count) for i in range(count)])
     near = lax.ppermute(near, "col", [(i, i ^ 1) for i in range(count)])
-    far = lax.ppermute(far, "col", [(i, (i + i % 2 * 2 - 1) % count) for i in range(count)])
     return near, far
 
 
@@ -664,13 +623,14 @@
     tile = object_field.shape[2]
     size = probe.shape[1]
     count = offsets.shape[0]
-    off = offsets[:, 0]
+    off = jnp.transpose(offsets[:, 0])
     span = tile + 2 * HALO
     ext = pltpu.VMEM((2, tile // LANES + 2, span, LANES), F32)
     flops = count * 2 * 4 * 3 * 2 * size**3
 
     edges0 = cut_rows(object_field, 0)
-    edges1, near, far = cut(off, object_field)
+    near, far = cut(object_field)
+    edges1 = cut_rows(object_field, 1)
     rows0 = to_both(edges0, "row", HALO, 1)
     near, far = exchange(near, far)
     prop, t = prepare(phase)

time: 85.2 us -> 83.3 us (0.978)
  Pallas kernels: 29.7 us -> 24.4 us
  waiting for transfers between devices: 24.7 us -> 28 us
    pallas_call x2 -> x3, Pallas kernels: 5.3 us -> 0.32 us  [the longest x1 0.27 us: cut(): call(cut_kernel, (rim, rim), in_specs=[VMEM], out_specs=(VMEM,) * 2, name...]
    ppermute x5, waiting for transfers between devices: 7.77 us -> 11.6 us  [shift(): return lax.ppermute(x, axis, [(i, (i + by) % count) for i in range(count)])]
    pallas_call x1, Pallas kernels: 1.09 us -> 0.1 us  [row_corners(): call(row_corners_kernel, (out, out), in_specs=[VMEM], out_specs=(VMEM, VM...]
  transfers between devices with their start and end apart: 21 -> 21, of which waited for: 9 -> 9; matrix products, arithmetic and copies ran while one was open for 1% -> 0% of each run, Pallas kernels for 20% -> 15%
where the time goes in v4:
time: 83.3 us; the launch traced here: 83.2 us
  starting transfers between devices  28 us (34%)
  waiting for transfers between devices  28 us (34%)
  Pallas kernels  24.4 us (29%)
  local copies, waits for them, and re-layouts  1.69 us (2%)
  between operations  1.09 us (1%)
    ppermute x4, starting transfers between devices, exchange(): lax.ppermute(far, 'col', [(i, (i + i % 2 * 2 - 1) % count) for i in range...  16.8 us
    ppermute x8, waiting for transfers between devices, swap(): return lax.ppermute(y, axis, [(i, i ^ bit) for i in range(sizes[axis])])  16.4 us
    ppermute x5, waiting for transfers between devices, shift(): return lax.ppermute(x, axis, [(i, (i + by) % count) for i in range(count)])  11.6 us
    ppermute x5, starting transfers between devices, shift(): return lax.ppermute(x, axis, [(i, (i + by) % count) for i in range(count)])  7.37 us
    pallas_call x1, Pallas kernels, local(): call(second_kernel, (field, *left_over), flops=flops, room=ROOM, in_specs...  6.84 us
    pallas_call x1, Pallas kernels, local(): call(first_kernel, (field, field), flops=flops, room=ROOM, in_specs=[SMEM...  5.49 us
    pallas_call x1, Pallas kernels, local(): call(functools.partial(third_kernel, factor), (field, shaped(size, size),...  4.35 us
    ppermute x8, starting transfers between devices, swap(): return lax.ppermute(y, axis, [(i, i ^ bit) for i in range(sizes[axis])])  3.45 us
  transfers between devices with their start and end apart: 21, of which 9 were waited for; matrix products, arithmetic and copies ran while one was open for 0% of the time, Pallas kernels for 15%

profile of v4, /device:TPU:0, one launch (start us, length us, event | category | flops | bytes accessed | tf_op | source)
XLA Modules:
  0.0 83.2 jit_solution(5086701460589156851)
XLA Ops:
  0.6 1.7 %copy-done = f32[2,2,384,384]{3,2,1,0:T(8,128)S(1)} copy-done((f32[2,2,384,384]{3,2,1,0:T(8,128)S(1)}, f32[2,2,384,384]{3,2,1,0:T(8,128)}, u32[]{:S(2)}) %copy-start) | copy-done | bytes 2359320
  2.3 3.1 %collective-permute-start.4 = (f32[2,128,384]{2,1,0:T(8,128)S(1)}, f32[2,128,384]{2,1,0:T(8,128)S(1)}, u32[]{:S(2)}, u32[]{:S(2)}) collective-permute-start(f32[2,128,384]{2,1,0:T(8,128)S(1)} %cut.5), channel_id=1, source_target_pairs={{0,16},{16,0},{1,17},{17,1},{2,18},{18,2},{3,19},{19,3},{4,20},{20... | collective-permute-start | bytes 1179656 | tf_op jit(solution)/shard_map/ppermute | solution.py:517
  5.8 4.6 %collective-permute-start.2 = (f32[2,384,128]{2,1,0:T(8,128)S(1)}, f32[2,384,128]{2,1,0:T(8,128)S(1)}, u32[]{:S(2)}, u32[]{:S(2)}) collective-permute-start(f32[2,384,128]{2,1,0:T(8,128)S(1)} %get-tuple-element.25), channel_id=1, source_target_pairs={{0,15},{1,2},{2,1},{3,4},{4,3},{5,6},{6,5},{7,8},{8,7},{9,10},{10,... | collective-permute-start | bytes 1179656 | tf_op jit(solution)/shard_map/ppermute | solution.py:522
  11.0 4.4 %collective-permute-done.4.rows_ref.rows = f32[2,128,384]{2,1,0:T(8,128)S(1)} collective-permute-done((f32[2,128,384]{2,1,0:T(8,128)S(1)}, f32[2,128,384]{2,1,0:T(8,128)S(1)}, u32[]{:S(2)}, u32[]{:S(2)}) %collective-permute-start.4) | collective-permute-done | bytes 393248 | tf_op jit(solution)/shard_map/ppermute | solution.py:517
  15.6 5.1 %collective-permute-start.6 = (f32[128,128]{1,0:T(8,128)S(1)}, f32[128,128]{1,0:T(8,128)S(1)}, u32[]{:S(2)}, u32[]{:S(2)}) collective-permute-start(f32[128,128]{1,0:T(8,128)S(1)} %get-tuple-element.27), channel_id=1, source_target_pairs={{0,15},{1,2},{2,1},{3,4},{4,3},{5,6},{6,5},{7,8},{8,7},{9,10},{10,... | collective-permute-start | bytes 196616 | tf_op jit(solution)/shard_map/ppermute | solution.py:522
  20.7 2.3 %prepare.1 = (f32[2,256,256]{2,1,0:T(8,128)S(1)}, bf16[8,256,256]{2,1,0:T(8,128)(2,1)S(1)}) custom-call(f32[256,256]{1,0:T(8,128)S(1)} %copy-done.5), custom_call_target="tpu_custom_call" | custom-call | flops 268435456 | bytes 4194304 | tf_op jit(solution)/shard_map/prepare/pallas_call | solution.py:261
  23.0 1.6 %collective-permute-start.3 = (f32[2,128,128]{2,1,0:T(8,128)S(1)}, f32[2,128,128]{2,1,0:T(8,128)S(1)}, u32[]{:S(2)}, u32[]{:S(2)}) collective-permute-start(f32[2,128,128]{2,1,0:T(8,128)S(1)} %corners.2), channel_id=1, source_target_pairs={{0,16},{16,0},{1,17},{17,1},{2,18},{18,2},{3,19},{19,3},{4,20},{20... | collective-permute-start | bytes 393224 | tf_op jit(solution)/shard_map/ppermute | solution.py:517
  24.7 5.5 %first.1 = (f32[4,2,256,256]{3,2,1,0:T(8,128)S(1)}, f32[4,2,256,256]{3,2,1,0:T(8,128)S(1)}) custom-call(s32[2,4]{1,0:T(2,128)S(1)} %bitcast.4, f32[2,2,384,384]{3,2,1,0:T(8,128)S(1)} %copy-done.1, f32[2,128,384]{2,1,0:T(8,128)S(1)} %collective-permute-done.4.rows_ref.rows, f32[2,384,128]{2,1,0:T(8,128)S(1)} %collective-permute-done.1.near, ...), custom_call_target="tpu_custom_call" | custom-call | flops 3221225472 | bytes 4194304 | tf_op jit(solution)/shard_map/first/pallas_call | solution.py:648
  30.2 6.8 %second.1 = (f32[4,2,256,256]{3,2,1,0:T(8,128)S(1)}, f32[2,5,512,128]{3,2,1,0:T(8,128)S(1)}, f32[512,128]{1,0:T(8,128)S(1)}, f32[512,128]{1,0:T(8,128)S(1)}) custom-call(s32[2,4]{1,0:T(2,128)S(1)} %bitcast.5, f32[2,2,384,384]{3,2,1,0:T(8,128)S(1)} %copy-done.1, f32[2,128,384]{2,1,0:T(8,128)S(1)} %collective-permute-done.rows, ...), custom_call_target="tpu_custom_call" | custom-call | flops 3221225472 | bytes 4194304 | tf_op jit(solution)/shard_map/second/pallas_call | solution.py:659
  37.0 4.4 %third.1 = (f32[4,2,256,256]{3,2,1,0:T(8,128)S(1)}, f32[256,256]{1,0:T(8,128)S(1)}, f32[256,256]{1,0:T(8,128)S(1)}) custom-call(f32[4,2,256,256]{3,2,1,0:T(8,128)S(1)} %get-tuple-element.31.u, f32[4,2,256,256]{3,2,1,0:T(8,128)S(1)} %get-tuple-element.32.w, f32[2,256,256]{2,1,0:T(8,128)S(1)} %get-tuple-element.28.prop, ...), custom_call_target="tpu_custom_call" | custom-call | flops 3221225472 | bytes 4194304 | tf_op jit(solution)/shard_map/third/pallas_call | solution.py:677
  41.5 1.5 %collective-permute-done.13.came = f32[256,256]{1,0:T(8,128)S(1)} collective-permute-done((f32[256,256]{1,0:T(8,128)S(1)}, f32[256,256]{1,0:T(8,128)S(1)}, u32[]{:S(2)}, u32[]{:S(2)}) %collective-permute-start.13) | collective-permute-done | bytes 262176 | tf_op jit(solution)/shard_map/ppermute | solution.py:580
  43.3 2.4 %collective-permute-start.11 = (f32[512,128]{1,0:T(8,128)S(1)}, f32[512,128]{1,0:T(8,128)S(1)}, u32[]{:S(2)}, u32[]{:S(2)}) collective-permute-start(f32[512,128]{1,0:T(8,128)S(1)} %get-tuple-element.39), channel_id=1, source_target_pairs={{0,15},{1,2},{2,1},{3,4},{4,3},{5,6},{6,5},{7,8},{8,7},{9,10},{10,... | collective-permute-start | bytes 786440 | tf_op jit(solution)/shard_map/ppermute | solution.py:522
  45.7 1.9 %spread.1 = (f32[2,5,512,128]{3,2,1,0:T(8,128)S(1)}, f32[512,128]{1,0:T(8,128)S(1)}, f32[512,128]{1,0:T(8,128)S(1)}) custom-call(s32[2,4]{1,0:T(2,128)S(1)} %bitcast.6, f32[4,2,256,256]{3,2,1,0:T(8,128)S(1)} %get-tuple-element.33.beta, f32[2,256,256]{2,1,0:T(8,128)S(1)} %copy-done.2), custom_call_target="tpu_custom_call" | custom-call | bytes 4194304 | tf_op jit(solution)/shard_map/spread/pallas_call | solution.py:687
  49.2 4.7 %collective-permute-start.8 = (f32[512,128]{1,0:T(8,128)S(1)}, f32[512,128]{1,0:T(8,128)S(1)}, u32[]{:S(2)}, u32[]{:S(2)}) collective-permute-start(f32[512,128]{1,0:T(8,128)S(1)} %get-tuple-element.36), channel_id=1, source_target_pairs={{0,15},{1,2},{2,1},{3,4},{4,3},{5,6},{6,5},{7,8},{8,7},{9,10},{10,... | collective-permute-start | bytes 786440 | tf_op jit(solution)/shard_map/ppermute | solution.py:522
  54.0 4.3 %collective-permute-done.16.came = f32[64,256]{1,0:T(8,128)S(1)} collective-permute-done((f32[64,256]{1,0:T(8,128)S(1)}, f32[64,256]{1,0:T(8,128)S(1)}, u32[]{:S(2)}, u32[]{:S(2)}) %collective-permute-start.16) | collective-permute-done | bytes 65568 | tf_op jit(solution)/shard_map/ppermute | solution.py:580
  58.3 1.4 %collective-permute-start.17 = (f32[64,256]{1,0:T(8,128)S(1)}, f32[64,256]{1,0:T(8,128)S(1)}, u32[]{:S(2)}, u32[]{:S(2)}) collective-permute-start(f32[64,256]{1,0:T(8,128)S(1)} %adding.4.mine), channel_id=1, source_target_pairs={{0,8},{1,9},{2,10},{3,11},{4,12},{5,13},{6,14},{7,15},{8,0},{9,1},... | collective-permute-start | bytes 196616 | tf_op jit(solution)/shard_map/ppermute | solution.py:580
  59.7 3.9 %collective-permute-done.17.came = f32[64,256]{1,0:T(8,128)S(1)} collective-permute-done((f32[64,256]{1,0:T(8,128)S(1)}, f32[64,256]{1,0:T(8,128)S(1)}, u32[]{:S(2)}, u32[]{:S(2)}) %collective-permute-start.17) | collective-permute-done | bytes 65568 | tf_op jit(solution)/shard_map/ppermute | solution.py:580
  63.8 1.2 %collective-permute-start.12 = (f32[2,128,384]{2,1,0:T(8,128)S(1)}, f32[2,128,384]{2,1,0:T(8,128)S(1)}, u32[]{:S(2)}, u32[]{:S(2)}) collective-permute-start(f32[2,128,384]{2,1,0:T(8,128)S(1)} %merge.3), channel_id=1, source_target_pairs={{0,16},{16,0},{1,17},{17,1},{2,18},{18,2},{3,19},{19,3},{4,20},{20... | collective-permute-start | bytes 1179656 | tf_op jit(solution)/shard_map/ppermute | solution.py:517
  66.1 1.8 %collective-permute-done.18.came = f32[64,256]{1,0:T(8,128)S(1)} collective-permute-done((f32[64,256]{1,0:T(8,128)S(1)}, f32[64,256]{1,0:T(8,128)S(1)}, u32[]{:S(2)}, u32[]{:S(2)}) %collective-permute-start.18) | collective-permute-done | bytes 65568 | tf_op jit(solution)/shard_map/ppermute | solution.py:580
  68.0 1.1 %collective-permute-start.19 = (f32[128,256]{1,0:T(8,128)S(1)}, f32[128,256]{1,0:T(8,128)S(1)}, u32[]{:S(2)}, u32[]{:S(2)}) collective-permute-start(f32[128,256]{1,0:T(8,128)S(1)} %joining.2.mine), channel_id=1, source_target_pairs={{0,2},{1,3},{2,0},{3,1},{4,6},{5,7},{6,4},{7,5},{8,10},{9,11},{10,... | collective-permute-start | bytes 393224 | tf_op jit(solution)/shard_map/ppermute | solution.py:580
  69.0 3.9 %collective-permute-done.19.came = f32[128,256]{1,0:T(8,128)S(1)} collective-permute-done((f32[128,256]{1,0:T(8,128)S(1)}, f32[128,256]{1,0:T(8,128)S(1)}, u32[]{:S(2)}, u32[]{:S(2)}) %collective-permute-start.19) | collective-permute-done | bytes 131104 | tf_op jit(solution)/shard_map/ppermute | solution.py:580
  73.1 2.8 %collective-permute-done.12.refs_7_ = f32[2,128,384]{2,1,0:T(8,128)S(1)} collective-permute-done((f32[2,128,384]{2,1,0:T(8,128)S(1)}, f32[2,128,384]{2,1,0:T(8,128)S(1)}, u32[]{:S(2)}, u32[]{:S(2)}) %collective-permute-start.12) | collective-permute-done | bytes 393248 | tf_op jit(solution)/shard_map/ppermute | solution.py:517
  75.9 4.4 %collective-permute-done.9.refs_3_ = f32[2,128,384]{2,1,0:T(8,128)S(1)} collective-permute-done((f32[2,128,384]{2,1,0:T(8,128)S(1)}, f32[2,128,384]{2,1,0:T(8,128)S(1)}, u32[]{:S(2)}, u32[]{:S(2)}) %collective-permute-start.9) | collective-permute-done | bytes 393248 | tf_op jit(solution)/shard_map/ppermute | solution.py:517
  80.3 1.9 %finish.1 = f32[2,2,384,384]{3,2,1,0:T(8,128)} custom-call(f32[2,5,512,128]{3,2,1,0:T(8,128)S(1)} %get-tuple-element.34.acc.refs_0_, f32[512,128]{1,0:T(8,128)S(1)} %collective-permute-done.7.near.refs_1_, f32[512,128]{1,0:T(8,128)S(1)} %collective-permute-done.8.far.refs_2_, f32[2,128,384]{2,1,0:T(8,128)S(1)} %collective-permute-done.9.refs_3_, ...), custom_call_target="tpu_custom_call" | custom-call | bytes 4194304 | tf_op jit(solution)/shard_map/finish/pallas_call | solution.py:707
  (51 shorter events, 5.4 us)
Async XLA Ops:
  2.3 13.0 %collective-permute-start.4 = (f32[2,128,384]{2,1,0:T(8,128)S(1)}, f32[2,128,384]{2,1,0:T(8,128)S(1)}, u32[]{:S(2)}, u32[]{:S(2)}) collective-permute-start(f32[2,128,384]{2,1,0:T(8,128)S(1)} %cut.5), channel_id=1, source_target_pairs={{0,16},{16,0},{1,17},{17,1},{2,18},{18,2},{3,19},{19,3},{4,20},{20... | collective-permute-start | bytes 1179656 | tf_op jit(solution)/shard_map/ppermute | solution.py:517
  5.7 17.3 %collective-permute-start.1 = (f32[2,384,128]{2,1,0:T(8,128)S(1)}, f32[2,384,128]{2,1,0:T(8,128)S(1)}, u32[]{:S(2)}, u32[]{:S(2)}) collective-permute-start(f32[2,384,128]{2,1,0:T(8,128)S(1)} %get-tuple-element.24), channel_id=1, source_target_pairs={{0,1},{1,0},{2,3},{3,2},{4,5},{5,4},{6,7},{7,6},{8,9},{9,8},{10,11... | collective-permute-start | bytes 1179656 | tf_op jit(solution)/shard_map/ppermute | solution.py:523
  5.8 18.9 %copy-start.1 = (f32[2,2,384,384]{3,2,1,0:T(8,128)S(1)}, f32[2,2,384,384]{3,2,1,0:T(8,128)}, u32[]{:S(2)}) copy-start(f32[2,2,384,384]{3,2,1,0:T(8,128)} %x.3) | copy-start | bytes 7077892
  5.8 18.9 %copy-start.2 = (f32[2,256,256]{2,1,0:T(8,128)S(1)}, f32[2,256,256]{2,1,0:T(8,128)}, u32[]{:S(2)}) copy-start(f32[2,256,256]{2,1,0:T(8,128)} %probe.3) | copy-start | bytes 1572868
  5.8 18.9 %copy-start.3 = (s32[4,1,2]{0,2,1:T(2,128)S(1)}, s32[4,1,2]{0,2,1:T(2,128)}, u32[]{:S(2)}) copy-start(s32[4,1,2]{0,2,1:T(2,128)} %param.6) | copy-start | bytes 100
  5.8 17.2 %collective-permute-start.2 = (f32[2,384,128]{2,1,0:T(8,128)S(1)}, f32[2,384,128]{2,1,0:T(8,128)S(1)}, u32[]{:S(2)}, u32[]{:S(2)}) collective-permute-start(f32[2,384,128]{2,1,0:T(8,128)S(1)} %get-tuple-element.25), channel_id=1, source_target_pairs={{0,15},{1,2},{2,1},{3,4},{4,3},{5,6},{6,5},{7,8},{8,7},{9,10},{10,... | collective-permute-start | bytes 1179656 | tf_op jit(solution)/shard_map/ppermute | solution.py:522
  10.4 19.7 %collective-permute-start = (f32[2,128,384]{2,1,0:T(8,128)S(1)}, f32[2,128,384]{2,1,0:T(8,128)S(1)}, u32[]{:S(2)}, u32[]{:S(2)}) collective-permute-start(f32[2,128,384]{2,1,0:T(8,128)S(1)} %cut.3), channel_id=1, source_target_pairs={{0,16},{16,0},{1,17},{17,1},{2,18},{18,2},{3,19},{19,3},{4,20},{20... | collective-permute-start | bytes 1179656 | tf_op jit(solution)/shard_map/ppermute | solution.py:517
  15.5 9.1 %collective-permute-start.5 = (f32[128,128]{1,0:T(8,128)S(1)}, f32[128,128]{1,0:T(8,128)S(1)}, u32[]{:S(2)}, u32[]{:S(2)}) collective-permute-start(f32[128,128]{1,0:T(8,128)S(1)} %get-tuple-element.26), channel_id=1, source_target_pairs={{0,1},{1,0},{2,3},{3,2},{4,5},{5,4},{6,7},{7,6},{8,9},{9,8},{10,11... | collective-permute-start | bytes 196616 | tf_op jit(solution)/shard_map/ppermute | solution.py:523
  15.6 9.1 %collective-permute-start.6 = (f32[128,128]{1,0:T(8,128)S(1)}, f32[128,128]{1,0:T(8,128)S(1)}, u32[]{:S(2)}, u32[]{:S(2)}) collective-permute-start(f32[128,128]{1,0:T(8,128)S(1)} %get-tuple-element.27), channel_id=1, source_target_pairs={{0,15},{1,2},{2,1},{3,4},{4,3},{5,6},{6,5},{7,8},{8,7},{9,10},{10,... | collective-permute-start | bytes 196616 | tf_op jit(solution)/shard_map/ppermute | solution.py:522
  23.0 7.1 %collective-permute-start.3 = (f32[2,128,128]{2,1,0:T(8,128)S(1)}, f32[2,128,128]{2,1,0:T(8,128)S(1)}, u32[]{:S(2)}, u32[]{:S(2)}) collective-permute-start(f32[2,128,128]{2,1,0:T(8,128)S(1)} %corners.2), channel_id=1, source_target_pairs={{0,16},{16,0},{1,17},{17,1},{2,18},{18,2},{3,19},{19,3},{4,20},{20... | collective-permute-start | bytes 393224 | tf_op jit(solution)/shard_map/ppermute | solution.py:517
  41.4 1.6 %collective-permute-start.13 = (f32[256,256]{1,0:T(8,128)S(1)}, f32[256,256]{1,0:T(8,128)S(1)}, u32[]{:S(2)}, u32[]{:S(2)}) collective-permute-start(f32[256,256]{1,0:T(8,128)S(1)} %get-tuple-element.41), channel_id=1, source_target_pairs={{0,1},{1,0},{2,3},{3,2},{4,5},{5,4},{6,7},{7,6},{8,9},{9,8},{10,11... | collective-permute-start | bytes 786440 | tf_op jit(solution)/shard_map/ppermute | solution.py:580
  43.0 5.6 %collective-permute-start.14 = (f32[128,256]{1,0:T(8,128)S(1)}, f32[128,256]{1,0:T(8,128)S(1)}, u32[]{:S(2)}, u32[]{:S(2)}) collective-permute-start(f32[128,256]{1,0:T(8,128)S(1)} %get-tuple-element.43), channel_id=1, source_target_pairs={{0,2},{1,3},{2,0},{3,1},{4,6},{5,7},{6,4},{7,5},{8,10},{9,11},{10,... | collective-permute-start | bytes 393224 | tf_op jit(solution)/shard_map/ppermute | solution.py:580
  43.1 20.6 %collective-permute-start.10 = (f32[512,128]{1,0:T(8,128)S(1)}, f32[512,128]{1,0:T(8,128)S(1)}, u32[]{:S(2)}, u32[]{:S(2)}) collective-permute-start(f32[512,128]{1,0:T(8,128)S(1)} %get-tuple-element.38), channel_id=1, source_target_pairs={{0,1},{1,0},{2,3},{3,2},{4,5},{5,4},{6,7},{7,6},{8,9},{9,8},{10,11... | collective-permute-start | bytes 786440 | tf_op jit(solution)/shard_map/ppermute | solution.py:523
  43.3 20.4 %collective-permute-start.11 = (f32[512,128]{1,0:T(8,128)S(1)}, f32[512,128]{1,0:T(8,128)S(1)}, u32[]{:S(2)}, u32[]{:S(2)}) collective-permute-start(f32[512,128]{1,0:T(8,128)S(1)} %get-tuple-element.39), channel_id=1, source_target_pairs={{0,15},{1,2},{2,1},{3,4},{4,3},{5,6},{6,5},{7,8},{8,7},{9,10},{10,... | collective-permute-start | bytes 786440 | tf_op jit(solution)/shard_map/ppermute | solution.py:522
  48.7 5.2 %collective-permute-start.15 = (f32[64,256]{1,0:T(8,128)S(1)}, f32[64,256]{1,0:T(8,128)S(1)}, u32[]{:S(2)}, u32[]{:S(2)}) collective-permute-start(f32[64,256]{1,0:T(8,128)S(1)} %get-tuple-element.45), channel_id=1, source_target_pairs={{0,4},{1,5},{2,6},{3,7},{4,0},{5,1},{6,2},{7,3},{8,12},{9,13},{10,... | collective-permute-start | bytes 196616 | tf_op jit(solution)/shard_map/ppermute | solution.py:580
  49.2 15.8 %collective-permute-start.7 = (f32[512,128]{1,0:T(8,128)S(1)}, f32[512,128]{1,0:T(8,128)S(1)}, u32[]{:S(2)}, u32[]{:S(2)}) collective-permute-start(f32[512,128]{1,0:T(8,128)S(1)} %get-tuple-element.35), channel_id=1, source_target_pairs={{0,1},{1,0},{2,3},{3,2},{4,5},{5,4},{6,7},{7,6},{8,9},{9,8},{10,11... | collective-permute-start | bytes 786440 | tf_op jit(solution)/shard_map/ppermute | solution.py:523
  49.2 15.8 %collective-permute-start.8 = (f32[512,128]{1,0:T(8,128)S(1)}, f32[512,128]{1,0:T(8,128)S(1)}, u32[]{:S(2)}, u32[]{:S(2)}) collective-permute-start(f32[512,128]{1,0:T(8,128)S(1)} %get-tuple-element.36), channel_id=1, source_target_pairs={{0,15},{1,2},{2,1},{3,4},{4,3},{5,6},{6,5},{7,8},{8,7},{9,10},{10,... | collective-permute-start | bytes 786440 | tf_op jit(solution)/shard_map/ppermute | solution.py:522
  53.9 4.3 %collective-permute-start.16 = (f32[64,256]{1,0:T(8,128)S(1)}, f32[64,256]{1,0:T(8,128)S(1)}, u32[]{:S(2)}, u32[]{:S(2)}) collective-permute-start(f32[64,256]{1,0:T(8,128)S(1)} %adding.3.mine), channel_id=1, source_target_pairs={{0,16},{16,0},{1,17},{17,1},{2,18},{18,2},{3,19},{19,3},{4,20},{20... | collective-permute-start | bytes 196616 | tf_op jit(solution)/shard_map/ppermute | solution.py:580
  58.3 5.3 %collective-permute-start.17 = (f32[64,256]{1,0:T(8,128)S(1)}, f32[64,256]{1,0:T(8,128)S(1)}, u32[]{:S(2)}, u32[]{:S(2)}) collective-permute-start(f32[64,256]{1,0:T(8,128)S(1)} %adding.4.mine), channel_id=1, source_target_pairs={{0,8},{1,9},{2,10},{3,11},{4,12},{5,13},{6,14},{7,15},{8,0},{9,1},... | collective-permute-start | bytes 196616 | tf_op jit(solution)/shard_map/ppermute | solution.py:580
  63.6 4.3 %collective-permute-start.18 = (f32[64,256]{1,0:T(8,128)S(1)}, f32[64,256]{1,0:T(8,128)S(1)}, u32[]{:S(2)}, u32[]{:S(2)}) collective-permute-start(f32[64,256]{1,0:T(8,128)S(1)} %adding.5.mine), channel_id=1, source_target_pairs={{0,4},{1,5},{2,6},{3,7},{4,0},{5,1},{6,2},{7,3},{8,12},{9,13},{10,... | collective-permute-start | bytes 196616 | tf_op jit(solution)/shard_map/ppermute | solution.py:580
  63.8 12.1 %collective-permute-start.12 = (f32[2,128,384]{2,1,0:T(8,128)S(1)}, f32[2,128,384]{2,1,0:T(8,128)S(1)}, u32[]{:S(2)}, u32[]{:S(2)}) collective-permute-start(f32[2,128,384]{2,1,0:T(8,128)S(1)} %merge.3), channel_id=1, source_target_pairs={{0,16},{16,0},{1,17},{17,1},{2,18},{18,2},{3,19},{19,3},{4,20},{20... | collective-permute-start | bytes 1179656 | tf_op jit(solution)/shard_map/ppermute | solution.py:517
  65.1 15.2 %collective-permute-start.9 = (f32[2,128,384]{2,1,0:T(8,128)S(1)}, f32[2,128,384]{2,1,0:T(8,128)S(1)}, u32[]{:S(2)}, u32[]{:S(2)}) collective-permute-start(f32[2,128,384]{2,1,0:T(8,128)S(1)} %merge.2), channel_id=1, source_target_pairs={{0,16},{16,0},{1,17},{17,1},{2,18},{18,2},{3,19},{19,3},{4,20},{20... | collective-permute-start | bytes 1179656 | tf_op jit(solution)/shard_map/ppermute | solution.py:517
  68.0 5.0 %collective-permute-start.19 = (f32[128,256]{1,0:T(8,128)S(1)}, f32[128,256]{1,0:T(8,128)S(1)}, u32[]{:S(2)}, u32[]{:S(2)}) collective-permute-start(f32[128,256]{1,0:T(8,128)S(1)} %joining.2.mine), channel_id=1, source_target_pairs={{0,2},{1,3},{2,0},{3,1},{4,6},{5,7},{6,4},{7,5},{8,10},{9,11},{10,... | collective-permute-start | bytes 393224 | tf_op jit(solution)/shard_map/ppermute | solution.py:580
  73.0 9.2 %collective-permute-start.20 = (f32[256,256]{1,0:T(8,128)S(1)}, f32[256,256]{1,0:T(8,128)S(1)}, u32[]{:S(2)}, u32[]{:S(2)}) collective-permute-start(f32[256,256]{1,0:T(8,128)S(1)} %joining.3.mine), channel_id=1, source_target_pairs={{0,1},{1,0},{2,3},{3,2},{4,5},{5,4},{6,7},{7,6},{8,9},{9,8},{10,11... | collective-permute-start | bytes 786440 | tf_op jit(solution)/shard_map/ppermute | solution.py:580
  (3 other events, 25.6 us)

commit v5 on v4

--- a/solution.py
+++ b/solution.py
@@ -245,28 +245,41 @@
                 t_out[(2 * which, *at)], t_out[(2 * which + 1, *at)] = split(part)
 
 
-def prepare_kernel(phase_ref, prop_ref, t_out, turned):
+def prepare_kernel(phase_ref, amp, prop_ref, t_out, level, turned, order):
     write_tables(t_out)
     x = phase_ref[...]
     choose = chooser(x.shape[0])
+    order[...] = choose
     first, rest = split(x)
     third = (x - first.astype(F32) - rest.astype(F32)).astype(BF16)
     phase = unmixed(dot(first, choose) + dot(rest, choose) + dot(third, choose), turned)
     prop_ref[0] = jnp.cos(phase)
     prop_ref[1] = jnp.sin(phase)
 
-
-def prepare(phase):
+    @pl.loop(0, amp.shape[0])
+    def _(p):
+        top, low = split(amp[p])
+        level[p] = unmixed(dot(top, order[...]) + dot(low, order[...]), turned)
+
+
+def prepare(phase, amplitudes):
     size = phase.shape[0]
     return call(
         prepare_kernel,
-        (shaped(2, size, size), jax.ShapeDtypeStruct((8, size, size), BF16)),
+        (
+            shaped(2, size, size),
+            jax.ShapeDtypeStruct((8, size, size), BF16),
+            shaped(*amplitudes.shape),
+        ),
         flops=1 << 28,
-        in_specs=[VMEM],
-        out_specs=(VMEM, VMEM),
-        scratch_shapes=[pltpu.VMEM((size // LANES, size, LANES), F32)],
+        in_specs=[VMEM, VMEM],
+        out_specs=(VMEM,) * 3,
+        scratch_shapes=[
+            pltpu.VMEM((size // LANES, size, LANES), F32),
+            pltpu.VMEM((size, size), BF16),
+        ],
         name="prepare",
-    )(phase)
+    )(phase, amplitudes)
 
 
 def assemble(ext, tile, rows, near, far, corner_near, corner_far, odd):
@@ -359,49 +372,18 @@
         stage.inverse(change, sink)
 
 
-def leave(acc, near, far, odd):
-    last = acc.shape[1] - 1
-    near[...], far[...] = swapped(
-        odd, low_rim(acc[0, last], acc[1, last]), high_rim(acc[0, 0], acc[1, 0])
-    )
-
-
 def second_kernel(
-    off,
-    x,
-    rows,
-    near,
-    far,
-    corners,
-    psi,
-    amp,
-    t,
-    u_out,
-    acc,
-    near_out,
-    far_out,
-    ext,
-    kept,
-    choose,
-    turned,
-    level,
-    *buffers,
+    off, x, rows, near, far, corners, psi, level, t, u_out, beta_out, ext, kept, *buffers
 ):
     stage = Stage(t, *buffers)
     count, _, size, _ = psi.shape
     many = len(stage.group)
     h = stage.half
-    odd = on_odd()
-    assemble(ext, x.at[1], rows, near.at[1], far.at[1], corners.at[0], corners.at[1], odd)
-    acc[...] = jnp.zeros_like(acc)
-    choose[...] = chooser(size)
+    assemble(ext, x.at[1], rows, near.at[1], far.at[1], corners.at[0], corners.at[1], on_odd())
 
     @pl.loop(0, count // many)
     def _(i):
         first = i * many
-        for q in stage.group:
-            top, rest = split(amp[first + q])
-            level[q] = unmixed(dot(top, choose[...]) + dot(rest, choose[...]), turned.at[q])
 
         def source(q):
             w = [window(ext, off, first + q, c, size) for c in (0, 1)]
@@ -410,19 +392,16 @@
 
         def change(q, e, re, im):
             magnitude = jnp.sqrt(re * re + im * im)
-            keep = 1.0 - level[q, e * h : (e + 1) * h] / jnp.maximum(magnitude, 0.5)
+            keep = 1.0 - level[first + q, e * h : (e + 1) * h] / jnp.maximum(magnitude, 0.5)
             return re * keep, im * keep
 
         def sink(q, re, im):
             p = first + q
             u_out[p, 0], u_out[p, 1] = conj_times(kept[q, 0], kept[q, 1], re, im)
-            for c, g in enumerate(conj_times(psi[p, 0], psi[p, 1], re, im)):
-                add_window(acc, off, p, c, g)
+            beta_out[p, 0], beta_out[p, 1] = re, im
 
         stage.forward(source)
         stage.inverse(change, sink)
-
-    leave(acc, near_out, far_out, odd)
 
 
 def third_kernel(factor, u, w, prop, t, beta_out, mine_out, other_out, acc, *buffers):
@@ -456,15 +435,19 @@
     other_out[...] = acc[1 - upper(0)] * factor
 
 
-def spread_kernel(off, beta, probe, acc, near_out, far_out):
+def spread_kernel(off, beta, wave, acc, near, far):
     acc[...] = jnp.zeros_like(acc)
 
     @pl.loop(0, beta.shape[0])
     def _(p):
-        for c, g in enumerate(conj_times(probe[0], probe[1], beta[p, 0], beta[p, 1])):
+        psi = wave.at[p] if len(wave.shape) == 4 else wave
+        for c, g in enumerate(conj_times(psi[0], psi[1], beta[p, 0], beta[p, 1])):
             add_window(acc, off, p, c, g)
 
-    leave(acc, near_out, far_out, on_odd())
+    last = acc.shape[1] - 1
+    near[...], far[...] = swapped(
+        on_odd(), low_rim(acc[0, last], acc[1, last]), high_rim(acc[0, 0], acc[1, 0])
+    )
 
 
 def rim_parts(near, far, odd, c):
@@ -491,25 +474,36 @@
                 strip_ref[c, here, j * LANES : (j + 1) * LANES] = value
 
 
-def finish_kernel(*refs):
+def finish_kernel(acc, near, far, strip, *refs):
     out_ref = refs[-1]
     size = out_ref.shape[2]
     tiles = size // LANES
     middle = pl.ds(HALO, size)
-    for s in range(out_ref.shape[0]):
-        acc, near, far, strip = refs[4 * s : 4 * s + 4]
-        for c in range(2):
-            h, w = rim_parts(near[middle], far[middle], on_odd(), c)
-            for j in range(tiles):
-                value = acc[c, j + 1, middle]
-                if j == 0:
-                    value += w
-                if j == tiles - 1:
-                    value += h
-                across = slice(j * LANES, (j + 1) * LANES)
-                out_ref[s, c, HALO:-HALO, across] = value[HALO:-HALO]
-                out_ref[s, c, :HALO, across] = value[:HALO] + strip[c, HALO:, across]
-                out_ref[s, c, -HALO:, across] = value[-HALO:] + strip[c, :HALO, across]
+    for c in range(2):
+        h, w = rim_parts(near[middle], far[middle], on_odd(), c)
+        for j in range(tiles):
+            value = acc[c, j + 1, middle]
+            if j == 0:
+                value += w
+            if j == tiles - 1:
+                value += h
+            across = slice(j * LANES, (j + 1) * LANES)
+            out_ref[0, c, HALO:-HALO, across] = value[HALO:-HALO]
+            out_ref[0, c, :HALO, across] = value[:HALO] + strip[c, HALO:, across]
+            out_ref[0, c, -HALO:, across] = value[-HALO:] + strip[c, :HALO, across]
+
+
+def finish(s, shape, arrays, before=()):
+    return call(
+        finish_kernel,
+        shaped(*shape),
+        room=16,
+        grid=(1,),
+        in_specs=[VMEM] * 4 + [pl.BlockSpec(memory_space=pl.ANY)] * len(before),
+        out_specs=pl.BlockSpec((1, *shape[1:]), lambda i: (s, 0, 0, 0)),
+        input_output_aliases={4: 0} if before else {},
+        name="finish",
+    )(*arrays, *before)
 
 
 def shift(x, axis, by):
@@ -633,7 +627,7 @@
     edges1 = cut_rows(object_field, 1)
     rows0 = to_both(edges0, "row", HALO, 1)
     near, far = exchange(near, far)
-    prop, t = prepare(phase)
+    prop, t, level = prepare(phase, amplitudes[:, 0])
     rows1 = to_both(edges1, "row", HALO, 1)
     corner_near, corner_far = row_corners(rows0)
     corner_near, corner_far = exchange(corner_near, corner_far)
@@ -655,25 +649,16 @@
         scratch_shapes=[ext, *buffers],
         name="first",
     )(off, object_field, rows0, near, far, corner_near, corner_far, probe, prop, t)
-    left_over = (shaped(*ext.shape), shaped(span, LANES), shaped(span, LANES))
-    u, sum1, near1, far1 = call(
+    u, beta1 = call(
         second_kernel,
-        (field, *left_over),
+        (field, field),
         flops=flops,
         room=ROOM,
         in_specs=[SMEM] + [VMEM] * 8,
-        out_specs=(VMEM,) * 4,
-        scratch_shapes=[
-            ext,
-            pltpu.VMEM((many, 2, size, size), F32),
-            pltpu.VMEM((size, size), BF16),
-            pltpu.VMEM((many, size // LANES, size, LANES), F32),
-            pltpu.VMEM((many, size, size), F32),
-            *buffers,
-        ],
+        out_specs=(VMEM,) * 2,
+        scratch_shapes=[ext, pltpu.VMEM((many, 2, size, size), F32), *buffers],
         name="second",
-    )(off, object_field, rows1, near, far, corners1, psi, amplitudes[:, 0], t)
-    near1, far1 = exchange(near1, far1)
+    )(off, object_field, rows1, near, far, corners1, psi, level, t)
     beta, mine, other = call(
         functools.partial(third_kernel, factor),
         (field, shaped(size, size), shaped(size, size)),
@@ -684,14 +669,20 @@
         scratch_shapes=[pltpu.VMEM((2, size, size), F32), *buffers],
         name="third",
     )(u, w0, prop, t)
-    sum0, near0, far0 = call(
-        spread_kernel,
-        left_over,
-        room=ROOM,
-        in_specs=[SMEM] + [VMEM] * 2,
-        out_specs=(VMEM,) * 3,
-        name="spread",
-    )(off, beta, probe)
+
+    def spread(beta, wave):
+        return call(
+            spread_kernel,
+            (shaped(*ext.shape), shaped(span, LANES), shaped(span, LANES)),
+            room=ROOM,
+            in_specs=[SMEM] + [VMEM] * 2,
+            out_specs=(VMEM,) * 3,
+            name="spread",
+        )(off, beta, wave)
+
+    sum1, near1, far1 = spread(beta1, psi)
+    near1, far1 = exchange(near1, far1)
+    sum0, near0, far0 = spread(beta, probe)
     near0, far0 = exchange(near0, far0)
     merge = call(
         merge_kernel,
@@ -704,14 +695,8 @@
     back1 = to_both(strip1, "row", HALO, -1)
     strip0 = merge(sum0, near0, far0)
     back0 = to_both(strip0, "row", HALO, -1)
-    grad = call(
-        finish_kernel,
-        shaped(2, 2, tile, tile),
-        room=16,
-        in_specs=[VMEM] * 8,
-        out_specs=VMEM,
-        name="finish",
-    )(sum0, near0, far0, back0, sum1, near1, far1, back1)
+    grad = finish(1, object_field.shape, (sum1, near1, far1, back1))
+    grad = finish(0, object_field.shape, (sum0, near0, far0, back0), (grad,))
     return grad, total(mine, other)
 
 

time: 83.3 us -> 85.6 us (1.028); the launches traced: 83.2 us -> 84.1 us
  starting transfers between devices: 28 us -> 23.1 us
  waiting for transfers between devices: 28 us -> 31.5 us
  Pallas kernels: 24.4 us -> 26.7 us
    ppermute x8, waiting for transfers between devices: 16.4 us -> 21.9 us  [swap(): return lax.ppermute(y, axis, [(i, i ^ bit) for i in range(sizes[axis])])]
    ppermute x4, starting transfers between devices: 16.8 us -> 12.8 us  [exchange(): lax.ppermute(far, 'col', [(i, (i + i % 2 * 2 - 1) % count) for i in range...]
    ppermute x5, waiting for transfers between devices: 11.6 us -> 9.5 us  [shift(): return lax.ppermute(x, axis, [(i, (i + by) % count) for i in range(count)])]
    pallas_call x3 -> x5, Pallas kernels: 10.7 us -> 12.1 us  [the longest x1 5.65 us: local(): call(second_kernel, (field, field), flops=flops, room=ROOM, in_specs=[SME...]
    pallas_call x1, Pallas kernels: 2.3 us -> 3.49 us  [prepare(): call(prepare_kernel, (shaped(2, size, size), jax.ShapeDtypeStruct((8, siz...]
  transfers between devices with their start and end apart: 21 -> 21, of which waited for: 9 -> 8; matrix products, arithmetic and copies ran while one was open for 0% -> 0% of each run, Pallas kernels for 15% -> 19%
where the time goes in v5:
time: 85.6 us; the launch traced here: 84.1 us
  waiting for transfers between devices  31.5 us (37%)
  Pallas kernels  26.7 us (31%)
  starting transfers between devices  23.1 us (27%)
  local copies, waits for them, and re-layouts  1.69 us (2%)
  between operations  1.1 us (1%)
    ppermute x8, waiting for transfers between devices, swap(): return lax.ppermute(y, axis, [(i, i ^ bit) for i in range(sizes[axis])])  21.9 us
    ppermute x4, starting transfers between devices, exchange(): lax.ppermute(far, 'col', [(i, (i + i % 2 * 2 - 1) % count) for i in range...  12.8 us
    ppermute x5, waiting for transfers between devices, shift(): return lax.ppermute(x, axis, [(i, (i + by) % count) for i in range(count)])  9.5 us
    ppermute x5, starting transfers between devices, shift(): return lax.ppermute(x, axis, [(i, (i + by) % count) for i in range(count)])  7.37 us
    pallas_call x1, Pallas kernels, local(): call(second_kernel, (field, field), flops=flops, room=ROOM, in_specs=[SME...  5.65 us
    pallas_call x1, Pallas kernels, local(): call(first_kernel, (field, field), flops=flops, room=ROOM, in_specs=[SMEM...  5.3 us
    pallas_call x1, Pallas kernels, local(): call(functools.partial(third_kernel, factor), (field, shaped(size, size),...  4.28 us
    pallas_call x2, Pallas kernels, spread(): call(spread_kernel, (shaped(*ext.shape), shaped(span, LANES), shaped(span...  3.86 us
  transfers between devices with their start and end apart: 21, of which 8 were waited for; matrix products, arithmetic and copies ran while one was open for 0% of the time, Pallas kernels for 19%

profile of v5, /device:TPU:0, one launch (start us, length us, event | category | flops | bytes accessed | tf_op | source)
XLA Modules:
  0.0 84.1 jit_solution(11133390477739356228)
XLA Ops:
  0.6 1.7 %copy-done = f32[2,2,384,384]{3,2,1,0:T(8,128)S(1)} copy-done((f32[2,2,384,384]{3,2,1,0:T(8,128)S(1)}, f32[2,2,384,384]{3,2,1,0:T(8,128)}, u32[]{:S(2)}) %copy-start) | copy-done | bytes 2359320
  2.4 3.1 %collective-permute-start.4 = (f32[2,128,384]{2,1,0:T(8,128)S(1)}, f32[2,128,384]{2,1,0:T(8,128)S(1)}, u32[]{:S(2)}, u32[]{:S(2)}) collective-permute-start(f32[2,128,384]{2,1,0:T(8,128)S(1)} %cut.5), channel_id=1, source_target_pairs={{0,16},{16,0},{1,17},{17,1},{2,18},{18,2},{3,19},{19,3},{4,20},{20... | collective-permute-start | bytes 1179656 | tf_op jit(solution)/shard_map/ppermute | solution.py:511
  5.8 4.6 %collective-permute-start.2 = (f32[2,384,128]{2,1,0:T(8,128)S(1)}, f32[2,384,128]{2,1,0:T(8,128)S(1)}, u32[]{:S(2)}, u32[]{:S(2)}) collective-permute-start(f32[2,384,128]{2,1,0:T(8,128)S(1)} %get-tuple-element.27), channel_id=1, source_target_pairs={{0,15},{1,2},{2,1},{3,4},{4,3},{5,6},{6,5},{7,8},{8,7},{9,10},{10,... | collective-permute-start | bytes 1179656 | tf_op jit(solution)/shard_map/ppermute | solution.py:516
  11.0 4.4 %collective-permute-done.4.rows_ref.rows = f32[2,128,384]{2,1,0:T(8,128)S(1)} collective-permute-done((f32[2,128,384]{2,1,0:T(8,128)S(1)}, f32[2,128,384]{2,1,0:T(8,128)S(1)}, u32[]{:S(2)}, u32[]{:S(2)}) %collective-permute-start.4) | collective-permute-done | bytes 393248 | tf_op jit(solution)/shard_map/ppermute | solution.py:511
  15.6 5.1 %collective-permute-start.6 = (f32[128,128]{1,0:T(8,128)S(1)}, f32[128,128]{1,0:T(8,128)S(1)}, u32[]{:S(2)}, u32[]{:S(2)}) collective-permute-start(f32[128,128]{1,0:T(8,128)S(1)} %get-tuple-element.29), channel_id=1, source_target_pairs={{0,15},{1,2},{2,1},{3,4},{4,3},{5,6},{6,5},{7,8},{8,7},{9,10},{10,... | collective-permute-start | bytes 196616 | tf_op jit(solution)/shard_map/ppermute | solution.py:516
  20.7 3.5 %prepare.1 = (f32[2,256,256]{2,1,0:T(8,128)S(1)}, bf16[8,256,256]{2,1,0:T(8,128)(2,1)S(1)}, f32[4,256,256]{2,1,0:T(8,128)S(1)}) custom-call(f32[256,256]{1,0:T(8,128)S(1)} %copy-done.4, f32[4,256,256]{2,1,0:T(8,128)S(1)} %bitcast.4), custom_call_target="tpu_custom_call" | custom-call | flops 268435456 | bytes 4194304 | tf_op jit(solution)/shard_map/prepare/pallas_call | solution.py:267
  24.2 1.6 %collective-permute-start.3 = (f32[2,128,128]{2,1,0:T(8,128)S(1)}, f32[2,128,128]{2,1,0:T(8,128)S(1)}, u32[]{:S(2)}, u32[]{:S(2)}) collective-permute-start(f32[2,128,128]{2,1,0:T(8,128)S(1)} %corners.2), channel_id=1, source_target_pairs={{0,16},{16,0},{1,17},{17,1},{2,18},{18,2},{3,19},{19,3},{4,20},{20... | collective-permute-start | bytes 393224 | tf_op jit(solution)/shard_map/ppermute | solution.py:511
  25.9 5.3 %first.1 = (f32[4,2,256,256]{3,2,1,0:T(8,128)S(1)}, f32[4,2,256,256]{3,2,1,0:T(8,128)S(1)}) custom-call(s32[2,4]{1,0:T(2,128)S(1)} %bitcast.5, f32[2,2,384,384]{3,2,1,0:T(8,128)S(1)} %copy-done.1, f32[2,128,384]{2,1,0:T(8,128)S(1)} %collective-permute-done.4.rows_ref.rows, f32[2,384,128]{2,1,0:T(8,128)S(1)} %collective-permute-done.1.near, ...), custom_call_target="tpu_custom_call" | custom-call | flops 3221225472 | bytes 4194304 | tf_op jit(solution)/shard_map/first/pallas_call | solution.py:642
  31.2 5.7 %second.1 = (f32[4,2,256,256]{3,2,1,0:T(8,128)S(1)}, f32[4,2,256,256]{3,2,1,0:T(8,128)S(1)}) custom-call(s32[2,4]{1,0:T(2,128)S(1)} %bitcast.6, f32[2,2,384,384]{3,2,1,0:T(8,128)S(1)} %copy-done.1, f32[2,128,384]{2,1,0:T(8,128)S(1)} %collective-permute-done.rows, f32[2,384,128]{2,1,0:T(8,128)S(1)} %collective-permute-done.1.near, ...), custom_call_target="tpu_custom_call" | custom-call | flops 3221225472 | bytes 4194304 | tf_op jit(solution)/shard_map/second/pallas_call | solution.py:652
  36.8 4.3 %third.1 = (f32[4,2,256,256]{3,2,1,0:T(8,128)S(1)}, f32[256,256]{1,0:T(8,128)S(1)}, f32[256,256]{1,0:T(8,128)S(1)}) custom-call(f32[4,2,256,256]{3,2,1,0:T(8,128)S(1)} %get-tuple-element.34.u, f32[4,2,256,256]{3,2,1,0:T(8,128)S(1)} %get-tuple-element.35.w, f32[2,256,256]{2,1,0:T(8,128)S(1)} %get-tuple-element.30.prop, ...), custom_call_target="tpu_custom_call" | custom-call | flops 3221225472 | bytes 4194304 | tf_op jit(solution)/shard_map/third/pallas_call | solution.py:662
  41.2 1.5 %collective-permute-done.13.came = f32[256,256]{1,0:T(8,128)S(1)} collective-permute-done((f32[256,256]{1,0:T(8,128)S(1)}, f32[256,256]{1,0:T(8,128)S(1)}, u32[]{:S(2)}, u32[]{:S(2)}) %collective-permute-start.13) | collective-permute-done | bytes 262176 | tf_op jit(solution)/shard_map/ppermute | solution.py:574
  42.8 1.9 %spread.2 = (f32[2,5,512,128]{3,2,1,0:T(8,128)S(1)}, f32[512,128]{1,0:T(8,128)S(1)}, f32[512,128]{1,0:T(8,128)S(1)}) custom-call(s32[2,4]{1,0:T(2,128)S(1)} %bitcast.7, f32[4,2,256,256]{3,2,1,0:T(8,128)S(1)} %get-tuple-element.36.beta, f32[2,256,256]{2,1,0:T(8,128)S(1)} %copy-done.3), custom_call_target="tpu_custom_call" | custom-call | bytes 4194304 | tf_op jit(solution)/shard_map/spread/pallas_call | solution.py:674
  44.8 1.9 %spread.3 = (f32[2,5,512,128]{3,2,1,0:T(8,128)S(1)}, f32[512,128]{1,0:T(8,128)S(1)}, f32[512,128]{1,0:T(8,128)S(1)}) custom-call(s32[2,4]{1,0:T(2,128)S(1)} %bitcast.8, f32[4,2,256,256]{3,2,1,0:T(8,128)S(1)} %get-tuple-element.40.beta, f32[4,2,256,256]{3,2,1,0:T(8,128)S(1)} %get-tuple-element.32.psi.wave), custom_call_target="tpu_custom_call" | custom-call | bytes 4194304 | tf_op jit(solution)/shard_map/spread/pallas_call | solution.py:674
  46.9 1.9 %collective-permute-start.8 = (f32[512,128]{1,0:T(8,128)S(1)}, f32[512,128]{1,0:T(8,128)S(1)}, u32[]{:S(2)}, u32[]{:S(2)}) collective-permute-start(f32[512,128]{1,0:T(8,128)S(1)} %get-tuple-element.39), channel_id=1, source_target_pairs={{0,15},{1,2},{2,1},{3,4},{4,3},{5,6},{6,5},{7,8},{8,7},{9,10},{10,... | collective-permute-start | bytes 786440 | tf_op jit(solution)/shard_map/ppermute | solution.py:516
  48.8 1.6 %collective-permute-start.15 = (f32[64,256]{1,0:T(8,128)S(1)}, f32[64,256]{1,0:T(8,128)S(1)}, u32[]{:S(2)}, u32[]{:S(2)}) collective-permute-start(f32[64,256]{1,0:T(8,128)S(1)} %get-tuple-element.49), channel_id=1, source_target_pairs={{0,4},{1,5},{2,6},{3,7},{4,0},{5,1},{6,2},{7,3},{8,12},{9,13},{10,... | collective-permute-start | bytes 196616 | tf_op jit(solution)/shard_map/ppermute | solution.py:574
  51.6 4.3 %collective-permute-done.15.came = f32[64,256]{1,0:T(8,128)S(1)} collective-permute-done((f32[64,256]{1,0:T(8,128)S(1)}, f32[64,256]{1,0:T(8,128)S(1)}, u32[]{:S(2)}, u32[]{:S(2)}) %collective-permute-start.15) | collective-permute-done | bytes 65568 | tf_op jit(solution)/shard_map/ppermute | solution.py:574
  56.5 3.8 %collective-permute-done.16.came = f32[64,256]{1,0:T(8,128)S(1)} collective-permute-done((f32[64,256]{1,0:T(8,128)S(1)}, f32[64,256]{1,0:T(8,128)S(1)}, u32[]{:S(2)}, u32[]{:S(2)}) %collective-permute-start.16) | collective-permute-done | bytes 65568 | tf_op jit(solution)/shard_map/ppermute | solution.py:574
  60.4 5.5 %collective-permute-done.17.came = f32[64,256]{1,0:T(8,128)S(1)} collective-permute-done((f32[64,256]{1,0:T(8,128)S(1)}, f32[64,256]{1,0:T(8,128)S(1)}, u32[]{:S(2)}, u32[]{:S(2)}) %collective-permute-start.17) | collective-permute-done | bytes 65568 | tf_op jit(solution)/shard_map/ppermute | solution.py:574
  66.9 1.5 %collective-permute-start.12 = (f32[2,128,384]{2,1,0:T(8,128)S(1)}, f32[2,128,384]{2,1,0:T(8,128)S(1)}, u32[]{:S(2)}, u32[]{:S(2)}) collective-permute-start(f32[2,128,384]{2,1,0:T(8,128)S(1)} %merge.3), channel_id=1, source_target_pairs={{0,16},{16,0},{1,17},{17,1},{2,18},{18,2},{3,19},{19,3},{4,20},{20... | collective-permute-start | bytes 1179656 | tf_op jit(solution)/shard_map/ppermute | solution.py:511
  68.4 1.8 %collective-permute-done.18.came = f32[64,256]{1,0:T(8,128)S(1)} collective-permute-done((f32[64,256]{1,0:T(8,128)S(1)}, f32[64,256]{1,0:T(8,128)S(1)}, u32[]{:S(2)}, u32[]{:S(2)}) %collective-permute-start.18) | collective-permute-done | bytes 65568 | tf_op jit(solution)/shard_map/ppermute | solution.py:574
  70.3 5.0 %collective-permute-done.19.came = f32[128,256]{1,0:T(8,128)S(1)} collective-permute-done((f32[128,256]{1,0:T(8,128)S(1)}, f32[128,256]{1,0:T(8,128)S(1)}, u32[]{:S(2)}, u32[]{:S(2)}) %collective-permute-start.19) | collective-permute-done | bytes 131104 | tf_op jit(solution)/shard_map/ppermute | solution.py:574
  75.4 5.1 %collective-permute-done.12.strip = f32[2,128,384]{2,1,0:T(8,128)S(1)} collective-permute-done((f32[2,128,384]{2,1,0:T(8,128)S(1)}, f32[2,128,384]{2,1,0:T(8,128)S(1)}, u32[]{:S(2)}, u32[]{:S(2)}) %collective-permute-start.12) | collective-permute-done | bytes 393248 | tf_op jit(solution)/shard_map/ppermute | solution.py:511
  80.5 1.3 %finish.2.refs_0_ = f32[2,2,384,384]{3,2,1,0:T(8,128)} custom-call(f32[2,5,512,128]{3,2,1,0:T(8,128)S(1)} %get-tuple-element.41.acc, f32[512,128]{1,0:T(8,128)S(1)} %collective-permute-done.10.near, f32[512,128]{1,0:T(8,128)S(1)} %collective-permute-done.11.far, f32[2,128,384]{2,1,0:T(8,128)S(1)} %collective-permute-done.12.strip), custom_call_target="tpu_custom_call" | custom-call | bytes 4194304 | tf_op jit(solution)/shard_map/finish/pallas_call | solution.py:497
  81.8 1.3 %finish.3 = f32[2,2,384,384]{3,2,1,0:T(8,128)} custom-call(f32[2,5,512,128]{3,2,1,0:T(8,128)S(1)} %get-tuple-element.37.acc, f32[512,128]{1,0:T(8,128)S(1)} %collective-permute-done.7.near, f32[512,128]{1,0:T(8,128)S(1)} %collective-permute-done.8.far, f32[2,128,384]{2,1,0:T(8,128)S(1)} %collective-permute-done.9.strip, ...), custom_call_target="tpu_custom_call", output_to_operand_aliasing={{}: (4, {})} | custom-call | bytes 4194304 | tf_op jit(solution)/shard_map/finish/pallas_call | solution.py:497
  (53 shorter events, 5.3 us)
Async XLA Ops:
  2.4 13.0 %collective-permute-start.4 = (f32[2,128,384]{2,1,0:T(8,128)S(1)}, f32[2,128,384]{2,1,0:T(8,128)S(1)}, u32[]{:S(2)}, u32[]{:S(2)}) collective-permute-start(f32[2,128,384]{2,1,0:T(8,128)S(1)} %cut.5), channel_id=1, source_target_pairs={{0,16},{16,0},{1,17},{17,1},{2,18},{18,2},{3,19},{19,3},{4,20},{20... | collective-permute-start | bytes 1179656 | tf_op jit(solution)/shard_map/ppermute | solution.py:511
  5.7 18.5 %collective-permute-start.1 = (f32[2,384,128]{2,1,0:T(8,128)S(1)}, f32[2,384,128]{2,1,0:T(8,128)S(1)}, u32[]{:S(2)}, u32[]{:S(2)}) collective-permute-start(f32[2,384,128]{2,1,0:T(8,128)S(1)} %get-tuple-element.26), channel_id=1, source_target_pairs={{0,1},{1,0},{2,3},{3,2},{4,5},{5,4},{6,7},{7,6},{8,9},{9,8},{10,11... | collective-permute-start | bytes 1179656 | tf_op jit(solution)/shard_map/ppermute | solution.py:517
  5.8 20.1 %copy-start.1 = (f32[2,2,384,384]{3,2,1,0:T(8,128)S(1)}, f32[2,2,384,384]{3,2,1,0:T(8,128)}, u32[]{:S(2)}) copy-start(f32[2,2,384,384]{3,2,1,0:T(8,128)} %x.3) | copy-start | bytes 7077892
  5.8 20.1 %copy-start.3 = (f32[2,256,256]{2,1,0:T(8,128)S(1)}, f32[2,256,256]{2,1,0:T(8,128)}, u32[]{:S(2)}) copy-start(f32[2,256,256]{2,1,0:T(8,128)} %wave.1) | copy-start | bytes 1572868
  5.8 20.1 %copy-start.5 = (s32[4,1,2]{0,2,1:T(2,128)S(1)}, s32[4,1,2]{0,2,1:T(2,128)}, u32[]{:S(2)}) copy-start(s32[4,1,2]{0,2,1:T(2,128)} %param.6) | copy-start | bytes 100
  5.8 18.4 %collective-permute-start.2 = (f32[2,384,128]{2,1,0:T(8,128)S(1)}, f32[2,384,128]{2,1,0:T(8,128)S(1)}, u32[]{:S(2)}, u32[]{:S(2)}) collective-permute-start(f32[2,384,128]{2,1,0:T(8,128)S(1)} %get-tuple-element.27), channel_id=1, source_target_pairs={{0,15},{1,2},{2,1},{3,4},{4,3},{5,6},{6,5},{7,8},{8,7},{9,10},{10,... | collective-permute-start | bytes 1179656 | tf_op jit(solution)/shard_map/ppermute | solution.py:516
  10.4 20.7 %collective-permute-start = (f32[2,128,384]{2,1,0:T(8,128)S(1)}, f32[2,128,384]{2,1,0:T(8,128)S(1)}, u32[]{:S(2)}, u32[]{:S(2)}) collective-permute-start(f32[2,128,384]{2,1,0:T(8,128)S(1)} %cut.3), channel_id=1, source_target_pairs={{0,16},{16,0},{1,17},{17,1},{2,18},{18,2},{3,19},{19,3},{4,20},{20... | collective-permute-start | bytes 1179656 | tf_op jit(solution)/shard_map/ppermute | solution.py:511
  15.5 10.3 %collective-permute-start.5 = (f32[128,128]{1,0:T(8,128)S(1)}, f32[128,128]{1,0:T(8,128)S(1)}, u32[]{:S(2)}, u32[]{:S(2)}) collective-permute-start(f32[128,128]{1,0:T(8,128)S(1)} %get-tuple-element.28), channel_id=1, source_target_pairs={{0,1},{1,0},{2,3},{3,2},{4,5},{5,4},{6,7},{7,6},{8,9},{9,8},{10,11... | collective-permute-start | bytes 196616 | tf_op jit(solution)/shard_map/ppermute | solution.py:517
  15.6 10.3 %collective-permute-start.6 = (f32[128,128]{1,0:T(8,128)S(1)}, f32[128,128]{1,0:T(8,128)S(1)}, u32[]{:S(2)}, u32[]{:S(2)}) collective-permute-start(f32[128,128]{1,0:T(8,128)S(1)} %get-tuple-element.29), channel_id=1, source_target_pairs={{0,15},{1,2},{2,1},{3,4},{4,3},{5,6},{6,5},{7,8},{8,7},{9,10},{10,... | collective-permute-start | bytes 196616 | tf_op jit(solution)/shard_map/ppermute | solution.py:516
  24.2 6.9 %collective-permute-start.3 = (f32[2,128,128]{2,1,0:T(8,128)S(1)}, f32[2,128,128]{2,1,0:T(8,128)S(1)}, u32[]{:S(2)}, u32[]{:S(2)}) collective-permute-start(f32[2,128,128]{2,1,0:T(8,128)S(1)} %corners.2), channel_id=1, source_target_pairs={{0,16},{16,0},{1,17},{17,1},{2,18},{18,2},{3,19},{19,3},{4,20},{20... | collective-permute-start | bytes 393224 | tf_op jit(solution)/shard_map/ppermute | solution.py:511
  41.1 1.6 %collective-permute-start.13 = (f32[256,256]{1,0:T(8,128)S(1)}, f32[256,256]{1,0:T(8,128)S(1)}, u32[]{:S(2)}, u32[]{:S(2)}) collective-permute-start(f32[256,256]{1,0:T(8,128)S(1)} %get-tuple-element.45), channel_id=1, source_target_pairs={{0,1},{1,0},{2,3},{3,2},{4,5},{5,4},{6,7},{7,6},{8,9},{9,8},{10,11... | collective-permute-start | bytes 786440 | tf_op jit(solution)/shard_map/ppermute | solution.py:574
  42.8 6.0 %collective-permute-start.14 = (f32[128,256]{1,0:T(8,128)S(1)}, f32[128,256]{1,0:T(8,128)S(1)}, u32[]{:S(2)}, u32[]{:S(2)}) collective-permute-start(f32[128,256]{1,0:T(8,128)S(1)} %get-tuple-element.47), channel_id=1, source_target_pairs={{0,2},{1,3},{2,0},{3,1},{4,6},{5,7},{6,4},{7,5},{8,10},{9,11},{10,... | collective-permute-start | bytes 393224 | tf_op jit(solution)/shard_map/ppermute | solution.py:574
  46.7 19.3 %collective-permute-start.7 = (f32[512,128]{1,0:T(8,128)S(1)}, f32[512,128]{1,0:T(8,128)S(1)}, u32[]{:S(2)}, u32[]{:S(2)}) collective-permute-start(f32[512,128]{1,0:T(8,128)S(1)} %get-tuple-element.38), channel_id=1, source_target_pairs={{0,1},{1,0},{2,3},{3,2},{4,5},{5,4},{6,7},{7,6},{8,9},{9,8},{10,11... | collective-permute-start | bytes 786440 | tf_op jit(solution)/shard_map/ppermute | solution.py:517
  46.9 19.1 %collective-permute-start.8 = (f32[512,128]{1,0:T(8,128)S(1)}, f32[512,128]{1,0:T(8,128)S(1)}, u32[]{:S(2)}, u32[]{:S(2)}) collective-permute-start(f32[512,128]{1,0:T(8,128)S(1)} %get-tuple-element.39), channel_id=1, source_target_pairs={{0,15},{1,2},{2,1},{3,4},{4,3},{5,6},{6,5},{7,8},{8,7},{9,10},{10,... | collective-permute-start | bytes 786440 | tf_op jit(solution)/shard_map/ppermute | solution.py:516
  48.8 7.1 %collective-permute-start.15 = (f32[64,256]{1,0:T(8,128)S(1)}, f32[64,256]{1,0:T(8,128)S(1)}, u32[]{:S(2)}, u32[]{:S(2)}) collective-permute-start(f32[64,256]{1,0:T(8,128)S(1)} %get-tuple-element.49), channel_id=1, source_target_pairs={{0,4},{1,5},{2,6},{3,7},{4,0},{5,1},{6,2},{7,3},{8,12},{9,13},{10,... | collective-permute-start | bytes 196616 | tf_op jit(solution)/shard_map/ppermute | solution.py:574
  50.5 16.3 %collective-permute-start.10 = (f32[512,128]{1,0:T(8,128)S(1)}, f32[512,128]{1,0:T(8,128)S(1)}, u32[]{:S(2)}, u32[]{:S(2)}) collective-permute-start(f32[512,128]{1,0:T(8,128)S(1)} %get-tuple-element.42), channel_id=1, source_target_pairs={{0,1},{1,0},{2,3},{3,2},{4,5},{5,4},{6,7},{7,6},{8,9},{9,8},{10,11... | collective-permute-start | bytes 786440 | tf_op jit(solution)/shard_map/ppermute | solution.py:517
  50.5 16.3 %collective-permute-start.11 = (f32[512,128]{1,0:T(8,128)S(1)}, f32[512,128]{1,0:T(8,128)S(1)}, u32[]{:S(2)}, u32[]{:S(2)}) collective-permute-start(f32[512,128]{1,0:T(8,128)S(1)} %get-tuple-element.43), channel_id=1, source_target_pairs={{0,15},{1,2},{2,1},{3,4},{4,3},{5,6},{6,5},{7,8},{8,7},{9,10},{10,... | collective-permute-start | bytes 786440 | tf_op jit(solution)/shard_map/ppermute | solution.py:516
  55.9 4.3 %collective-permute-start.16 = (f32[64,256]{1,0:T(8,128)S(1)}, f32[64,256]{1,0:T(8,128)S(1)}, u32[]{:S(2)}, u32[]{:S(2)}) collective-permute-start(f32[64,256]{1,0:T(8,128)S(1)} %adding.3.mine), channel_id=1, source_target_pairs={{0,16},{16,0},{1,17},{17,1},{2,18},{18,2},{3,19},{19,3},{4,20},{20... | collective-permute-start | bytes 196616 | tf_op jit(solution)/shard_map/ppermute | solution.py:574
  60.3 5.6 %collective-permute-start.17 = (f32[64,256]{1,0:T(8,128)S(1)}, f32[64,256]{1,0:T(8,128)S(1)}, u32[]{:S(2)}, u32[]{:S(2)}) collective-permute-start(f32[64,256]{1,0:T(8,128)S(1)} %adding.4.mine), channel_id=1, source_target_pairs={{0,8},{1,9},{2,10},{3,11},{4,12},{5,13},{6,14},{7,15},{8,0},{9,1},... | collective-permute-start | bytes 196616 | tf_op jit(solution)/shard_map/ppermute | solution.py:574
  65.9 4.3 %collective-permute-start.18 = (f32[64,256]{1,0:T(8,128)S(1)}, f32[64,256]{1,0:T(8,128)S(1)}, u32[]{:S(2)}, u32[]{:S(2)}) collective-permute-start(f32[64,256]{1,0:T(8,128)S(1)} %adding.5.mine), channel_id=1, source_target_pairs={{0,4},{1,5},{2,6},{3,7},{4,0},{5,1},{6,2},{7,3},{8,12},{9,13},{10,... | collective-permute-start | bytes 196616 | tf_op jit(solution)/shard_map/ppermute | solution.py:574
  66.1 15.7 %collective-permute-start.9 = (f32[2,128,384]{2,1,0:T(8,128)S(1)}, f32[2,128,384]{2,1,0:T(8,128)S(1)}, u32[]{:S(2)}, u32[]{:S(2)}) collective-permute-start(f32[2,128,384]{2,1,0:T(8,128)S(1)} %merge.2), channel_id=1, source_target_pairs={{0,16},{16,0},{1,17},{17,1},{2,18},{18,2},{3,19},{19,3},{4,20},{20... | collective-permute-start | bytes 1179656 | tf_op jit(solution)/shard_map/ppermute | solution.py:511
  66.9 13.6 %collective-permute-start.12 = (f32[2,128,384]{2,1,0:T(8,128)S(1)}, f32[2,128,384]{2,1,0:T(8,128)S(1)}, u32[]{:S(2)}, u32[]{:S(2)}) collective-permute-start(f32[2,128,384]{2,1,0:T(8,128)S(1)} %merge.3), channel_id=1, source_target_pairs={{0,16},{16,0},{1,17},{17,1},{2,18},{18,2},{3,19},{19,3},{4,20},{20... | collective-permute-start | bytes 1179656 | tf_op jit(solution)/shard_map/ppermute | solution.py:511
  70.3 5.0 %collective-permute-start.19 = (f32[128,256]{1,0:T(8,128)S(1)}, f32[128,256]{1,0:T(8,128)S(1)}, u32[]{:S(2)}, u32[]{:S(2)}) collective-permute-start(f32[128,256]{1,0:T(8,128)S(1)} %joining.2.mine), channel_id=1, source_target_pairs={{0,2},{1,3},{2,0},{3,1},{4,6},{5,7},{6,4},{7,5},{8,10},{9,11},{10,... | collective-permute-start | bytes 393224 | tf_op jit(solution)/shard_map/ppermute | solution.py:574
  75.3 7.8 %collective-permute-start.20 = (f32[256,256]{1,0:T(8,128)S(1)}, f32[256,256]{1,0:T(8,128)S(1)}, u32[]{:S(2)}, u32[]{:S(2)}) collective-permute-start(f32[256,256]{1,0:T(8,128)S(1)} %joining.3.mine), channel_id=1, source_target_pairs={{0,1},{1,0},{2,3},{3,2},{4,5},{5,4},{6,7},{7,6},{8,9},{9,8},{10,11... | collective-permute-start | bytes 786440 | tf_op jit(solution)/shard_map/ppermute | solution.py:574
  (3 other events, 38.4 us)

commit v6 on v5

--- a/solution.py
+++ b/solution.py
@@ -352,7 +352,7 @@
     h = stage.half
     assemble(ext, x.at[0], rows, near.at[0], far.at[0], cn, cf, on_odd())
 
-    @pl.loop(0, count // many)
+    @pl.loop(0, count // many, unroll=True)
     def _(i):
         first = i * many
 
@@ -381,7 +381,7 @@
     h = stage.half
     assemble(ext, x.at[1], rows, near.at[1], far.at[1], corners.at[0], corners.at[1], on_odd())
 
-    @pl.loop(0, count // many)
+    @pl.loop(0, count // many, unroll=True)
     def _(i):
         first = i * many
 
@@ -411,7 +411,7 @@
     h = stage.half
     acc[...] = jnp.zeros_like(acc)
 
-    @pl.loop(0, count // many)
+    @pl.loop(0, count // many, unroll=True)
     def _(i):
         first = i * many
 
@@ -438,7 +438,7 @@
 def spread_kernel(off, beta, wave, acc, near, far):
     acc[...] = jnp.zeros_like(acc)
 
-    @pl.loop(0, beta.shape[0])
+    @pl.loop(0, beta.shape[0], unroll=True)
     def _(p):
         psi = wave.at[p] if len(wave.shape) == 4 else wave
         for c, g in enumerate(conj_times(psi[0], psi[1], beta[p, 0], beta[p, 1])):

time: 85.6 us -> 84.6 us (0.988)
  no operation moved by 1% of the time
where the time goes in v6:
time: 84.6 us; the launch traced here: 83.4 us
  waiting for transfers between devices  31.4 us (37%)
  Pallas kernels  25.9 us (31%)
  starting transfers between devices  23.2 us (27%)
  local copies, waits for them, and re-layouts  1.69 us (2%)
  between operations  1.12 us (1%)
    ppermute x8, waiting for transfers between devices, swap(): return lax.ppermute(y, axis, [(i, i ^ bit) for i in range(sizes[axis])])  21.9 us
    ppermute x4, starting transfers between devices, exchange(): lax.ppermute(far, 'col', [(i, (i + i % 2 * 2 - 1) % count) for i in range...  12.8 us
    ppermute x5, waiting for transfers between devices, shift(): return lax.ppermute(x, axis, [(i, (i + by) % count) for i in range(count)])  9.49 us
    ppermute x5, starting transfers between devices, shift(): return lax.ppermute(x, axis, [(i, (i + by) % count) for i in range(count)])  7.37 us
    pallas_call x1, Pallas kernels, local(): call(second_kernel, (field, field), flops=flops, room=ROOM, in_specs=[SME...  5.4 us
    pallas_call x1, Pallas kernels, local(): call(first_kernel, (field, field), flops=flops, room=ROOM, in_specs=[SMEM...  5.08 us
    pallas_call x1, Pallas kernels, local(): call(functools.partial(third_kernel, factor), (field, shaped(size, size),...  4.13 us
    pallas_call x2, Pallas kernels, spread(): call(spread_kernel, (shaped(*ext.shape), shaped(span, LANES), shaped(span...  3.7 us
  transfers between devices with their start and end apart: 21, of which 8 were waited for; matrix products, arithmetic and copies ran while one was open for 0% of the time, Pallas kernels for 19%

profile of v6, /device:TPU:0, one launch (start us, length us, event | category | flops | bytes accessed | tf_op | source)
XLA Modules:
  0.0 83.4 jit_solution(7332697761462724582)
XLA Ops:
  0.6 1.7 %copy-done = f32[2,2,384,384]{3,2,1,0:T(8,128)S(1)} copy-done((f32[2,2,384,384]{3,2,1,0:T(8,128)S(1)}, f32[2,2,384,384]{3,2,1,0:T(8,128)}, u32[]{:S(2)}) %copy-start) | copy-done | bytes 2359320
  2.4 3.1 %collective-permute-start.4 = (f32[2,128,384]{2,1,0:T(8,128)S(1)}, f32[2,128,384]{2,1,0:T(8,128)S(1)}, u32[]{:S(2)}, u32[]{:S(2)}) collective-permute-start(f32[2,128,384]{2,1,0:T(8,128)S(1)} %cut.5), channel_id=1, source_target_pairs={{0,16},{16,0},{1,17},{17,1},{2,18},{18,2},{3,19},{19,3},{4,20},{20... | collective-permute-start | bytes 1179656 | tf_op jit(solution)/shard_map/ppermute | solution.py:511
  5.8 4.6 %collective-permute-start.2 = (f32[2,384,128]{2,1,0:T(8,128)S(1)}, f32[2,384,128]{2,1,0:T(8,128)S(1)}, u32[]{:S(2)}, u32[]{:S(2)}) collective-permute-start(f32[2,384,128]{2,1,0:T(8,128)S(1)} %get-tuple-element.27), channel_id=1, source_target_pairs={{0,15},{1,2},{2,1},{3,4},{4,3},{5,6},{6,5},{7,8},{8,7},{9,10},{10,... | collective-permute-start | bytes 1179656 | tf_op jit(solution)/shard_map/ppermute | solution.py:516
  11.0 4.4 %collective-permute-done.4.rows_ref.rows = f32[2,128,384]{2,1,0:T(8,128)S(1)} collective-permute-done((f32[2,128,384]{2,1,0:T(8,128)S(1)}, f32[2,128,384]{2,1,0:T(8,128)S(1)}, u32[]{:S(2)}, u32[]{:S(2)}) %collective-permute-start.4) | collective-permute-done | bytes 393248 | tf_op jit(solution)/shard_map/ppermute | solution.py:511
  15.6 5.1 %collective-permute-start.6 = (f32[128,128]{1,0:T(8,128)S(1)}, f32[128,128]{1,0:T(8,128)S(1)}, u32[]{:S(2)}, u32[]{:S(2)}) collective-permute-start(f32[128,128]{1,0:T(8,128)S(1)} %get-tuple-element.29), channel_id=1, source_target_pairs={{0,15},{1,2},{2,1},{3,4},{4,3},{5,6},{6,5},{7,8},{8,7},{9,10},{10,... | collective-permute-start | bytes 196616 | tf_op jit(solution)/shard_map/ppermute | solution.py:516
  20.7 3.5 %prepare.1 = (f32[2,256,256]{2,1,0:T(8,128)S(1)}, bf16[8,256,256]{2,1,0:T(8,128)(2,1)S(1)}, f32[4,256,256]{2,1,0:T(8,128)S(1)}) custom-call(f32[256,256]{1,0:T(8,128)S(1)} %copy-done.4, f32[4,256,256]{2,1,0:T(8,128)S(1)} %bitcast.4), custom_call_target="tpu_custom_call" | custom-call | flops 268435456 | bytes 4194304 | tf_op jit(solution)/shard_map/prepare/pallas_call | solution.py:267
  24.2 1.6 %collective-permute-start.3 = (f32[2,128,128]{2,1,0:T(8,128)S(1)}, f32[2,128,128]{2,1,0:T(8,128)S(1)}, u32[]{:S(2)}, u32[]{:S(2)}) collective-permute-start(f32[2,128,128]{2,1,0:T(8,128)S(1)} %corners.2), channel_id=1, source_target_pairs={{0,16},{16,0},{1,17},{17,1},{2,18},{18,2},{3,19},{19,3},{4,20},{20... | collective-permute-start | bytes 393224 | tf_op jit(solution)/shard_map/ppermute | solution.py:511
  25.9 5.1 %first.1 = (f32[4,2,256,256]{3,2,1,0:T(8,128)S(1)}, f32[4,2,256,256]{3,2,1,0:T(8,128)S(1)}) custom-call(s32[2,4]{1,0:T(2,128)S(1)} %bitcast.5, f32[2,2,384,384]{3,2,1,0:T(8,128)S(1)} %copy-done.1, f32[2,128,384]{2,1,0:T(8,128)S(1)} %collective-permute-done.4.rows_ref.rows, f32[2,384,128]{2,1,0:T(8,128)S(1)} %collective-permute-done.1.near, ...), custom_call_target="tpu_custom_call" | custom-call | flops 3221225472 | bytes 4194304 | tf_op jit(solution)/shard_map/first/pallas_call | solution.py:642
  31.0 5.4 %second.1 = (f32[4,2,256,256]{3,2,1,0:T(8,128)S(1)}, f32[4,2,256,256]{3,2,1,0:T(8,128)S(1)}) custom-call(s32[2,4]{1,0:T(2,128)S(1)} %bitcast.6, f32[2,2,384,384]{3,2,1,0:T(8,128)S(1)} %copy-done.1, f32[2,128,384]{2,1,0:T(8,128)S(1)} %collective-permute-done.rows, f32[2,384,128]{2,1,0:T(8,128)S(1)} %collective-permute-done.1.near, ...), custom_call_target="tpu_custom_call" | custom-call | flops 3221225472 | bytes 4194304 | tf_op jit(solution)/shard_map/second/pallas_call | solution.py:652
  36.4 4.1 %third.1 = (f32[4,2,256,256]{3,2,1,0:T(8,128)S(1)}, f32[256,256]{1,0:T(8,128)S(1)}, f32[256,256]{1,0:T(8,128)S(1)}) custom-call(f32[4,2,256,256]{3,2,1,0:T(8,128)S(1)} %get-tuple-element.34.u, f32[4,2,256,256]{3,2,1,0:T(8,128)S(1)} %get-tuple-element.35.w, f32[2,256,256]{2,1,0:T(8,128)S(1)} %get-tuple-element.30.prop, ...), custom_call_target="tpu_custom_call" | custom-call | flops 3221225472 | bytes 4194304 | tf_op jit(solution)/shard_map/third/pallas_call | solution.py:662
  40.6 1.5 %collective-permute-done.13.came = f32[256,256]{1,0:T(8,128)S(1)} collective-permute-done((f32[256,256]{1,0:T(8,128)S(1)}, f32[256,256]{1,0:T(8,128)S(1)}, u32[]{:S(2)}, u32[]{:S(2)}) %collective-permute-start.13) | collective-permute-done | bytes 262176 | tf_op jit(solution)/shard_map/ppermute | solution.py:574
  42.2 2.0 %spread.2 = (f32[2,5,512,128]{3,2,1,0:T(8,128)S(1)}, f32[512,128]{1,0:T(8,128)S(1)}, f32[512,128]{1,0:T(8,128)S(1)}) custom-call(s32[2,4]{1,0:T(2,128)S(1)} %bitcast.7, f32[4,2,256,256]{3,2,1,0:T(8,128)S(1)} %get-tuple-element.36.beta, f32[2,256,256]{2,1,0:T(8,128)S(1)} %copy-done.3), custom_call_target="tpu_custom_call" | custom-call | bytes 4194304 | tf_op jit(solution)/shard_map/spread/pallas_call | solution.py:674
  44.2 1.7 %spread.3 = (f32[2,5,512,128]{3,2,1,0:T(8,128)S(1)}, f32[512,128]{1,0:T(8,128)S(1)}, f32[512,128]{1,0:T(8,128)S(1)}) custom-call(s32[2,4]{1,0:T(2,128)S(1)} %bitcast.8, f32[4,2,256,256]{3,2,1,0:T(8,128)S(1)} %get-tuple-element.40.beta, f32[4,2,256,256]{3,2,1,0:T(8,128)S(1)} %get-tuple-element.32.psi.wave), custom_call_target="tpu_custom_call" | custom-call | bytes 4194304 | tf_op jit(solution)/shard_map/spread/pallas_call | solution.py:674
  46.2 2.0 %collective-permute-start.8 = (f32[512,128]{1,0:T(8,128)S(1)}, f32[512,128]{1,0:T(8,128)S(1)}, u32[]{:S(2)}, u32[]{:S(2)}) collective-permute-start(f32[512,128]{1,0:T(8,128)S(1)} %get-tuple-element.39), channel_id=1, source_target_pairs={{0,15},{1,2},{2,1},{3,4},{4,3},{5,6},{6,5},{7,8},{8,7},{9,10},{10,... | collective-permute-start | bytes 786440 | tf_op jit(solution)/shard_map/ppermute | solution.py:516
  48.2 1.6 %collective-permute-start.15 = (f32[64,256]{1,0:T(8,128)S(1)}, f32[64,256]{1,0:T(8,128)S(1)}, u32[]{:S(2)}, u32[]{:S(2)}) collective-permute-start(f32[64,256]{1,0:T(8,128)S(1)} %get-tuple-element.49), channel_id=1, source_target_pairs={{0,4},{1,5},{2,6},{3,7},{4,0},{5,1},{6,2},{7,3},{8,12},{9,13},{10,... | collective-permute-start | bytes 196616 | tf_op jit(solution)/shard_map/ppermute | solution.py:574
  50.9 4.4 %collective-permute-done.15.came = f32[64,256]{1,0:T(8,128)S(1)} collective-permute-done((f32[64,256]{1,0:T(8,128)S(1)}, f32[64,256]{1,0:T(8,128)S(1)}, u32[]{:S(2)}, u32[]{:S(2)}) %collective-permute-start.15) | collective-permute-done | bytes 65568 | tf_op jit(solution)/shard_map/ppermute | solution.py:574
  55.9 3.7 %collective-permute-done.16.came = f32[64,256]{1,0:T(8,128)S(1)} collective-permute-done((f32[64,256]{1,0:T(8,128)S(1)}, f32[64,256]{1,0:T(8,128)S(1)}, u32[]{:S(2)}, u32[]{:S(2)}) %collective-permute-start.16) | collective-permute-done | bytes 65568 | tf_op jit(solution)/shard_map/ppermute | solution.py:574
  59.7 5.5 %collective-permute-done.17.came = f32[64,256]{1,0:T(8,128)S(1)} collective-permute-done((f32[64,256]{1,0:T(8,128)S(1)}, f32[64,256]{1,0:T(8,128)S(1)}, u32[]{:S(2)}, u32[]{:S(2)}) %collective-permute-start.17) | collective-permute-done | bytes 65568 | tf_op jit(solution)/shard_map/ppermute | solution.py:574
  66.3 1.4 %collective-permute-start.12 = (f32[2,128,384]{2,1,0:T(8,128)S(1)}, f32[2,128,384]{2,1,0:T(8,128)S(1)}, u32[]{:S(2)}, u32[]{:S(2)}) collective-permute-start(f32[2,128,384]{2,1,0:T(8,128)S(1)} %merge.3), channel_id=1, source_target_pairs={{0,16},{16,0},{1,17},{17,1},{2,18},{18,2},{3,19},{19,3},{4,20},{20... | collective-permute-start | bytes 1179656 | tf_op jit(solution)/shard_map/ppermute | solution.py:511
  67.7 1.8 %collective-permute-done.18.came = f32[64,256]{1,0:T(8,128)S(1)} collective-permute-done((f32[64,256]{1,0:T(8,128)S(1)}, f32[64,256]{1,0:T(8,128)S(1)}, u32[]{:S(2)}, u32[]{:S(2)}) %collective-permute-start.18) | collective-permute-done | bytes 65568 | tf_op jit(solution)/shard_map/ppermute | solution.py:574
  69.7 5.0 %collective-permute-done.19.came = f32[128,256]{1,0:T(8,128)S(1)} collective-permute-done((f32[128,256]{1,0:T(8,128)S(1)}, f32[128,256]{1,0:T(8,128)S(1)}, u32[]{:S(2)}, u32[]{:S(2)}) %collective-permute-start.19) | collective-permute-done | bytes 131104 | tf_op jit(solution)/shard_map/ppermute | solution.py:574
  74.7 5.1 %collective-permute-done.12.strip = f32[2,128,384]{2,1,0:T(8,128)S(1)} collective-permute-done((f32[2,128,384]{2,1,0:T(8,128)S(1)}, f32[2,128,384]{2,1,0:T(8,128)S(1)}, u32[]{:S(2)}, u32[]{:S(2)}) %collective-permute-start.12) | collective-permute-done | bytes 393248 | tf_op jit(solution)/shard_map/ppermute | solution.py:511
  79.8 1.3 %finish.2.refs_0_ = f32[2,2,384,384]{3,2,1,0:T(8,128)} custom-call(f32[2,5,512,128]{3,2,1,0:T(8,128)S(1)} %get-tuple-element.41.acc, f32[512,128]{1,0:T(8,128)S(1)} %collective-permute-done.10.near, f32[512,128]{1,0:T(8,128)S(1)} %collective-permute-done.11.far, f32[2,128,384]{2,1,0:T(8,128)S(1)} %collective-permute-done.12.strip), custom_call_target="tpu_custom_call" | custom-call | bytes 4194304 | tf_op jit(solution)/shard_map/finish/pallas_call | solution.py:497
  81.1 1.3 %finish.3 = f32[2,2,384,384]{3,2,1,0:T(8,128)} custom-call(f32[2,5,512,128]{3,2,1,0:T(8,128)S(1)} %get-tuple-element.37.acc, f32[512,128]{1,0:T(8,128)S(1)} %collective-permute-done.7.near, f32[512,128]{1,0:T(8,128)S(1)} %collective-permute-done.8.far, f32[2,128,384]{2,1,0:T(8,128)S(1)} %collective-permute-done.9.strip, ...), custom_call_target="tpu_custom_call", output_to_operand_aliasing={{}: (4, {})} | custom-call | bytes 4194304 | tf_op jit(solution)/shard_map/finish/pallas_call | solution.py:497
  (53 shorter events, 5.5 us)
Async XLA Ops:
  2.4 13.0 %collective-permute-start.4 = (f32[2,128,384]{2,1,0:T(8,128)S(1)}, f32[2,128,384]{2,1,0:T(8,128)S(1)}, u32[]{:S(2)}, u32[]{:S(2)}) collective-permute-start(f32[2,128,384]{2,1,0:T(8,128)S(1)} %cut.5), channel_id=1, source_target_pairs={{0,16},{16,0},{1,17},{17,1},{2,18},{18,2},{3,19},{19,3},{4,20},{20... | collective-permute-start | bytes 1179656 | tf_op jit(solution)/shard_map/ppermute | solution.py:511
  5.7 18.5 %collective-permute-start.1 = (f32[2,384,128]{2,1,0:T(8,128)S(1)}, f32[2,384,128]{2,1,0:T(8,128)S(1)}, u32[]{:S(2)}, u32[]{:S(2)}) collective-permute-start(f32[2,384,128]{2,1,0:T(8,128)S(1)} %get-tuple-element.26), channel_id=1, source_target_pairs={{0,1},{1,0},{2,3},{3,2},{4,5},{5,4},{6,7},{7,6},{8,9},{9,8},{10,11... | collective-permute-start | bytes 1179656 | tf_op jit(solution)/shard_map/ppermute | solution.py:517
  5.8 20.1 %copy-start.1 = (f32[2,2,384,384]{3,2,1,0:T(8,128)S(1)}, f32[2,2,384,384]{3,2,1,0:T(8,128)}, u32[]{:S(2)}) copy-start(f32[2,2,384,384]{3,2,1,0:T(8,128)} %x.3) | copy-start | bytes 7077892
  5.8 20.1 %copy-start.3 = (f32[2,256,256]{2,1,0:T(8,128)S(1)}, f32[2,256,256]{2,1,0:T(8,128)}, u32[]{:S(2)}) copy-start(f32[2,256,256]{2,1,0:T(8,128)} %wave.1) | copy-start | bytes 1572868
  5.8 20.1 %copy-start.5 = (s32[4,1,2]{0,2,1:T(2,128)S(1)}, s32[4,1,2]{0,2,1:T(2,128)}, u32[]{:S(2)}) copy-start(s32[4,1,2]{0,2,1:T(2,128)} %param.6) | copy-start | bytes 100
  5.8 18.4 %collective-permute-start.2 = (f32[2,384,128]{2,1,0:T(8,128)S(1)}, f32[2,384,128]{2,1,0:T(8,128)S(1)}, u32[]{:S(2)}, u32[]{:S(2)}) collective-permute-start(f32[2,384,128]{2,1,0:T(8,128)S(1)} %get-tuple-element.27), channel_id=1, source_target_pairs={{0,15},{1,2},{2,1},{3,4},{4,3},{5,6},{6,5},{7,8},{8,7},{9,10},{10,... | collective-permute-start | bytes 1179656 | tf_op jit(solution)/shard_map/ppermute | solution.py:516
  10.4 20.5 %collective-permute-start = (f32[2,128,384]{2,1,0:T(8,128)S(1)}, f32[2,128,384]{2,1,0:T(8,128)S(1)}, u32[]{:S(2)}, u32[]{:S(2)}) collective-permute-start(f32[2,128,384]{2,1,0:T(8,128)S(1)} %cut.3), channel_id=1, source_target_pairs={{0,16},{16,0},{1,17},{17,1},{2,18},{18,2},{3,19},{19,3},{4,20},{20... | collective-permute-start | bytes 1179656 | tf_op jit(solution)/shard_map/ppermute | solution.py:511
  15.5 10.3 %collective-permute-start.5 = (f32[128,128]{1,0:T(8,128)S(1)}, f32[128,128]{1,0:T(8,128)S(1)}, u32[]{:S(2)}, u32[]{:S(2)}) collective-permute-start(f32[128,128]{1,0:T(8,128)S(1)} %get-tuple-element.28), channel_id=1, source_target_pairs={{0,1},{1,0},{2,3},{3,2},{4,5},{5,4},{6,7},{7,6},{8,9},{9,8},{10,11... | collective-permute-start | bytes 196616 | tf_op jit(solution)/shard_map/ppermute | solution.py:517
  15.6 10.3 %collective-permute-start.6 = (f32[128,128]{1,0:T(8,128)S(1)}, f32[128,128]{1,0:T(8,128)S(1)}, u32[]{:S(2)}, u32[]{:S(2)}) collective-permute-start(f32[128,128]{1,0:T(8,128)S(1)} %get-tuple-element.29), channel_id=1, source_target_pairs={{0,15},{1,2},{2,1},{3,4},{4,3},{5,6},{6,5},{7,8},{8,7},{9,10},{10,... | collective-permute-start | bytes 196616 | tf_op jit(solution)/shard_map/ppermute | solution.py:516
  24.2 6.7 %collective-permute-start.3 = (f32[2,128,128]{2,1,0:T(8,128)S(1)}, f32[2,128,128]{2,1,0:T(8,128)S(1)}, u32[]{:S(2)}, u32[]{:S(2)}) collective-permute-start(f32[2,128,128]{2,1,0:T(8,128)S(1)} %corners.2), channel_id=1, source_target_pairs={{0,16},{16,0},{1,17},{17,1},{2,18},{18,2},{3,19},{19,3},{4,20},{20... | collective-permute-start | bytes 393224 | tf_op jit(solution)/shard_map/ppermute | solution.py:511
  40.5 1.6 %collective-permute-start.13 = (f32[256,256]{1,0:T(8,128)S(1)}, f32[256,256]{1,0:T(8,128)S(1)}, u32[]{:S(2)}, u32[]{:S(2)}) collective-permute-start(f32[256,256]{1,0:T(8,128)S(1)} %get-tuple-element.45), channel_id=1, source_target_pairs={{0,1},{1,0},{2,3},{3,2},{4,5},{5,4},{6,7},{7,6},{8,9},{9,8},{10,11... | collective-permute-start | bytes 786440 | tf_op jit(solution)/shard_map/ppermute | solution.py:574
  42.1 6.0 %collective-permute-start.14 = (f32[128,256]{1,0:T(8,128)S(1)}, f32[128,256]{1,0:T(8,128)S(1)}, u32[]{:S(2)}, u32[]{:S(2)}) collective-permute-start(f32[128,256]{1,0:T(8,128)S(1)} %get-tuple-element.47), channel_id=1, source_target_pairs={{0,2},{1,3},{2,0},{3,1},{4,6},{5,7},{6,4},{7,5},{8,10},{9,11},{10,... | collective-permute-start | bytes 393224 | tf_op jit(solution)/shard_map/ppermute | solution.py:574
  45.9 19.4 %collective-permute-start.7 = (f32[512,128]{1,0:T(8,128)S(1)}, f32[512,128]{1,0:T(8,128)S(1)}, u32[]{:S(2)}, u32[]{:S(2)}) collective-permute-start(f32[512,128]{1,0:T(8,128)S(1)} %get-tuple-element.38), channel_id=1, source_target_pairs={{0,1},{1,0},{2,3},{3,2},{4,5},{5,4},{6,7},{7,6},{8,9},{9,8},{10,11... | collective-permute-start | bytes 786440 | tf_op jit(solution)/shard_map/ppermute | solution.py:517
  46.2 19.1 %collective-permute-start.8 = (f32[512,128]{1,0:T(8,128)S(1)}, f32[512,128]{1,0:T(8,128)S(1)}, u32[]{:S(2)}, u32[]{:S(2)}) collective-permute-start(f32[512,128]{1,0:T(8,128)S(1)} %get-tuple-element.39), channel_id=1, source_target_pairs={{0,15},{1,2},{2,1},{3,4},{4,3},{5,6},{6,5},{7,8},{8,7},{9,10},{10,... | collective-permute-start | bytes 786440 | tf_op jit(solution)/shard_map/ppermute | solution.py:516
  48.2 7.1 %collective-permute-start.15 = (f32[64,256]{1,0:T(8,128)S(1)}, f32[64,256]{1,0:T(8,128)S(1)}, u32[]{:S(2)}, u32[]{:S(2)}) collective-permute-start(f32[64,256]{1,0:T(8,128)S(1)} %get-tuple-element.49), channel_id=1, source_target_pairs={{0,4},{1,5},{2,6},{3,7},{4,0},{5,1},{6,2},{7,3},{8,12},{9,13},{10,... | collective-permute-start | bytes 196616 | tf_op jit(solution)/shard_map/ppermute | solution.py:574
  49.8 16.4 %collective-permute-start.10 = (f32[512,128]{1,0:T(8,128)S(1)}, f32[512,128]{1,0:T(8,128)S(1)}, u32[]{:S(2)}, u32[]{:S(2)}) collective-permute-start(f32[512,128]{1,0:T(8,128)S(1)} %get-tuple-element.42), channel_id=1, source_target_pairs={{0,1},{1,0},{2,3},{3,2},{4,5},{5,4},{6,7},{7,6},{8,9},{9,8},{10,11... | collective-permute-start | bytes 786440 | tf_op jit(solution)/shard_map/ppermute | solution.py:517
  49.8 16.4 %collective-permute-start.11 = (f32[512,128]{1,0:T(8,128)S(1)}, f32[512,128]{1,0:T(8,128)S(1)}, u32[]{:S(2)}, u32[]{:S(2)}) collective-permute-start(f32[512,128]{1,0:T(8,128)S(1)} %get-tuple-element.43), channel_id=1, source_target_pairs={{0,15},{1,2},{2,1},{3,4},{4,3},{5,6},{6,5},{7,8},{8,7},{9,10},{10,... | collective-permute-start | bytes 786440 | tf_op jit(solution)/shard_map/ppermute | solution.py:516
  55.3 4.3 %collective-permute-start.16 = (f32[64,256]{1,0:T(8,128)S(1)}, f32[64,256]{1,0:T(8,128)S(1)}, u32[]{:S(2)}, u32[]{:S(2)}) collective-permute-start(f32[64,256]{1,0:T(8,128)S(1)} %adding.3.mine), channel_id=1, source_target_pairs={{0,16},{16,0},{1,17},{17,1},{2,18},{18,2},{3,19},{19,3},{4,20},{20... | collective-permute-start | bytes 196616 | tf_op jit(solution)/shard_map/ppermute | solution.py:574
  59.6 5.6 %collective-permute-start.17 = (f32[64,256]{1,0:T(8,128)S(1)}, f32[64,256]{1,0:T(8,128)S(1)}, u32[]{:S(2)}, u32[]{:S(2)}) collective-permute-start(f32[64,256]{1,0:T(8,128)S(1)} %adding.4.mine), channel_id=1, source_target_pairs={{0,8},{1,9},{2,10},{3,11},{4,12},{5,13},{6,14},{7,15},{8,0},{9,1},... | collective-permute-start | bytes 196616 | tf_op jit(solution)/shard_map/ppermute | solution.py:574
  65.2 4.3 %collective-permute-start.18 = (f32[64,256]{1,0:T(8,128)S(1)}, f32[64,256]{1,0:T(8,128)S(1)}, u32[]{:S(2)}, u32[]{:S(2)}) collective-permute-start(f32[64,256]{1,0:T(8,128)S(1)} %adding.5.mine), channel_id=1, source_target_pairs={{0,4},{1,5},{2,6},{3,7},{4,0},{5,1},{6,2},{7,3},{8,12},{9,13},{10,... | collective-permute-start | bytes 196616 | tf_op jit(solution)/shard_map/ppermute | solution.py:574
  65.4 15.7 %collective-permute-start.9 = (f32[2,128,384]{2,1,0:T(8,128)S(1)}, f32[2,128,384]{2,1,0:T(8,128)S(1)}, u32[]{:S(2)}, u32[]{:S(2)}) collective-permute-start(f32[2,128,384]{2,1,0:T(8,128)S(1)} %merge.2), channel_id=1, source_target_pairs={{0,16},{16,0},{1,17},{17,1},{2,18},{18,2},{3,19},{19,3},{4,20},{20... | collective-permute-start | bytes 1179656 | tf_op jit(solution)/shard_map/ppermute | solution.py:511
  66.3 13.5 %collective-permute-start.12 = (f32[2,128,384]{2,1,0:T(8,128)S(1)}, f32[2,128,384]{2,1,0:T(8,128)S(1)}, u32[]{:S(2)}, u32[]{:S(2)}) collective-permute-start(f32[2,128,384]{2,1,0:T(8,128)S(1)} %merge.3), channel_id=1, source_target_pairs={{0,16},{16,0},{1,17},{17,1},{2,18},{18,2},{3,19},{19,3},{4,20},{20... | collective-permute-start | bytes 1179656 | tf_op jit(solution)/shard_map/ppermute | solution.py:511
  69.6 5.0 %collective-permute-start.19 = (f32[128,256]{1,0:T(8,128)S(1)}, f32[128,256]{1,0:T(8,128)S(1)}, u32[]{:S(2)}, u32[]{:S(2)}) collective-permute-start(f32[128,256]{1,0:T(8,128)S(1)} %joining.2.mine), channel_id=1, source_target_pairs={{0,2},{1,3},{2,0},{3,1},{4,6},{5,7},{6,4},{7,5},{8,10},{9,11},{10,... | collective-permute-start | bytes 393224 | tf_op jit(solution)/shard_map/ppermute | solution.py:574
  74.6 7.8 %collective-permute-start.20 = (f32[256,256]{1,0:T(8,128)S(1)}, f32[256,256]{1,0:T(8,128)S(1)}, u32[]{:S(2)}, u32[]{:S(2)}) collective-permute-start(f32[256,256]{1,0:T(8,128)S(1)} %joining.3.mine), channel_id=1, source_target_pairs={{0,1},{1,0},{2,3},{3,2},{4,5},{5,4},{6,7},{7,6},{8,9},{9,8},{10,11... | collective-permute-start | bytes 786440 | tf_op jit(solution)/shard_map/ppermute | solution.py:574
  (3 other events, 38.4 us)
